TPU v7x, 32 devices: a whole 2x2x4 slice. The times are simulated.
32 devices in a mesh: dom: 8 (over z, y), near: 4 (over x, core).
Axes of the slice: x: 2, y: 2, z: 4, core: 2. Of those that a mesh axis runs over, the one named last changes fastest.
Arguments:
- solution: float32 [56, 9, 4096], P(None, None, ('dom', 'near')), may hold values from -6 to 6
- star_matrices: float32 [3, 9, 9, 4096], P(None, None, None, ('dom', 'near')), may hold values from -2.5 to 2.5
- flux_plus: float32 [4, 9, 9, 4096], P(None, None, None, ('dom', 'near')), may hold values from -1.2 to 1.2
- flux_minus: float32 [4, 9, 9, 4096], P(None, None, None, ('dom', 'near')), may hold values from -1.2 to 1.2
- stiffness: float32 [3, 56, 56], replicated, may hold values from -0.75 to 0.75
- face_lift: float32 [4, 56, 21], replicated, may hold values from -0.625 to 0.625
- face_project: float32 [4, 21, 56], replicated, may hold values from -0.75 to 0.75
- cluster: int32 [4096], P(('dom', 'near')), may hold values from 0 to 1, as said below
- neighbour_part: int32 [4, 4096], P(None, ('dom', 'near')), may hold values from 0 to 4, as said below
- neighbour_slot: int32 [4, 4096], P(None, ('dom', 'near')), may hold values from 0 to 127, as said below
- neighbour_face: int32 [4, 4096], P(None, ('dom', 'near')), may hold values from 0 to 3
- orientation: int32 [4, 4096], P(None, ('dom', 'near')), may hold values from 0 to 2
- halo_send: int32 [4, 512], P(None, ('dom', 'near')), may hold values from 0 to 127, as said below
Outputs:
- updated: float32 [56, 9, 4096], P(None, None, ('dom', 'near'))
Inputs may be any that keep to these rules, and one draw needn't show every extreme that they name: 0 marks an element that takes two half steps, 1 one that takes one step of length one. A partition holds at most 64 elements of cluster 0, and some partition exactly that many. `neighbour_part`: 0: the neighbour lies in the element's own partition; 1 to 4: it comes from the partition at near -1, near +1, dom -1, dom +1 (cyclic). In each partition each pair of a part p of 1 to 4 and a slot below 16 is named by exactly one face. `neighbour_slot`: an element of the own partition where the part is 0, a slot below 16 otherwise. `halo_send`: row r of a partition lists the elements it sends to the partition at near +1, near -1, dom +1, dom -1 for r = 0, 1, 2, 3; the 16 entries of a row are distinct.
All inputs are finite; a program needn't handle non-finite values.
Results may differ from a plain program's by a relative error of at most 0.0003.
Values sent between devices are 32-bit elements; how exact they have to be, the bound alone decides.
No kernel may reach another device: no remote copies, remote signals or barrier semaphores. Data moves between devices by JAX's collectives and lax.ppermute only.
A program may use at most 128 MiB of HBM per device.

v0:
```python
import functools
import math

import jax
import jax.numpy as jnp
import numpy as np
from jax import lax
from jax.experimental import pallas as pl
from jax.experimental.pallas import tpu as pltpu
from jax.sharding import PartitionSpec as P

MODES = 56
FIELDS = 9
NODES = 21
ORDER = 6
MPAD = 64
NPAD = 24
LANES = 128
FACES = 4 * NPAD
BF = jnp.bfloat16
F32 = jnp.float32


def rotations():
    degree = ORDER - 1
    nodes = [(a, b) for a in range(degree + 1) for b in range(degree + 1 - a)]
    lookup = {point: number for number, point in enumerate(nodes)}
    tables = []
    for rotation in range(3):
        row = []
        for a, b in nodes:
            triple = (a, b, degree - a - b)
            rolled = triple[rotation:] + triple[:rotation]
            row.append(lookup[rolled[0], rolled[1]])
        tables.append(row)
    return np.array(tables, dtype=np.int32)


def integral_weights(begin, end):
    return [(end ** (k + 1) - begin ** (k + 1)) / math.factorial(k + 1) for k in range(ORDER)]


def two_parts(x):
    high = x.astype(BF)
    low = (x - high.astype(F32)).astype(BF)
    return high, low


def outer_parts(x):
    high = lax.reduce_precision(x, 8, 7)
    return high, x - high


def field_lanes(f):
    return slice(f * LANES, (f + 1) * LANES)


def field_rows(f):
    return slice(f * MODES, (f + 1) * MODES)


def put_operand(xs_ref, f, x):
    x = jnp.concatenate([x, jnp.zeros((MPAD - MODES, LANES), F32)], axis=0)
    high, low = two_parts(x)
    lanes = field_lanes(f)
    xs_ref[0:MPAD, lanes] = high
    xs_ref[MPAD : 2 * MPAD, lanes] = low
    xs_ref[2 * MPAD : 3 * MPAD, lanes] = high


def big_dot(lhs, rhs):
    return jnp.dot(lhs, rhs, preferred_element_type=F32)


def wide_dot(lhs, xs_ref, y_ref):
    rows = lhs.shape[0]
    for f in range(0, FIELDS, 2):
        lanes = slice(f * LANES, min(f + 2, FIELDS) * LANES)
        y_ref[0:rows, lanes] = big_dot(lhs, xs_ref[:, lanes])


def star_sum(y_ref, star_ref, emit):
    for first in range(0, FIELDS, 3):
        sums = [None] * 3
        for d in range(3):
            for f in range(FIELDS):
                y = y_ref[d * MODES : (d + 1) * MODES, field_lanes(f)]
                for k in range(3):
                    scale = star_ref[d, f, first + k : first + k + 1, :]
                    term = y * scale
                    sums[k] = term if sums[k] is None else sums[k] + term
        for k in range(3):
            emit(first + k, sums[k])


def taylor(start_of, star_ref, forward, xs_ref, y_ref, integrals):
    for f in range(FIELDS):
        value = start_of(f)
        put_operand(xs_ref, f, value)
        for ref, weights in integrals:
            ref[field_rows(f), :] = weights[0] * value
    for k in range(1, ORDER):
        wide_dot(forward, xs_ref, y_ref)

        def emit(g, value, k=k):
            if k < ORDER - 1:
                put_operand(xs_ref, g, value)
            for ref, weights in integrals:
                ref[field_rows(g), :] = ref[field_rows(g), :] + weights[k] * value

        star_sum(y_ref, star_ref, emit)


def send_rims(xs_ref, halo_ref, sends):
    width = halo_ref.shape[1]
    element = lax.broadcasted_iota(jnp.int32, (LANES, width), 0)
    picks = []
    for r in range(4):
        pick = jnp.where(element == halo_ref[r : r + 1, :], 1.0, 0.0).astype(F32)
        picks.append(jnp.transpose(pick))
    pick = jnp.concatenate(picks, axis=0).astype(BF)
    for q in range((FIELDS + 1) // 2):
        if 2 * q + 1 < FIELDS:
            fields = (2 * q, 2 * q + 1)
        else:
            fields = (2 * q, 2 * q)
        total = None
        for piece in range(2):
            rows = slice(piece * MPAD, (piece + 1) * MPAD)
            both = jnp.concatenate([xs_ref[rows, field_lanes(f)] for f in fields], axis=0)
            part = lax.dot_general(
                pick, both, (((1,), (1,)), ((), ())), preferred_element_type=F32
            )
            total = part if total is None else total + part
        for r in range(4):
            sends[r][:, field_lanes(q)] = total[r * width : (r + 1) * width, :]


def local_pick(part, slot, face):
    target = jnp.where(part == 0, face * LANES + slot, -1)
    target = jnp.concatenate([target[i : i + 1, :] for i in range(4)], axis=1)
    row = lax.broadcasted_iota(jnp.int32, (4 * LANES, 4 * LANES), 0)
    return jnp.where(row == target, 1.0, 0.0).astype(BF)


def remote_pick(part, slot, width):
    target = jnp.where(part > 0, (part - 1) * width + slot, -1)
    target = jnp.concatenate([target[i : i + 1, :] for i in range(4)], axis=1)
    row = lax.broadcasted_iota(jnp.int32, (4 * width, 4 * LANES), 0)
    return jnp.where(row == target, 1.0, 0.0).astype(BF)


def pick_faces(y_ref, base_row, table_ref, pick):
    for f in range(FIELDS):
        for j in range(4):
            table_ref[f * NPAD : (f + 1) * NPAD, j * LANES : (j + 1) * LANES] = y_ref[
                base_row + j * NPAD : base_row + (j + 1) * NPAD, field_lanes(f)
            ]
    high, low = two_parts(table_ref[...])
    return big_dot(high, pick) + big_dot(low, pick)


def flux_sum(values_of, flux_ref, emit):
    for first in range(0, FIELDS, 3):
        sums = [[None] * 4 for _ in range(3)]
        for i in range(4):
            for f in range(FIELDS):
                value = values_of(i, f)
                for k in range(3):
                    term = value * flux_ref[i, f, first + k : first + k + 1, :]
                    old = sums[k][i]
                    sums[k][i] = term if old is None else old + term
        for k in range(3):
            emit(first + k, jnp.concatenate(sums[k], axis=0))


def turn_masks(turn):
    masks = []
    for h in range(3):
        rows = [
            jnp.broadcast_to(jnp.where(turn[i : i + 1, :] == h, 1.0, 0.0), (NPAD, LANES))
            for i in range(4)
        ]
        masks.append(jnp.concatenate(rows, axis=0).astype(BF))
    return masks


def stack_own(z_ref, g, value):
    high, low = two_parts(value)
    lanes = field_lanes(g)
    z_ref[0:FACES, lanes] = high
    z_ref[FACES : 2 * FACES, lanes] = low
    z_ref[2 * FACES : 3 * FACES, lanes] = high


def stack_turned(z_ref, base, g, value, masks):
    high, low = two_parts(value)
    lanes = field_lanes(g)
    for h in range(3):
        start = base + h * 3 * FACES
        turned = high * masks[h]
        z_ref[start : start + FACES, lanes] = turned
        z_ref[start + FACES : start + 2 * FACES, lanes] = low * masks[h]
        z_ref[start + 2 * FACES : start + 3 * FACES, lanes] = turned


def received_faces(received, pair_matrix, marks_ref, pick):
    rims = jnp.concatenate([ref[...] for ref in received], axis=0)
    high, low = two_parts(rims)
    parts = []
    for q in range((FIELDS + 1) // 2):
        lanes = field_lanes(q)
        rhs = jnp.concatenate([high[:, lanes], low[:, lanes], high[:, lanes]], axis=1)
        out = lax.dot_general(
            pair_matrix, rhs, (((1,), (1,)), ((), ())), preferred_element_type=F32
        )
        for side in range(2):
            if 2 * q + side < FIELDS:
                total = None
                for j in range(4):
                    start = side * FACES + j * NPAD
                    term = out[start : start + NPAD, :] * marks_ref[j : j + 1, :]
                    total = term if total is None else total + term
                parts.append(total)
    high, low = two_parts(jnp.concatenate(parts, axis=0))
    return big_dot(high, pick) + big_dot(low, pick)


def first_kernel(
    u_hbm, star_ref, forward_ref, halo_ref,
    u_ref, first_ref, second_ref, s0, s1, s2, s3, xs_ref, y_ref, sems,
):
    copies = []
    for f in range(FIELDS):
        copy = pltpu.make_async_copy(u_hbm.at[:, f, :], u_ref.at[field_rows(f), :], sems.at[f])
        copy.start()
        copies.append(copy)
    for copy in copies:
        copy.wait()
    taylor(
        lambda f: u_ref[field_rows(f), :], star_ref, forward_ref[...], xs_ref, y_ref,
        [(first_ref, integral_weights(0.0, 0.5)), (second_ref, integral_weights(0.5, 1.0))],
    )
    for f in range(FIELDS):
        put_operand(xs_ref, f, first_ref[field_rows(f), :])
    send_rims(xs_ref, halo_ref, (s0, s1, s2, s3))


def middle_local_kernel(
    u_ref, first_ref, star_ref, plus_ref, minus_ref, update_ref, lift_ref,
    part_ref, slot_ref, face_ref, turn_ref,
    base_ref, g_ref, marks_ref, xs_ref, y_ref, table_ref, z_ref,
):
    width = marks_ref.shape[1] // 4
    part, slot, face = part_ref[...], slot_ref[...], face_ref[...]
    for f in range(FIELDS):
        put_operand(xs_ref, f, first_ref[field_rows(f), :])
    wide_dot(update_ref[...], xs_ref, y_ref)
    g_ref[...] = pick_faces(y_ref, 3 * MODES, table_ref, local_pick(part, slot, face))
    far = remote_pick(part, slot, width)
    rows = [jnp.where(face == j, 1.0, 0.0) for j in range(4)]
    kinds = jnp.concatenate(
        [jnp.concatenate([row[i : i + 1, :] for i in range(4)], axis=1) for row in rows], axis=0
    )
    kinds = jnp.concatenate([kinds, jnp.zeros_like(kinds)], axis=0).astype(BF)
    marks_ref[...] = lax.dot_general(
        kinds, far, (((1,), (1,)), ((), ())), preferred_element_type=F32
    )
    finish_local(
        lambda f: u_ref[field_rows(f), :], star_ref, plus_ref, minus_ref, lift_ref,
        turn_ref[...], y_ref, g_ref, z_ref, base_ref,
    )


def finish_local(base_of, star_ref, plus_ref, minus_ref, lift_ref, turn, y_ref, g_ref, z_ref, base_ref):
    masks = turn_masks(turn)
    top = 3 * MODES
    flux_sum(
        lambda i, f: y_ref[top + i * NPAD : top + (i + 1) * NPAD, field_lanes(f)],
        plus_ref,
        lambda g, value: stack_own(z_ref, g, value),
    )
    flux_sum(
        lambda i, f: g_ref[f * NPAD : (f + 1) * NPAD, i * LANES : (i + 1) * LANES],
        minus_ref,
        lambda g, value: stack_turned(z_ref, 3 * FACES, g, value, masks),
    )

    def emit(g, value):
        base_ref[field_rows(g), :] = base_of(g) + value

    star_sum(y_ref, star_ref, emit)
    subtract_lift(lift_ref[...], z_ref, base_ref, base_ref)


def subtract_lift(lift, z_ref, base_ref, out_ref):
    for f in range(0, FIELDS, 2):
        fields = range(f, min(f + 2, FIELDS))
        lanes = slice(f * LANES, (fields[-1] + 1) * LANES)
        lifted = big_dot(lift, z_ref[:, lanes])
        for n, g in enumerate(fields):
            out_ref[field_rows(g), :] = base_ref[field_rows(g), :] - lifted[:, field_lanes(n)]


def middle_remote_kernel(
    r0, r1, r2, r3, u_ref, base_ref, g_ref, second_ref, star_ref, minus_ref,
    forward_ref, lift_ref, pair_ref, marks_ref, part_ref, slot_ref, turn_ref, cluster_ref, halo_ref,
    middle_ref, later_ref, gsum_ref, s0, s1, s2, s3, xs_ref, y_ref, z_ref, far_ref,
):
    pick = remote_pick(part_ref[...], slot_ref[...], r0.shape[0])
    far_ref[...] = received_faces((r0, r1, r2, r3), pair_ref[...], marks_ref, pick)
    gsum_ref[...] = g_ref[...] + far_ref[...]
    masks = turn_masks(turn_ref[...])
    flux_sum(
        lambda i, f: far_ref[f * NPAD : (f + 1) * NPAD, i * LANES : (i + 1) * LANES],
        minus_ref,
        lambda g, value: stack_turned(z_ref, 0, g, value, masks),
    )
    subtract_lift(lift_ref[:, 3 * FACES :], z_ref, base_ref, middle_ref)
    small = cluster_ref[...] == 0
    for f in range(FIELDS):
        middle_ref[field_rows(f), :] = jnp.where(
            small, middle_ref[field_rows(f), :], u_ref[field_rows(f), :]
        )
    taylor(
        lambda f: middle_ref[field_rows(f), :], star_ref, forward_ref[...], xs_ref, y_ref,
        [(later_ref, integral_weights(0.0, 0.5))],
    )
    for f in range(FIELDS):
        later = jnp.where(small, later_ref[field_rows(f), :], second_ref[field_rows(f), :])
        later_ref[field_rows(f), :] = later
        put_operand(xs_ref, f, later)
    send_rims(xs_ref, halo_ref, (s0, s1, s2, s3))


def last_local_kernel(
    u_ref, middle_ref, first_ref, second_ref, later_ref, gsum_ref, star_ref, plus_ref, minus_ref,
    update_ref, lift_ref, part_ref, slot_ref, face_ref, turn_ref, cluster_ref,
    base_ref, xs_ref, y_ref, table_ref, z_ref, g_ref,
):
    small = cluster_ref[...] == 0
    for f in range(FIELDS):
        put_operand(xs_ref, f, later_ref[field_rows(f), :])
    wide_dot(update_ref[3 * MODES :, :], xs_ref, y_ref)
    near = pick_faces(y_ref, 0, table_ref, local_pick(part_ref[...], slot_ref[...], face_ref[...]))
    large4 = jnp.concatenate([jnp.where(small, 0.0, 1.0)] * 4, axis=1)
    g_ref[...] = near + gsum_ref[...] * large4
    for f in range(FIELDS):
        rows = field_rows(f)
        put_operand(
            xs_ref, f, jnp.where(small, later_ref[rows, :], first_ref[rows, :] + second_ref[rows, :])
        )
    wide_dot(update_ref[...], xs_ref, y_ref)
    finish_local(
        lambda f: middle_ref[field_rows(f), :],
        star_ref, plus_ref, minus_ref, lift_ref, turn_ref[...], y_ref, g_ref, z_ref, base_ref,
    )


def last_remote_kernel(
    r0, r1, r2, r3, base_ref, minus_ref, lift_ref, pair_ref, marks_ref, part_ref, slot_ref, turn_ref,
    out_hbm, z_ref, far_ref, done_ref, sems,
):
    pick = remote_pick(part_ref[...], slot_ref[...], r0.shape[0])
    far_ref[...] = received_faces((r0, r1, r2, r3), pair_ref[...], marks_ref, pick)
    masks = turn_masks(turn_ref[...])
    flux_sum(
        lambda i, f: far_ref[f * NPAD : (f + 1) * NPAD, i * LANES : (i + 1) * LANES],
        minus_ref,
        lambda g, value: stack_turned(z_ref, 0, g, value, masks),
    )
    subtract_lift(lift_ref[:, 3 * FACES :], z_ref, base_ref, done_ref)
    copies = []
    for f in range(FIELDS):
        copy = pltpu.make_async_copy(done_ref.at[field_rows(f), :], out_hbm.at[:, f, :], sems.at[f])
        copy.start()
        copies.append(copy)
    for copy in copies:
        copy.wait()


def padded_to(x, shape):
    return jnp.pad(x, [(0, want - have) for have, want in zip(x.shape, shape)])


def triple(x):
    high, low = outer_parts(x)
    return jnp.concatenate([high, high, low], axis=-1).astype(BF)


def constants(stiffness, face_lift, face_project):
    forward = padded_to(stiffness, (3, MODES, MPAD)).reshape(3 * MODES, MPAD)
    backward = padded_to(jnp.transpose(stiffness, (0, 2, 1)), (3, MODES, MPAD))
    project = padded_to(face_project, (4, NPAD, MPAD)).reshape(FACES, MPAD)
    update = jnp.concatenate([backward.reshape(3 * MODES, MPAD), project], axis=0)
    zero = jnp.zeros_like(project)
    pair = jnp.concatenate(
        [jnp.concatenate([project, zero], axis=1), jnp.concatenate([zero, project], axis=1)], axis=0
    )
    lifts = []
    tables = rotations()
    for h in (0, 0, 1, 2):
        turned = face_lift[:, :, np.argsort(tables[h])]
        turned = padded_to(turned, (4, MODES, NPAD))
        lifts.append(triple(jnp.transpose(turned, (1, 0, 2)).reshape(MODES, FACES)))
    return triple(forward), triple(update), jnp.concatenate(lifts, axis=1), triple(pair)


VM = pl.BlockSpec(memory_space=pltpu.VMEM)
HB = pl.BlockSpec(memory_space=pl.ANY)
STATE = (FIELDS * MODES, LANES)
GATHERED = (FIELDS * NPAD, 4 * LANES)


def call(kernel, in_specs, outs, out_specs, scratch, name):
    return pl.pallas_call(
        kernel,
        out_shape=[jax.ShapeDtypeStruct(shape, F32) for shape in outs],
        in_specs=in_specs,
        out_specs=out_specs,
        scratch_shapes=scratch,
        compiler_params=pltpu.CompilerParams(vmem_limit_bytes=24 << 20),
        cost_estimate=pl.CostEstimate(flops=10**9, bytes_accessed=10**6, transcendentals=0),
        name=name,
    )


def scratch_xs():
    return pltpu.VMEM((3 * MPAD, FIELDS * LANES), BF)


def scratch_y(rows):
    return pltpu.VMEM((rows, FIELDS * LANES), F32)


def scratch_z(rows):
    return pltpu.VMEM((rows, FIELDS * LANES), BF)


def shift(x, axis, step):
    count = lax.axis_size(axis)
    return lax.ppermute(x, axis, [(i, (i + step) % count) for i in range(count)])


def trade(sends):
    return (
        shift(sends[0], "near", 1),
        shift(sends[1], "near", -1),
        shift(sends[2], "dom", 1),
        shift(sends[3], "dom", -1),
    )


def on_device(
    u, star, plus, minus, stiffness, face_lift, face_project,
    cluster, part, slot, face, turn, halo,
):
    width = halo.shape[1]
    cluster = cluster.reshape(1, LANES)
    forward, update, lift, pair = constants(stiffness, face_lift, face_project)
    rim = (width, 5 * LANES)
    ufm, first, second, *sends = call(
        first_kernel, [HB, VM, VM, VM], [STATE] * 3 + [rim] * 4, [VM] * 7,
        [scratch_xs(), scratch_y(3 * MODES), pltpu.SemaphoreType.DMA((FIELDS,))], "first",
    )(u, star, forward, halo)
    received = trade(sends)
    rows = 3 * MODES + FACES
    base, g, marks = call(
        middle_local_kernel, [VM] * 11, [STATE, GATHERED, (8, 4 * width)], [VM] * 3,
        [scratch_xs(), scratch_y(rows), pltpu.VMEM(GATHERED, F32), scratch_z(12 * FACES)],
        "middle_local",
    )(ufm, first, star, plus, minus, update, lift, part, slot, face, turn)
    middle, later, gsum, *sends = call(
        middle_remote_kernel, [VM] * 19, [STATE, STATE, GATHERED] + [rim] * 4, [VM] * 7,
        [scratch_xs(), scratch_y(3 * MODES), scratch_z(9 * FACES), pltpu.VMEM(GATHERED, F32)],
        "middle_remote",
    )(
        *received, ufm, base, g, second, star, minus, forward, lift, pair, marks,
        part, slot, turn, cluster, halo,
    )
    received = trade(sends)
    (base,) = call(
        last_local_kernel, [VM] * 16, [STATE], [VM],
        [
            scratch_xs(), scratch_y(rows), pltpu.VMEM(GATHERED, F32), scratch_z(12 * FACES),
            pltpu.VMEM(GATHERED, F32),
        ],
        "last_local",
    )(
        ufm, middle, first, second, later, gsum, star, plus, minus, update, lift,
        part, slot, face, turn, cluster,
    )
    (out,) = call(
        last_remote_kernel, [VM] * 12, [u.shape], [HB],
        [
            scratch_z(9 * FACES), pltpu.VMEM(GATHERED, F32), pltpu.VMEM(STATE, F32),
            pltpu.SemaphoreType.DMA((FIELDS,)),
        ],
        "last_remote",
    )(*received, base, minus, lift, pair, marks, part, slot, turn)
    return out


def solution(mesh):
    both = ("dom", "near")
    in_specs = (
        P(None, None, both), P(None, None, None, both), P(None, None, None, both),
        P(None, None, None, both), P(), P(), P(), P(both),
        P(None, both), P(None, both), P(None, both), P(None, both), P(None, both),
    )
    return jax.shard_map(
        on_device, mesh=mesh, in_specs=in_specs, out_specs=P(None, None, both), check_vma=False
    )
```

profile of v0, /device:TPU:0, one launch (start us, length us, event | category | flops | bytes accessed | tf_op | source)
XLA Modules:
  0.0 44.6 jit_solution(6741271479393744242)
XLA Ops:
  0.0 0.9 %pad.26 = f32[3,56,64]{2,1,0:T(8,128)S(1)} pad(f32[3,56,56]{2,1,0:T(8,128)} %param.25, f32[]{:T(128)} %constant.5.clone.1), padding=0_0x0_0x0_8 | pad | bytes 80644 | tf_op jit(solution)/shard_map/jit(_pad)/pad | solution.py:383
  1.0 0.9 %copy-done.8 = f32[56,9,128]{2,0,1:T(8,128)S(1)} copy-done((f32[56,9,128]{2,0,1:T(8,128)S(1)}, f32[56,9,128]{2,0,1:T(8,128)}, u32[]{:S(2)}) %copy-start.8) | copy-done | bytes 258072
  2.1 0.6 %copy-done.1 = s32[4,16]{1,0:T(4,128)S(1)} copy-done((s32[4,16]{1,0:T(4,128)S(1)}, s32[4,16]{1,0:T(4,128)}, u32[]{:S(2)}) %copy-start.1) | copy-done | bytes 280
  2.7 5.0 %first.1 = (f32[504,128]{1,0:T(8,128)S(1)}, f32[504,128]{1,0:T(8,128)S(1)}, f32[504,128]{1,0:T(8,128)S(1)}, f32[16,640]{1,0:T(8,128)S(1)}, f32[16,640]{1,0:T(8,1...) custom-call(f32[56,9,128]{2,1,0:T(8,128)S(1)} %copy.39.u_hbm, f32[3,9,9,128]{3,2,1,0:T(8,128)S(1)} %copy.40.star_ref, ...), custom_call_target="tpu_custom_call" | custom-call | flops 1000000000 | bytes 1000000 | tf_op jit(solution)/shard_map/first/pallas_call | solution.py:462
  8.2 2.0 %collective-permute-start.1 = (f32[16,640]{1,0:T(8,128)S(1)}, f32[16,640]{1,0:T(8,128)S(1)}, u32[]{:S(2)}, u32[]{:S(2)}) collective-permute-start(f32[16,640]{1,0:T(8,128)S(1)} %get-tuple-element.23), channel_id=1, source_target_pairs={{0,3},{1,0},{2,1},{3,2},{4,7},{5,4},{6,5},{7,6},{8,11},{9,8},{10,9... | collective-permute-start | bytes 122888 | tf_op jit(solution)/shard_map/ppermute | solution.py:442
  10.2 2.3 %collective-permute-start.2 = (f32[16,640]{1,0:T(8,128)S(1)}, f32[16,640]{1,0:T(8,128)S(1)}, u32[]{:S(2)}, u32[]{:S(2)}) collective-permute-start(f32[16,640]{1,0:T(8,128)S(1)} %get-tuple-element.24), channel_id=1, source_target_pairs={{0,4},{4,8},{8,12},{12,16},{16,20},{20,24},{24,28},{28,0},{1,5},{5... | collective-permute-start | bytes 122888 | tf_op jit(solution)/shard_map/ppermute | solution.py:442
  12.5 3.0 %collective-permute-start.3 = (f32[16,640]{1,0:T(8,128)S(1)}, f32[16,640]{1,0:T(8,128)S(1)}, u32[]{:S(2)}, u32[]{:S(2)}) collective-permute-start(f32[16,640]{1,0:T(8,128)S(1)} %get-tuple-element.25), channel_id=1, source_target_pairs={{0,28},{4,0},{8,4},{12,8},{16,12},{20,16},{24,20},{28,24},{1,29},{... | collective-permute-start | bytes 122888 | tf_op jit(solution)/shard_map/ppermute | solution.py:442
  15.5 0.6 %copy-done.14 = s32[21]{0:T(128)S(1)} copy-done((s32[21]{0:T(128)S(1)}, s32[21]{0:T(128)}, u32[]{:S(2)}) %copy-start.14) | copy-done | bytes 108
  16.2 0.6 %copy-done.13 = s32[21]{0:T(128)S(1)} copy-done((s32[21]{0:T(128)S(1)}, s32[21]{0:T(128)}, u32[]{:S(2)}) %copy-start.13) | copy-done | bytes 108
  16.8 0.6 %gather_fusion.2 = f32[21,4,56]{2,1,0:T(4,128)S(1)} fusion(f32[4,56,21]{1,0,2:T(4,128)S(1)} %copy-done, s32[1024]{0:T(1024)S(1)} %pad_clamp_fusion), kind=kCustom, calls=%fused_computation.2 | custom fusion | bytes 37716 | tf_op jit(solution)/shard_map/gather | solution.py:403
  17.6 0.6 %gather_fusion.1 = f32[21,4,56]{2,1,0:T(4,128)S(1)} fusion(f32[4,56,21]{1,0,2:T(4,128)S(1)} %copy-done, s32[1024]{0:T(1024)S(1)} %pad_clamp_fusion.1), kind=kCustom, calls=%fused_computation.1 | custom fusion | bytes 37716 | tf_op jit(solution)/shard_map/gather | solution.py:403
  18.3 0.6 %gather_fusion = f32[21,4,56]{2,1,0:T(4,128)S(1)} fusion(f32[4,56,21]{1,0,2:T(4,128)S(1)} %copy-done, s32[1024]{0:T(1024)S(1)} %pad_clamp_fusion.2), kind=kCustom, calls=%fused_computation | custom fusion | bytes 37716 | tf_op jit(solution)/shard_map/gather | solution.py:403
  19.0 0.7 %copy-done.12 = f32[4,21,56]{2,0,1:T(4,128)S(1)} copy-done((f32[4,21,56]{2,0,1:T(4,128)S(1)}, f32[4,21,56]{2,0,1:T(4,128)}, u32[]{:S(2)}) %copy-start.12) | copy-done | bytes 18840
  19.7 0.9 %copy-done.7 = f32[3,56,56]{2,1,0:T(8,128)S(1)} copy-done((f32[3,56,56]{2,1,0:T(8,128)S(1)}, f32[3,56,56]{2,1,0:T(8,128)}, u32[]{:S(2)}) %copy-start.7) | copy-done | bytes 37656
  20.8 0.9 %copy-done.9 = f32[4,9,9,128]{3,0,2,1:T(4,128)S(1)} copy-done((f32[4,9,9,128]{3,0,2,1:T(4,128)S(1)}, f32[4,9,9,128]{3,0,2,1:T(4,128)}, u32[]{:S(2)}) %copy-start.9) | copy-done | bytes 165912
  21.7 0.9 %copy-done.10 = f32[4,9,9,128]{3,0,2,1:T(4,128)S(1)} copy-done((f32[4,9,9,128]{3,0,2,1:T(4,128)S(1)}, f32[4,9,9,128]{3,0,2,1:T(4,128)}, u32[]{:S(2)}) %copy-start.10) | copy-done | bytes 165912
  23.7 2.4 %middle_local.1 = (f32[504,128]{1,0:T(8,128)S(1)}, f32[216,512]{1,0:T(8,128)S(1)}, f32[8,64]{1,0:T(8,128)S(1)}) custom-call(f32[504,128]{1,0:T(8,128)S(1)} %get-tuple-element.26.u_ref, f32[504,128]{1,0:T(8,128)S(1)} %get-tuple-element.27.first_ref, f32[3,9,9,128]{3,2,1,0:T(8,128)S(1)} %copy.40.star_ref, f32[4,9,9,128]{3,2,1,0:T(8,128)S(1)} %copy.53.plus_ref, ...), custom_call_target="tpu_custom_call" | custom-call | flops 1000000000 | bytes 1000000 | tf_op jit(solution)/shard_map/middle_local/pallas_call | solution.py:468
  26.2 0.6 %copy-done.6 = s32[128]{0:T(128)S(1)} copy-done((s32[128]{0:T(128)S(1)}, s32[128]{0:T(128)}, u32[]{:S(2)}) %copy-start.6) | copy-done | bytes 536
  26.8 6.0 %middle_remote.1 = (f32[504,128]{1,0:T(8,128)S(1)}, f32[504,128]{1,0:T(8,128)S(1)}, f32[216,512]{1,0:T(8,128)S(1)}, f32[16,640]{1,0:T(8,128)S(1)}, f32[16,640]{1...) custom-call(f32[16,640]{1,0:T(8,128)S(1)} %collective-permute-done.r0, ...), custom_call_target="tpu_custom_call" | custom-call | flops 1000000000 | bytes 1000000 | tf_op jit(solution)/shard_map/middle_remote/pallas_call | solution.py:473
  32.8 1.7 %collective-permute-start.5 = (f32[16,640]{1,0:T(8,128)S(1)}, f32[16,640]{1,0:T(8,128)S(1)}, u32[]{:S(2)}, u32[]{:S(2)}) collective-permute-start(f32[16,640]{1,0:T(8,128)S(1)} %get-tuple-element.33), channel_id=1, source_target_pairs={{0,3},{1,0},{2,1},{3,2},{4,7},{5,4},{6,5},{7,6},{8,11},{9,8},{10,9... | collective-permute-start | bytes 122888 | tf_op jit(solution)/shard_map/ppermute | solution.py:442
  34.6 4.7 %collective-permute-start.7 = (f32[16,640]{1,0:T(8,128)S(1)}, f32[16,640]{1,0:T(8,128)S(1)}, u32[]{:S(2)}, u32[]{:S(2)}) collective-permute-start(f32[16,640]{1,0:T(8,128)S(1)} %get-tuple-element.35), channel_id=1, source_target_pairs={{0,28},{4,0},{8,4},{12,8},{16,12},{20,16},{24,20},{28,24},{1,29},{... | collective-permute-start | bytes 122888 | tf_op jit(solution)/shard_map/ppermute | solution.py:442
  39.3 2.6 %last_local.1.base_ref = f32[504,128]{1,0:T(8,128)S(1)} custom-call(f32[504,128]{1,0:T(8,128)S(1)} %get-tuple-element.26.u_ref, f32[504,128]{1,0:T(8,128)S(1)} %get-tuple-element.36.middle_ref, f32[504,128]{1,0:T(8,128)S(1)} %get-tuple-element.27.first_ref, f32[504,128]{1,0:T(8,128)S(1)} %get-tuple-element.30.second_ref, ...), custom_call_target="tpu_custom_call" | custom-call | flops 1000000000 | bytes 1000000 | tf_op jit(solution)/shard_map/last_local/pallas_call | solution.py:482
  42.0 1.8 %last_remote.1 = f32[56,9,128]{2,1,0:T(8,128)S(1)} custom-call(f32[16,640]{1,0:T(8,128)S(1)} %collective-permute-done.4.r0, f32[16,640]{1,0:T(8,128)S(1)} %collective-permute-done.5.r1, f32[16,640]{1,0:T(8,128)S(1)} %collective-permute-done.6.r2, f32[16,640]{1,0:T(8,128)S(1)} %collective-permute-done.7.r3, f32[504,128]{1,0:T(8,128)S(1)} %last_local.1.base_ref, ...), custom_call_target="tpu_custom_call" | custom-call | flops 1000000000 | bytes 1000000 | tf_op jit(solution)/shard_map/last_remote/pallas_call | solution.py:493
  43.8 0.8 %copy.61 = f32[56,9,128]{2,0,1:T(8,128)} copy(f32[56,9,128]{2,1,0:T(8,128)S(1)} %last_remote.1) | data formatting | bytes 516096 | tf_op jit(solution)/shard_map/last_remote/pallas_call | solution.py:493
  (62 shorter events, 2.4 us)
Async XLA Ops:
  0.0 16.8 %copy-start = (f32[4,56,21]{1,0,2:T(4,128)S(1)}, f32[4,56,21]{1,0,2:T(4,128)}, u32[]{:S(2)}) copy-start(f32[4,56,21]{1,0,2:T(4,128)} %param.26) | copy-start | bytes 56452
  0.0 1.0 %copy-start.11 = (f32[3,9,9,128]{3,0,2,1:T(4,128)S(1)}, f32[3,9,9,128]{3,0,2,1:T(4,128)}, u32[]{:S(2)}) copy-start(f32[3,9,9,128]{3,0,2,1:T(4,128)} %param.22) | copy-start | bytes 373252
  0.9 1.0 %copy-start.8 = (f32[56,9,128]{2,0,1:T(8,128)S(1)}, f32[56,9,128]{2,0,1:T(8,128)}, u32[]{:S(2)}) copy-start(f32[56,9,128]{2,0,1:T(8,128)} %param.21) | copy-start | bytes 774148
  2.0 0.7 %copy-start.1 = (s32[4,16]{1,0:T(4,128)S(1)}, s32[4,16]{1,0:T(4,128)}, u32[]{:S(2)}) copy-start(s32[4,16]{1,0:T(4,128)} %halo_ref.3) | copy-start | bytes 772
  7.7 18.4 %collective-permute-start = (f32[16,640]{1,0:T(8,128)S(1)}, f32[16,640]{1,0:T(8,128)S(1)}, u32[]{:S(2)}, u32[]{:S(2)}) collective-permute-start(f32[16,640]{1,0:T(8,128)S(1)} %get-tuple-element.22), channel_id=1, source_target_pairs={{0,1},{1,2},{2,3},{3,0},{4,5},{5,6},{6,7},{7,4},{8,9},{9,10},{10,1... | collective-permute-start | bytes 122888 | tf_op jit(solution)/shard_map/ppermute | solution.py:442
  8.2 17.9 %collective-permute-start.1 = (f32[16,640]{1,0:T(8,128)S(1)}, f32[16,640]{1,0:T(8,128)S(1)}, u32[]{:S(2)}, u32[]{:S(2)}) collective-permute-start(f32[16,640]{1,0:T(8,128)S(1)} %get-tuple-element.23), channel_id=1, source_target_pairs={{0,3},{1,0},{2,1},{3,2},{4,7},{5,4},{6,5},{7,6},{8,11},{9,8},{10,9... | collective-permute-start | bytes 122888 | tf_op jit(solution)/shard_map/ppermute | solution.py:442
  10.2 15.9 %collective-permute-start.2 = (f32[16,640]{1,0:T(8,128)S(1)}, f32[16,640]{1,0:T(8,128)S(1)}, u32[]{:S(2)}, u32[]{:S(2)}) collective-permute-start(f32[16,640]{1,0:T(8,128)S(1)} %get-tuple-element.24), channel_id=1, source_target_pairs={{0,4},{4,8},{8,12},{12,16},{16,20},{20,24},{24,28},{28,0},{1,5},{5... | collective-permute-start | bytes 122888 | tf_op jit(solution)/shard_map/ppermute | solution.py:442
  12.5 13.7 %collective-permute-start.3 = (f32[16,640]{1,0:T(8,128)S(1)}, f32[16,640]{1,0:T(8,128)S(1)}, u32[]{:S(2)}, u32[]{:S(2)}) collective-permute-start(f32[16,640]{1,0:T(8,128)S(1)} %get-tuple-element.25), channel_id=1, source_target_pairs={{0,28},{4,0},{8,4},{12,8},{16,12},{20,16},{24,20},{28,24},{1,29},{... | collective-permute-start | bytes 122888 | tf_op jit(solution)/shard_map/ppermute | solution.py:442
  15.5 0.7 %copy-start.14 = (s32[21]{0:T(128)S(1)}, s32[21]{0:T(128)}, u32[]{:S(2)}) copy-start(s32[21]{0:T(128)} %constant.38) | copy-start | bytes 256
  16.2 0.7 %copy-start.13 = (s32[21]{0:T(128)S(1)}, s32[21]{0:T(128)}, u32[]{:S(2)}) copy-start(s32[21]{0:T(128)} %constant.39) | copy-start | bytes 256
  18.9 0.8 %copy-start.12 = (f32[4,21,56]{2,0,1:T(4,128)S(1)}, f32[4,21,56]{2,0,1:T(4,128)}, u32[]{:S(2)}) copy-start(f32[4,21,56]{2,0,1:T(4,128)} %param.27) | copy-start | bytes 56452
  19.7 0.9 %copy-start.7 = (f32[3,56,56]{2,1,0:T(8,128)S(1)}, f32[3,56,56]{2,1,0:T(8,128)}, u32[]{:S(2)}) copy-start(f32[3,56,56]{2,1,0:T(8,128)} %param.25) | copy-start | bytes 112900
  20.8 0.9 %copy-start.9 = (f32[4,9,9,128]{3,0,2,1:T(4,128)S(1)}, f32[4,9,9,128]{3,0,2,1:T(4,128)}, u32[]{:S(2)}) copy-start(f32[4,9,9,128]{3,0,2,1:T(4,128)} %param.24) | copy-start | bytes 497668
  21.7 0.9 %copy-start.10 = (f32[4,9,9,128]{3,0,2,1:T(4,128)S(1)}, f32[4,9,9,128]{3,0,2,1:T(4,128)}, u32[]{:S(2)}) copy-start(f32[4,9,9,128]{3,0,2,1:T(4,128)} %param.23) | copy-start | bytes 497668
  22.8 0.7 %copy-start.3 = (s32[4,128]{1,0:T(4,128)S(1)}, s32[4,128]{1,0:T(4,128)}, u32[]{:S(2)}) copy-start(s32[4,128]{1,0:T(4,128)} %part_ref.7) | copy-start | bytes 6148
  22.8 0.7 %copy-start.4 = (s32[4,128]{1,0:T(4,128)S(1)}, s32[4,128]{1,0:T(4,128)}, u32[]{:S(2)}) copy-start(s32[4,128]{1,0:T(4,128)} %slot_ref.7) | copy-start | bytes 6148
  22.8 0.7 %copy-start.5 = (s32[4,128]{1,0:T(4,128)S(1)}, s32[4,128]{1,0:T(4,128)}, u32[]{:S(2)}) copy-start(s32[4,128]{1,0:T(4,128)} %turn_ref.7) | copy-start | bytes 6148
  23.0 0.7 %copy-start.2 = (s32[4,128]{1,0:T(4,128)S(1)}, s32[4,128]{1,0:T(4,128)}, u32[]{:S(2)}) copy-start(s32[4,128]{1,0:T(4,128)} %face_ref.3) | copy-start | bytes 6148
  26.2 0.7 %copy-start.6 = (s32[128]{0:T(128)S(1)}, s32[128]{0:T(128)}, u32[]{:S(2)}) copy-start(s32[128]{0:T(128)} %param.28) | copy-start | bytes 1540
  32.8 9.1 %collective-permute-start.4 = (f32[16,640]{1,0:T(8,128)S(1)}, f32[16,640]{1,0:T(8,128)S(1)}, u32[]{:S(2)}, u32[]{:S(2)}) collective-permute-start(f32[16,640]{1,0:T(8,128)S(1)} %get-tuple-element.32), channel_id=1, source_target_pairs={{0,1},{1,2},{2,3},{3,0},{4,5},{5,6},{6,7},{7,4},{8,9},{9,10},{10,1... | collective-permute-start | bytes 122888 | tf_op jit(solution)/shard_map/ppermute | solution.py:442
  32.8 9.1 %collective-permute-start.5 = (f32[16,640]{1,0:T(8,128)S(1)}, f32[16,640]{1,0:T(8,128)S(1)}, u32[]{:S(2)}, u32[]{:S(2)}) collective-permute-start(f32[16,640]{1,0:T(8,128)S(1)} %get-tuple-element.33), channel_id=1, source_target_pairs={{0,3},{1,0},{2,1},{3,2},{4,7},{5,4},{6,5},{7,6},{8,11},{9,8},{10,9... | collective-permute-start | bytes 122888 | tf_op jit(solution)/shard_map/ppermute | solution.py:442
  34.6 7.4 %collective-permute-start.6 = (f32[16,640]{1,0:T(8,128)S(1)}, f32[16,640]{1,0:T(8,128)S(1)}, u32[]{:S(2)}, u32[]{:S(2)}) collective-permute-start(f32[16,640]{1,0:T(8,128)S(1)} %get-tuple-element.34), channel_id=1, source_target_pairs={{0,4},{4,8},{8,12},{12,16},{16,20},{20,24},{24,28},{28,0},{1,5},{5... | collective-permute-start | bytes 122888 | tf_op jit(solution)/shard_map/ppermute | solution.py:442
  34.6 7.4 %collective-permute-start.7 = (f32[16,640]{1,0:T(8,128)S(1)}, f32[16,640]{1,0:T(8,128)S(1)}, u32[]{:S(2)}, u32[]{:S(2)}) collective-permute-start(f32[16,640]{1,0:T(8,128)S(1)} %get-tuple-element.35), channel_id=1, source_target_pairs={{0,28},{4,0},{8,4},{12,8},{16,12},{20,16},{24,20},{28,24},{1,29},{... | collective-permute-start | bytes 122888 | tf_op jit(solution)/shard_map/ppermute | solution.py:442
where the time goes:
time: 45 us; the launch traced here: 44.6 us
  Pallas kernels  17.9 us (40%)
  starting transfers between devices  14.3 us (32%)
  local copies, waits for them, and re-layouts  11.6 us (26%)
    ppermute x8, starting transfers between devices, shift(): lax.ppermute(x, axis, [(i, (i + step) % count) for i in range(count)])  14.3 us
    unnamed x36, local copies, waits for them, and re-layouts  7.68 us
    pallas_call x1, Pallas kernels, on_device(): call(middle_remote_kernel, [VM] * 19, [STATE, STATE, GATHERED] + [rim] *...  5.98 us
    pallas_call x1, Pallas kernels, on_device(): call(first_kernel, [HB, VM, VM, VM], [STATE] * 3 + [rim] * 4, [VM] * 7, [...  5 us
    pallas_call x1, Pallas kernels, on_device(): call(last_local_kernel, [VM] * 16, [STATE], [VM], [scratch_xs(), scratch_...  2.64 us
    pallas_call x1, Pallas kernels, on_device(): call(middle_local_kernel, [VM] * 11, [STATE, GATHERED, (8, 4 * width)], [...  2.43 us
    pallas_call x1, Pallas kernels, on_device(): call(last_remote_kernel, [VM] * 12, [u.shape], [HB], [scratch_z(9 * FACES...  1.83 us
    gather x3, local copies, waits for them, and re-layouts, constants(): turned = face_lift[:, :, np.argsort(tables[h])]  1.79 us
  transfers between devices with their start and end apart: 8, of which 0 were waited for; matrix products, arithmetic and copies ran while one was open for 6% of the time, Pallas kernels for 11%

commit v1 on v0

--- a/solution.py
+++ b/solution.py
@@ -46,8 +46,8 @@
     return high, low
 
 
-def outer_parts(x):
-    high = lax.reduce_precision(x, 8, 7)
+def float_parts(x):
+    high = x.astype(BF).astype(F32)
     return high, x - high
 
 
@@ -86,7 +86,7 @@
             for f in range(FIELDS):
                 y = y_ref[d * MODES : (d + 1) * MODES, field_lanes(f)]
                 for k in range(3):
-                    scale = star_ref[d, f, first + k : first + k + 1, :]
+                    scale = star_ref[f, first + k, d : d + 1, :]
                     term = y * scale
                     sums[k] = term if sums[k] is None else sums[k] + term
         for k in range(3):
@@ -111,19 +111,22 @@
         star_sum(y_ref, star_ref, emit)
 
 
+def evens():
+    return [lax.rem(lax.axis_index(axis), 2) == 0 for axis in ("near", "dom")]
+
+
 def send_rims(xs_ref, halo_ref, sends):
     width = halo_ref.shape[1]
     element = lax.broadcasted_iota(jnp.int32, (LANES, width), 0)
     picks = []
-    for r in range(4):
-        pick = jnp.where(element == halo_ref[r : r + 1, :], 1.0, 0.0).astype(F32)
-        picks.append(jnp.transpose(pick))
+    for axis, even in enumerate(evens()):
+        up, down = halo_ref[2 * axis : 2 * axis + 1, :], halo_ref[2 * axis + 1 : 2 * axis + 2, :]
+        for row in (jnp.where(even, up, down), jnp.where(even, down, up)):
+            pick = jnp.where(element == row, 1.0, 0.0).astype(F32)
+            picks.append(jnp.transpose(pick))
     pick = jnp.concatenate(picks, axis=0).astype(BF)
     for q in range((FIELDS + 1) // 2):
-        if 2 * q + 1 < FIELDS:
-            fields = (2 * q, 2 * q + 1)
-        else:
-            fields = (2 * q, 2 * q)
+        fields = (2 * q, min(2 * q + 1, FIELDS - 1))
         total = None
         for piece in range(2):
             rows = slice(piece * MPAD, (piece + 1) * MPAD)
@@ -144,7 +147,11 @@
 
 
 def remote_pick(part, slot, width):
-    target = jnp.where(part > 0, (part - 1) * width + slot, -1)
+    near_even, dom_even = evens()
+    near_block = jnp.where(near_even, 2 - part, part - 1)
+    dom_block = jnp.where(dom_even, 6 - part, part - 1)
+    block = jnp.where(part > 2, dom_block, near_block)
+    target = jnp.where(part > 0, block * width + slot, -1)
     target = jnp.concatenate([target[i : i + 1, :] for i in range(4)], axis=1)
     row = lax.broadcasted_iota(jnp.int32, (4 * width, 4 * LANES), 0)
     return jnp.where(row == target, 1.0, 0.0).astype(BF)
@@ -167,7 +174,7 @@
             for f in range(FIELDS):
                 value = values_of(i, f)
                 for k in range(3):
-                    term = value * flux_ref[i, f, first + k : first + k + 1, :]
+                    term = value * flux_ref[f, first + k, i : i + 1, :]
                     old = sums[k][i]
                     sums[k][i] = term if old is None else old + term
         for k in range(3):
@@ -186,22 +193,27 @@
 
 
 def stack_own(z_ref, g, value):
-    high, low = two_parts(value)
     lanes = field_lanes(g)
-    z_ref[0:FACES, lanes] = high
-    z_ref[FACES : 2 * FACES, lanes] = low
-    z_ref[2 * FACES : 3 * FACES, lanes] = high
-
-
-def stack_turned(z_ref, base, g, value, masks):
-    high, low = two_parts(value)
+    for piece, part in enumerate(two_parts(value)):
+        z_ref[piece, 3 * FACES : 4 * FACES, lanes] = part
+
+
+def stack_turned(z_ref, g, value, masks):
     lanes = field_lanes(g)
-    for h in range(3):
-        start = base + h * 3 * FACES
-        turned = high * masks[h]
-        z_ref[start : start + FACES, lanes] = turned
-        z_ref[start + FACES : start + 2 * FACES, lanes] = low * masks[h]
-        z_ref[start + 2 * FACES : start + 3 * FACES, lanes] = turned
+    for piece, part in enumerate(two_parts(value)):
+        for h in range(3):
+            z_ref[piece, h * FACES : (h + 1) * FACES, lanes] = part * masks[h]
+
+
+def subtract_lift(lift_ref, rows, z_ref, base_ref, out_ref):
+    both = lift_ref[:, 0:rows]
+    for f in range(0, FIELDS, 2):
+        fields = range(f, min(f + 2, FIELDS))
+        lanes = slice(f * LANES, (fields[-1] + 1) * LANES)
+        high = big_dot(both, z_ref[0, 0:rows, lanes])
+        lifted = high[0:MODES] + high[MODES:] + big_dot(both[0:MODES], z_ref[1, 0:rows, lanes])
+        for n, g in enumerate(fields):
+            out_ref[field_rows(g), :] = base_ref[field_rows(g), :] - lifted[:, field_lanes(n)]
 
 
 def received_faces(received, pair_matrix, marks_ref, pick):
@@ -226,17 +238,56 @@
     return big_dot(high, pick) + big_dot(low, pick)
 
 
+def wide(x):
+    return jnp.concatenate([x, jnp.zeros((x.shape[0], LANES - x.shape[1]), F32)], axis=1)
+
+
+def tall(x, rows):
+    return jnp.concatenate([x, jnp.zeros((rows - x.shape[0], x.shape[1]), F32)], axis=0)
+
+
+def tripled(x):
+    high, low = float_parts(x)
+    first = high + pltpu.roll(high, MPAD, 1)
+    return jnp.concatenate([first, low], axis=1).astype(BF)[:, 0 : 3 * MPAD]
+
+
+def forward_matrix(stiff_ref):
+    return tripled(jnp.concatenate([wide(stiff_ref[d]) for d in range(3)], axis=0))
+
+
+def prepare(stiff_ref, lift_ref, project_ref, update_ref, lifts_ref, pair_ref, rows_ref):
+    backward = [
+        jnp.transpose(tall(wide(stiff_ref[d]), LANES))[0:MODES, :] for d in range(3)
+    ]
+    project = jnp.concatenate(
+        [wide(tall(project_ref[:, j, :], NPAD)) for j in range(4)], axis=0
+    )
+    update_ref[...] = tripled(jnp.concatenate(backward + [project], axis=0))
+    high, low = float_parts(project)
+    moved = [pltpu.roll(part, MPAD, 1) for part in (high, low)]
+    highs = jnp.concatenate([high, moved[0]], axis=0).astype(BF)
+    lows = jnp.concatenate([low, moved[1]], axis=0).astype(BF)
+    pair_ref[...] = jnp.concatenate([highs, highs, lows], axis=1)
+    rows_ref[...] = jnp.zeros(rows_ref.shape, F32)
+    tables = rotations()
+    for block, h in enumerate((0, 1, 2, 0)):
+        for i in range(4):
+            for p in range(NODES):
+                row = block * FACES + i * NPAD + int(tables[h][p])
+                rows_ref[row : row + 1, 0:MODES] = lift_ref[p, i : i + 1, :]
+    columns = []
+    for t in range(4 * FACES // LANES):
+        columns.append(jnp.transpose(rows_ref[t * LANES : (t + 1) * LANES, :])[0:MODES, :])
+    high, low = float_parts(jnp.concatenate(columns, axis=1))
+    lifts_ref[...] = jnp.concatenate([high, low], axis=0).astype(BF)
+
+
 def first_kernel(
-    u_hbm, star_ref, forward_ref, halo_ref,
-    u_ref, first_ref, second_ref, s0, s1, s2, s3, xs_ref, y_ref, sems,
+    u_ref, star_ref, stiff_ref, halo_ref,
+    first_ref, second_ref, forward_ref, s0, s1, s2, s3, xs_ref, y_ref,
 ):
-    copies = []
-    for f in range(FIELDS):
-        copy = pltpu.make_async_copy(u_hbm.at[:, f, :], u_ref.at[field_rows(f), :], sems.at[f])
-        copy.start()
-        copies.append(copy)
-    for copy in copies:
-        copy.wait()
+    forward_ref[...] = forward_matrix(stiff_ref)
     taylor(
         lambda f: u_ref[field_rows(f), :], star_ref, forward_ref[...], xs_ref, y_ref,
         [(first_ref, integral_weights(0.0, 0.5)), (second_ref, integral_weights(0.5, 1.0))],
@@ -247,11 +298,13 @@
 
 
 def middle_local_kernel(
-    u_ref, first_ref, star_ref, plus_ref, minus_ref, update_ref, lift_ref,
+    u_ref, first_ref, star_ref, plus_ref, minus_ref, stiff_ref, face_lift_ref, project_ref,
     part_ref, slot_ref, face_ref, turn_ref,
-    base_ref, g_ref, marks_ref, xs_ref, y_ref, table_ref, z_ref,
+    base_ref, g_ref, marks_ref, update_ref, lift_ref, pair_ref,
+    xs_ref, y_ref, table_ref, z_ref, rows_ref,
 ):
     width = marks_ref.shape[1] // 4
+    prepare(stiff_ref, face_lift_ref, project_ref, update_ref, lift_ref, pair_ref, rows_ref)
     part, slot, face = part_ref[...], slot_ref[...], face_ref[...]
     for f in range(FIELDS):
         put_operand(xs_ref, f, first_ref[field_rows(f), :])
@@ -283,23 +336,14 @@
     flux_sum(
         lambda i, f: g_ref[f * NPAD : (f + 1) * NPAD, i * LANES : (i + 1) * LANES],
         minus_ref,
-        lambda g, value: stack_turned(z_ref, 3 * FACES, g, value, masks),
+        lambda g, value: stack_turned(z_ref, g, value, masks),
     )
 
     def emit(g, value):
         base_ref[field_rows(g), :] = base_of(g) + value
 
     star_sum(y_ref, star_ref, emit)
-    subtract_lift(lift_ref[...], z_ref, base_ref, base_ref)
-
-
-def subtract_lift(lift, z_ref, base_ref, out_ref):
-    for f in range(0, FIELDS, 2):
-        fields = range(f, min(f + 2, FIELDS))
-        lanes = slice(f * LANES, (fields[-1] + 1) * LANES)
-        lifted = big_dot(lift, z_ref[:, lanes])
-        for n, g in enumerate(fields):
-            out_ref[field_rows(g), :] = base_ref[field_rows(g), :] - lifted[:, field_lanes(n)]
+    subtract_lift(lift_ref, 4 * FACES, z_ref, base_ref, base_ref)
 
 
 def middle_remote_kernel(
@@ -314,9 +358,9 @@
     flux_sum(
         lambda i, f: far_ref[f * NPAD : (f + 1) * NPAD, i * LANES : (i + 1) * LANES],
         minus_ref,
-        lambda g, value: stack_turned(z_ref, 0, g, value, masks),
-    )
-    subtract_lift(lift_ref[:, 3 * FACES :], z_ref, base_ref, middle_ref)
+        lambda g, value: stack_turned(z_ref, g, value, masks),
+    )
+    subtract_lift(lift_ref, 3 * FACES, z_ref, base_ref, middle_ref)
     small = cluster_ref[...] == 0
     for f in range(FIELDS):
         middle_ref[field_rows(f), :] = jnp.where(
@@ -359,7 +403,7 @@
 
 def last_remote_kernel(
     r0, r1, r2, r3, base_ref, minus_ref, lift_ref, pair_ref, marks_ref, part_ref, slot_ref, turn_ref,
-    out_hbm, z_ref, far_ref, done_ref, sems,
+    out_ref, z_ref, far_ref,
 ):
     pick = remote_pick(part_ref[...], slot_ref[...], r0.shape[0])
     far_ref[...] = received_faces((r0, r1, r2, r3), pair_ref[...], marks_ref, pick)
@@ -367,62 +411,28 @@
     flux_sum(
         lambda i, f: far_ref[f * NPAD : (f + 1) * NPAD, i * LANES : (i + 1) * LANES],
         minus_ref,
-        lambda g, value: stack_turned(z_ref, 0, g, value, masks),
-    )
-    subtract_lift(lift_ref[:, 3 * FACES :], z_ref, base_ref, done_ref)
-    copies = []
-    for f in range(FIELDS):
-        copy = pltpu.make_async_copy(done_ref.at[field_rows(f), :], out_hbm.at[:, f, :], sems.at[f])
-        copy.start()
-        copies.append(copy)
-    for copy in copies:
-        copy.wait()
-
-
-def padded_to(x, shape):
-    return jnp.pad(x, [(0, want - have) for have, want in zip(x.shape, shape)])
-
-
-def triple(x):
-    high, low = outer_parts(x)
-    return jnp.concatenate([high, high, low], axis=-1).astype(BF)
-
-
-def constants(stiffness, face_lift, face_project):
-    forward = padded_to(stiffness, (3, MODES, MPAD)).reshape(3 * MODES, MPAD)
-    backward = padded_to(jnp.transpose(stiffness, (0, 2, 1)), (3, MODES, MPAD))
-    project = padded_to(face_project, (4, NPAD, MPAD)).reshape(FACES, MPAD)
-    update = jnp.concatenate([backward.reshape(3 * MODES, MPAD), project], axis=0)
-    zero = jnp.zeros_like(project)
-    pair = jnp.concatenate(
-        [jnp.concatenate([project, zero], axis=1), jnp.concatenate([zero, project], axis=1)], axis=0
-    )
-    lifts = []
-    tables = rotations()
-    for h in (0, 0, 1, 2):
-        turned = face_lift[:, :, np.argsort(tables[h])]
-        turned = padded_to(turned, (4, MODES, NPAD))
-        lifts.append(triple(jnp.transpose(turned, (1, 0, 2)).reshape(MODES, FACES)))
-    return triple(forward), triple(update), jnp.concatenate(lifts, axis=1), triple(pair)
+        lambda g, value: stack_turned(z_ref, g, value, masks),
+    )
+    subtract_lift(lift_ref, 3 * FACES, z_ref, base_ref, out_ref)
 
 
 VM = pl.BlockSpec(memory_space=pltpu.VMEM)
-HB = pl.BlockSpec(memory_space=pl.ANY)
 STATE = (FIELDS * MODES, LANES)
 GATHERED = (FIELDS * NPAD, 4 * LANES)
 
 
-def call(kernel, in_specs, outs, out_specs, scratch, name):
+def call(kernel, inputs, outs, scratch, name):
+    out_shape = [jax.ShapeDtypeStruct(shape, kind) for shape, kind in outs]
     return pl.pallas_call(
         kernel,
-        out_shape=[jax.ShapeDtypeStruct(shape, F32) for shape in outs],
-        in_specs=in_specs,
-        out_specs=out_specs,
+        out_shape=out_shape,
+        in_specs=[VM] * len(inputs),
+        out_specs=[VM] * len(out_shape),
         scratch_shapes=scratch,
         compiler_params=pltpu.CompilerParams(vmem_limit_bytes=24 << 20),
         cost_estimate=pl.CostEstimate(flops=10**9, bytes_accessed=10**6, transcendentals=0),
         name=name,
-    )
+    )(*inputs)
 
 
 def scratch_xs():
@@ -434,21 +444,24 @@
 
 
 def scratch_z(rows):
-    return pltpu.VMEM((rows, FIELDS * LANES), BF)
-
-
-def shift(x, axis, step):
+    return pltpu.VMEM((2, rows, FIELDS * LANES), BF)
+
+
+def swap(x, axis, kind):
     count = lax.axis_size(axis)
-    return lax.ppermute(x, axis, [(i, (i + step) % count) for i in range(count)])
+    pairs = []
+    for a in range(kind, count, 2):
+        b = (a + 1) % count
+        pairs += [(a, b), (b, a)]
+    return lax.ppermute(x, axis, pairs)
 
 
 def trade(sends):
-    return (
-        shift(sends[0], "near", 1),
-        shift(sends[1], "near", -1),
-        shift(sends[2], "dom", 1),
-        shift(sends[3], "dom", -1),
-    )
+    dom_odd = swap(sends[3], "dom", 1)
+    dom_even = swap(sends[2], "dom", 0)
+    near_odd = swap(sends[1], "near", 1)
+    near_even = swap(sends[0], "near", 0)
+    return near_even, near_odd, dom_even, dom_odd
 
 
 def on_device(
@@ -456,49 +469,65 @@
     cluster, part, slot, face, turn, halo,
 ):
     width = halo.shape[1]
+    u = jnp.transpose(u, (1, 0, 2)).reshape(STATE)
+    star, plus, minus = [jnp.transpose(x, (1, 2, 0, 3)) for x in (star, plus, minus)]
+    face_lift = jnp.transpose(face_lift, (2, 0, 1))
+    face_project = jnp.transpose(face_project, (1, 0, 2))
     cluster = cluster.reshape(1, LANES)
-    forward, update, lift, pair = constants(stiffness, face_lift, face_project)
-    rim = (width, 5 * LANES)
-    ufm, first, second, *sends = call(
-        first_kernel, [HB, VM, VM, VM], [STATE] * 3 + [rim] * 4, [VM] * 7,
-        [scratch_xs(), scratch_y(3 * MODES), pltpu.SemaphoreType.DMA((FIELDS,))], "first",
-    )(u, star, forward, halo)
+    state, gathered = (STATE, F32), (GATHERED, F32)
+    rims = [((width, 5 * LANES), F32)] * 4
+    update_rows = 3 * MODES + FACES
+    first, second, forward, *sends = call(
+        first_kernel, (u, star, stiffness, halo),
+        [state, state, ((3 * MODES, 3 * MPAD), BF)] + rims,
+        [scratch_xs(), scratch_y(3 * MODES)], "first",
+    )
     received = trade(sends)
-    rows = 3 * MODES + FACES
-    base, g, marks = call(
-        middle_local_kernel, [VM] * 11, [STATE, GATHERED, (8, 4 * width)], [VM] * 3,
-        [scratch_xs(), scratch_y(rows), pltpu.VMEM(GATHERED, F32), scratch_z(12 * FACES)],
+    base, g, marks, update, lift, pair = call(
+        middle_local_kernel,
+        (u, first, star, plus, minus, stiffness, face_lift, face_project, part, slot, face, turn),
+        [
+            state, gathered, ((8, 4 * width), F32), ((update_rows, 3 * MPAD), BF),
+            ((2 * MODES, 4 * FACES), BF), ((2 * FACES, 3 * LANES), BF),
+        ],
+        [
+            scratch_xs(), scratch_y(update_rows), pltpu.VMEM(GATHERED, F32), scratch_z(4 * FACES),
+            pltpu.VMEM((4 * FACES, LANES), F32),
+        ],
         "middle_local",
-    )(ufm, first, star, plus, minus, update, lift, part, slot, face, turn)
+    )
     middle, later, gsum, *sends = call(
-        middle_remote_kernel, [VM] * 19, [STATE, STATE, GATHERED] + [rim] * 4, [VM] * 7,
-        [scratch_xs(), scratch_y(3 * MODES), scratch_z(9 * FACES), pltpu.VMEM(GATHERED, F32)],
+        middle_remote_kernel,
+        (
+            *received, u, base, g, second, star, minus, forward, lift, pair, marks,
+            part, slot, turn, cluster, halo,
+        ),
+        [state, state, gathered] + rims,
+        [scratch_xs(), scratch_y(3 * MODES), scratch_z(3 * FACES), pltpu.VMEM(GATHERED, F32)],
         "middle_remote",
-    )(
-        *received, ufm, base, g, second, star, minus, forward, lift, pair, marks,
-        part, slot, turn, cluster, halo,
     )
     received = trade(sends)
     (base,) = call(
-        last_local_kernel, [VM] * 16, [STATE], [VM],
+        last_local_kernel,
+        (
+            u, middle, first, second, later, gsum, star, plus, minus, update, lift,
+            part, slot, face, turn, cluster,
+        ),
+        [state],
         [
-            scratch_xs(), scratch_y(rows), pltpu.VMEM(GATHERED, F32), scratch_z(12 * FACES),
+            scratch_xs(), scratch_y(update_rows), pltpu.VMEM(GATHERED, F32), scratch_z(4 * FACES),
             pltpu.VMEM(GATHERED, F32),
         ],
         "last_local",
-    )(
-        ufm, middle, first, second, later, gsum, star, plus, minus, update, lift,
-        part, slot, face, turn, cluster,
     )
     (out,) = call(
-        last_remote_kernel, [VM] * 12, [u.shape], [HB],
-        [
-            scratch_z(9 * FACES), pltpu.VMEM(GATHERED, F32), pltpu.VMEM(STATE, F32),
-            pltpu.SemaphoreType.DMA((FIELDS,)),
-        ],
+        last_remote_kernel,
+        (*received, base, minus, lift, pair, marks, part, slot, turn),
+        [state],
+        [scratch_z(3 * FACES), pltpu.VMEM(GATHERED, F32)],
         "last_remote",
-    )(*received, base, minus, lift, pair, marks, part, slot, turn)
-    return out
+    )
+    return jnp.transpose(out.reshape(FIELDS, MODES, LANES), (1, 0, 2))
 
 
 def solution(mesh):

time: 45 us -> 36.2 us (0.80)
  local copies, waits for them, and re-layouts: 11.6 us -> 4.74 us
  starting transfers between devices: 14.3 us -> 12.2 us
  waiting for transfers between devices: 0.02 us -> 0.74 us
    unnamed x36 -> x26, local copies, waits for them, and re-layouts: 7.68 us -> 4.74 us
    ppermute x8, starting transfers between devices: 14.3 us -> 12.2 us  [swap(): return lax.ppermute(x, axis, pairs)]
    gather x3 -> x0, local copies, waits for them, and re-layouts: 1.79 us -> none  [constants(): turned = face_lift[:, :, np.argsort(tables[h])]]
    pad x3 -> x0, local copies, waits for them, and re-layouts: 0.96 us -> none  [padded_to(): return jnp.pad(x, [(0, want - have) for have, want in zip(x.shape, shape)])]
    pallas_call x1 -> x0, local copies, waits for them, and re-layouts: 0.78 us -> none  [on_device(): call(last_remote_kernel, [VM] * 12, [u.shape], [HB], [scratch_z(9 * FACES...]
    ppermute x8, waiting for transfers between devices: 0.02 us -> 0.74 us  [swap(): return lax.ppermute(x, axis, pairs)]
  transfers between devices with their start and end apart: 8 -> 8, of which waited for: 0 -> 1; matrix products, arithmetic and copies ran while one was open for 6% -> 0% of each run, Pallas kernels for 11% -> 14%
where the time goes in v1:
time: 36.2 us; the launch traced here: 35.9 us
  Pallas kernels  18 us (50%)
  starting transfers between devices  12.2 us (34%)
  local copies, waits for them, and re-layouts  4.74 us (13%)
  waiting for transfers between devices  0.74 us (2%)
    pallas_call x5, Pallas kernels, call(): pl.pallas_call(kernel, out_shape=out_shape, in_specs=[VM] * len(inputs),...  18 us
    ppermute x8, starting transfers between devices, swap(): return lax.ppermute(x, axis, pairs)  12.2 us
    unnamed x26, local copies, waits for them, and re-layouts  4.74 us
    ppermute x8, waiting for transfers between devices, swap(): return lax.ppermute(x, axis, pairs)  0.74 us
  transfers between devices with their start and end apart: 8, of which 1 were waited for; matrix products, arithmetic and copies ran while one was open for 0% of the time, Pallas kernels for 14%

profile of v1, /device:TPU:0, one launch (start us, length us, event | category | flops | bytes accessed | tf_op | source)
XLA Modules:
  0.0 35.9 jit_solution(12382569664934250090)
XLA Ops:
  0.0 0.7 %copy-done.7 = s32[4,16]{1,0:T(4,128)S(1)} copy-done((s32[4,16]{1,0:T(4,128)S(1)}, s32[4,16]{1,0:T(4,128)}, u32[]{:S(2)}) %copy-start.7) | copy-done | bytes 280
  0.7 0.9 %copy-done = f32[56,9,128]{2,0,1:T(8,128)S(1)} copy-done((f32[56,9,128]{2,0,1:T(8,128)S(1)}, f32[56,9,128]{2,0,1:T(8,128)}, u32[]{:S(2)}) %copy-start) | copy-done | bytes 258072
  1.6 0.9 %copy-done.1 = f32[3,9,9,128]{3,0,2,1:T(4,128)S(1)} copy-done((f32[3,9,9,128]{3,0,2,1:T(4,128)S(1)}, f32[3,9,9,128]{3,0,2,1:T(4,128)}, u32[]{:S(2)}) %copy-start.1) | copy-done | bytes 124440
  2.6 0.9 %copy-done.4 = f32[3,56,56]{2,1,0:T(8,128)S(1)} copy-done((f32[3,56,56]{2,1,0:T(8,128)S(1)}, f32[3,56,56]{2,1,0:T(8,128)}, u32[]{:S(2)}) %copy-start.4) | copy-done | bytes 37656
  3.5 4.8 %first.1 = (f32[504,128]{1,0:T(8,128)S(1)}, f32[504,128]{1,0:T(8,128)S(1)}, bf16[168,192]{1,0:T(8,128)(2,1)S(1)}, f32[16,640]{1,0:T(8,128)S(1)}, f32[16,640]{1,0...) custom-call(f32[504,128]{1,0:T(8,128)S(1)} %bitcast.12, f32[9,9,3,128]{3,2,1,0:T(4,128)S(1)} %bitcast.16, ...), custom_call_target="tpu_custom_call" | custom-call | flops 1000000000 | bytes 1000000 | tf_op jit(solution)/shard_map/first/pallas_call | solution.py:426
  8.3 0.5 %collective-permute-start = (f32[16,640]{1,0:T(8,128)S(1)}, f32[16,640]{1,0:T(8,128)S(1)}, u32[]{:S(2)}, u32[]{:S(2)}) collective-permute-start(f32[16,640]{1,0:T(8,128)S(1)} %get-tuple-element.25), channel_id=1, source_target_pairs={{0,1},{1,0},{2,3},{3,2},{4,5},{5,4},{6,7},{7,6},{8,9},{9,8},{10,11... | collective-permute-start | bytes 122888 | tf_op jit(solution)/shard_map/ppermute | solution.py:456
  8.8 2.6 %collective-permute-start.1 = (f32[16,640]{1,0:T(8,128)S(1)}, f32[16,640]{1,0:T(8,128)S(1)}, u32[]{:S(2)}, u32[]{:S(2)}) collective-permute-start(f32[16,640]{1,0:T(8,128)S(1)} %get-tuple-element.26), channel_id=1, source_target_pairs={{1,2},{2,1},{3,0},{0,3},{5,6},{6,5},{7,4},{4,7},{9,10},{10,9},{11,... | collective-permute-start | bytes 122888 | tf_op jit(solution)/shard_map/ppermute | solution.py:456
  11.4 1.5 %collective-permute-start.2 = (f32[16,640]{1,0:T(8,128)S(1)}, f32[16,640]{1,0:T(8,128)S(1)}, u32[]{:S(2)}, u32[]{:S(2)}) collective-permute-start(f32[16,640]{1,0:T(8,128)S(1)} %get-tuple-element.27), channel_id=1, source_target_pairs={{0,4},{4,0},{8,12},{12,8},{16,20},{20,16},{24,28},{28,24},{1,5},{5... | collective-permute-start | bytes 122888 | tf_op jit(solution)/shard_map/ppermute | solution.py:456
  12.9 3.5 %collective-permute-start.3 = (f32[16,640]{1,0:T(8,128)S(1)}, f32[16,640]{1,0:T(8,128)S(1)}, u32[]{:S(2)}, u32[]{:S(2)}) collective-permute-start(f32[16,640]{1,0:T(8,128)S(1)} %get-tuple-element.28), channel_id=1, source_target_pairs={{4,8},{8,4},{12,16},{16,12},{20,24},{24,20},{28,0},{0,28},{5,9},{9... | collective-permute-start | bytes 122888 | tf_op jit(solution)/shard_map/ppermute | solution.py:456
  16.5 0.6 %copy-done.8 = s32[4,128]{1,0:T(4,128)S(1)} copy-done((s32[4,128]{1,0:T(4,128)S(1)}, s32[4,128]{1,0:T(4,128)}, u32[]{:S(2)}) %copy-start.8) | copy-done | bytes 2072
  17.2 2.6 %middle_local.1 = (f32[504,128]{1,0:T(8,128)S(1)}, f32[216,512]{1,0:T(8,128)S(1)}, f32[8,64]{1,0:T(8,128)S(1)}, bf16[264,192]{1,0:T(8,128)(2,1)S(1)}, bf16[112,3...) custom-call(f32[504,128]{1,0:T(8,128)S(1)} %bitcast.13, f32[504,128]{1,0:T(8,128)S(1)} %get-tuple-element.29.first_ref, ...), custom_call_target="tpu_custom_call" | custom-call | flops 1000000000 | bytes 1000000 | tf_op jit(solution)/shard_map/middle_local/pallas_call | solution.py:426
  19.7 0.0 collective-permute-done.1.r1
  19.7 0.0 collective-permute-done.2.r2
  19.8 0.0 copy-start.12
  19.8 0.6 %copy-done.12 = s32[128]{0:T(128)S(1)} copy-done((s32[128]{0:T(128)S(1)}, s32[128]{0:T(128)}, u32[]{:S(2)}) %copy-start.12) | copy-done | bytes 536
  20.4 6.0 %middle_remote.1 = (f32[504,128]{1,0:T(8,128)S(1)}, f32[504,128]{1,0:T(8,128)S(1)}, f32[216,512]{1,0:T(8,128)S(1)}, f32[16,640]{1,0:T(8,128)S(1)}, f32[16,640]{1...) custom-call(f32[16,640]{1,0:T(8,128)S(1)} %collective-permute-done.r0, ...), custom_call_target="tpu_custom_call" | custom-call | flops 1000000000 | bytes 1000000 | tf_op jit(solution)/shard_map/middle_remote/pallas_call | solution.py:426
  26.4 0.0 collective-permute-start.4
  26.5 0.6 %collective-permute-start.5 = (f32[16,640]{1,0:T(8,128)S(1)}, f32[16,640]{1,0:T(8,128)S(1)}, u32[]{:S(2)}, u32[]{:S(2)}) collective-permute-start(f32[16,640]{1,0:T(8,128)S(1)} %get-tuple-element.38), channel_id=1, source_target_pairs={{1,2},{2,1},{3,0},{0,3},{5,6},{6,5},{7,4},{4,7},{9,10},{10,9},{11,... | collective-permute-start | bytes 122888 | tf_op jit(solution)/shard_map/ppermute | solution.py:456
  27.1 0.0 collective-permute-start.6
  27.1 3.4 %collective-permute-start.7 = (f32[16,640]{1,0:T(8,128)S(1)}, f32[16,640]{1,0:T(8,128)S(1)}, u32[]{:S(2)}, u32[]{:S(2)}) collective-permute-start(f32[16,640]{1,0:T(8,128)S(1)} %get-tuple-element.40), channel_id=1, source_target_pairs={{4,8},{8,4},{12,16},{16,12},{20,24},{24,20},{28,0},{0,28},{5,9},{9... | collective-permute-start | bytes 122888 | tf_op jit(solution)/shard_map/ppermute | solution.py:456
  30.5 2.5 %last_local.1.base_ref = f32[504,128]{1,0:T(8,128)S(1)} custom-call(f32[504,128]{1,0:T(8,128)S(1)} %bitcast.15, f32[504,128]{1,0:T(8,128)S(1)} %get-tuple-element.41.middle_ref, f32[504,128]{1,0:T(8,128)S(1)} %get-tuple-element.29.first_ref, f32[504,128]{1,0:T(8,128)S(1)} %get-tuple-element.32.second_ref, f32[504,128]{1,0:T(8,128)S(1)} %get-tuple-element.42.later_ref, ...), custom_call_target="tpu_custom_call" | custom-call | flops 1000000000 | bytes 1000000 | tf_op jit(solution)/shard_map/last_local/pallas_call | solution.py:426
  33.0 0.0 collective-permute-done.4.r0
  33.1 0.7 %collective-permute-done.7.r3 = f32[16,640]{1,0:T(8,128)S(1)} collective-permute-done((f32[16,640]{1,0:T(8,128)S(1)}, f32[16,640]{1,0:T(8,128)S(1)}, u32[]{:S(2)}, u32[]{:S(2)}) %collective-permute-start.7) | collective-permute-done | bytes 40992 | tf_op jit(solution)/shard_map/ppermute | solution.py:456
  33.8 2.1 %last_remote.1 = f32[504,128]{1,0:T(8,128)} custom-call(f32[16,640]{1,0:T(8,128)S(1)} %collective-permute-done.4.r0, f32[16,640]{1,0:T(8,128)S(1)} %collective-permute-done.5.r1, f32[16,640]{1,0:T(8,128)S(1)} %collective-permute-done.6.r2, f32[16,640]{1,0:T(8,128)S(1)} %collective-permute-done.7.r3, f32[504,128]{1,0:T(8,128)S(1)} %last_local.1.base_ref, ...), custom_call_target="tpu_custom_call" | custom-call | flops 1000000000 | bytes 1000000 | tf_op jit(solution)/shard_map/last_remote/pallas_call | solution.py:426
  (23 shorter events, 0.0 us)
Async XLA Ops:
  0.0 0.7 %copy-start.7 = (s32[4,16]{1,0:T(4,128)S(1)}, s32[4,16]{1,0:T(4,128)}, u32[]{:S(2)}) copy-start(s32[4,16]{1,0:T(4,128)} %halo_ref.3) | copy-start | bytes 772
  0.7 0.9 %copy-start = (f32[56,9,128]{2,0,1:T(8,128)S(1)}, f32[56,9,128]{2,0,1:T(8,128)}, u32[]{:S(2)}) copy-start(f32[56,9,128]{2,0,1:T(8,128)} %param.13) | copy-start | bytes 774148
  1.6 0.9 %copy-start.1 = (f32[3,9,9,128]{3,0,2,1:T(4,128)S(1)}, f32[3,9,9,128]{3,0,2,1:T(4,128)}, u32[]{:S(2)}) copy-start(f32[3,9,9,128]{3,0,2,1:T(4,128)} %param.14) | copy-start | bytes 373252
  2.5 0.9 %copy-start.4 = (f32[3,56,56]{2,1,0:T(8,128)S(1)}, f32[3,56,56]{2,1,0:T(8,128)}, u32[]{:S(2)}) copy-start(f32[3,56,56]{2,1,0:T(8,128)} %stiff_ref.3) | copy-start | bytes 112900
  3.4 13.0 %copy-start.2 = (f32[4,9,9,128]{3,0,2,1:T(4,128)S(1)}, f32[4,9,9,128]{3,0,2,1:T(4,128)}, u32[]{:S(2)}) copy-start(f32[4,9,9,128]{3,0,2,1:T(4,128)} %param.15) | copy-start | bytes 497668
  3.4 13.0 %copy-start.3 = (f32[4,9,9,128]{3,0,2,1:T(4,128)S(1)}, f32[4,9,9,128]{3,0,2,1:T(4,128)}, u32[]{:S(2)}) copy-start(f32[4,9,9,128]{3,0,2,1:T(4,128)} %param.16) | copy-start | bytes 497668
  3.4 13.0 %copy-start.5 = (f32[4,56,21]{1,0,2:T(4,128)S(1)}, f32[4,56,21]{1,0,2:T(4,128)}, u32[]{:S(2)}) copy-start(f32[4,56,21]{1,0,2:T(4,128)} %param.18) | copy-start | bytes 56452
  3.4 13.0 %copy-start.6 = (f32[4,21,56]{2,0,1:T(4,128)S(1)}, f32[4,21,56]{2,0,1:T(4,128)}, u32[]{:S(2)}) copy-start(f32[4,21,56]{2,0,1:T(4,128)} %param.19) | copy-start | bytes 56452
  3.4 13.0 %copy-start.9 = (s32[4,128]{1,0:T(4,128)S(1)}, s32[4,128]{1,0:T(4,128)}, u32[]{:S(2)}) copy-start(s32[4,128]{1,0:T(4,128)} %part_ref.7) | copy-start | bytes 6148
  3.5 13.0 %copy-start.10 = (s32[4,128]{1,0:T(4,128)S(1)}, s32[4,128]{1,0:T(4,128)}, u32[]{:S(2)}) copy-start(s32[4,128]{1,0:T(4,128)} %slot_ref.7) | copy-start | bytes 6148
  3.5 13.0 %copy-start.11 = (s32[4,128]{1,0:T(4,128)S(1)}, s32[4,128]{1,0:T(4,128)}, u32[]{:S(2)}) copy-start(s32[4,128]{1,0:T(4,128)} %turn_ref.7) | copy-start | bytes 6148
  8.3 11.4 %collective-permute-start = (f32[16,640]{1,0:T(8,128)S(1)}, f32[16,640]{1,0:T(8,128)S(1)}, u32[]{:S(2)}, u32[]{:S(2)}) collective-permute-start(f32[16,640]{1,0:T(8,128)S(1)} %get-tuple-element.25), channel_id=1, source_target_pairs={{0,1},{1,0},{2,3},{3,2},{4,5},{5,4},{6,7},{7,6},{8,9},{9,8},{10,11... | collective-permute-start | bytes 122888 | tf_op jit(solution)/shard_map/ppermute | solution.py:456
  8.8 10.9 %collective-permute-start.1 = (f32[16,640]{1,0:T(8,128)S(1)}, f32[16,640]{1,0:T(8,128)S(1)}, u32[]{:S(2)}, u32[]{:S(2)}) collective-permute-start(f32[16,640]{1,0:T(8,128)S(1)} %get-tuple-element.26), channel_id=1, source_target_pairs={{1,2},{2,1},{3,0},{0,3},{5,6},{6,5},{7,4},{4,7},{9,10},{10,9},{11,... | collective-permute-start | bytes 122888 | tf_op jit(solution)/shard_map/ppermute | solution.py:456
  11.4 8.3 %collective-permute-start.2 = (f32[16,640]{1,0:T(8,128)S(1)}, f32[16,640]{1,0:T(8,128)S(1)}, u32[]{:S(2)}, u32[]{:S(2)}) collective-permute-start(f32[16,640]{1,0:T(8,128)S(1)} %get-tuple-element.27), channel_id=1, source_target_pairs={{0,4},{4,0},{8,12},{12,8},{16,20},{20,16},{24,28},{28,24},{1,5},{5... | collective-permute-start | bytes 122888 | tf_op jit(solution)/shard_map/ppermute | solution.py:456
  12.9 6.8 %collective-permute-start.3 = (f32[16,640]{1,0:T(8,128)S(1)}, f32[16,640]{1,0:T(8,128)S(1)}, u32[]{:S(2)}, u32[]{:S(2)}) collective-permute-start(f32[16,640]{1,0:T(8,128)S(1)} %get-tuple-element.28), channel_id=1, source_target_pairs={{4,8},{8,4},{12,16},{16,12},{20,24},{24,20},{28,0},{0,28},{5,9},{9... | collective-permute-start | bytes 122888 | tf_op jit(solution)/shard_map/ppermute | solution.py:456
  16.5 0.7 %copy-start.8 = (s32[4,128]{1,0:T(4,128)S(1)}, s32[4,128]{1,0:T(4,128)}, u32[]{:S(2)}) copy-start(s32[4,128]{1,0:T(4,128)} %face_ref.3) | copy-start | bytes 6148
  19.8 0.7 %copy-start.12 = (s32[128]{0:T(128)S(1)}, s32[128]{0:T(128)}, u32[]{:S(2)}) copy-start(s32[128]{0:T(128)} %param.20) | copy-start | bytes 1540
  26.4 6.6 %collective-permute-start.4 = (f32[16,640]{1,0:T(8,128)S(1)}, f32[16,640]{1,0:T(8,128)S(1)}, u32[]{:S(2)}, u32[]{:S(2)}) collective-permute-start(f32[16,640]{1,0:T(8,128)S(1)} %get-tuple-element.37), channel_id=1, source_target_pairs={{0,1},{1,0},{2,3},{3,2},{4,5},{5,4},{6,7},{7,6},{8,9},{9,8},{10,11... | collective-permute-start | bytes 122888 | tf_op jit(solution)/shard_map/ppermute | solution.py:456
  26.5 6.6 %collective-permute-start.5 = (f32[16,640]{1,0:T(8,128)S(1)}, f32[16,640]{1,0:T(8,128)S(1)}, u32[]{:S(2)}, u32[]{:S(2)}) collective-permute-start(f32[16,640]{1,0:T(8,128)S(1)} %get-tuple-element.38), channel_id=1, source_target_pairs={{1,2},{2,1},{3,0},{0,3},{5,6},{6,5},{7,4},{4,7},{9,10},{10,9},{11,... | collective-permute-start | bytes 122888 | tf_op jit(solution)/shard_map/ppermute | solution.py:456
  27.1 6.0 %collective-permute-start.6 = (f32[16,640]{1,0:T(8,128)S(1)}, f32[16,640]{1,0:T(8,128)S(1)}, u32[]{:S(2)}, u32[]{:S(2)}) collective-permute-start(f32[16,640]{1,0:T(8,128)S(1)} %get-tuple-element.39), channel_id=1, source_target_pairs={{0,4},{4,0},{8,12},{12,8},{16,20},{20,16},{24,28},{28,24},{1,5},{5... | collective-permute-start | bytes 122888 | tf_op jit(solution)/shard_map/ppermute | solution.py:456
  27.1 6.7 %collective-permute-start.7 = (f32[16,640]{1,0:T(8,128)S(1)}, f32[16,640]{1,0:T(8,128)S(1)}, u32[]{:S(2)}, u32[]{:S(2)}) collective-permute-start(f32[16,640]{1,0:T(8,128)S(1)} %get-tuple-element.40), channel_id=1, source_target_pairs={{4,8},{8,4},{12,16},{16,12},{20,24},{24,20},{28,0},{0,28},{5,9},{9... | collective-permute-start | bytes 122888 | tf_op jit(solution)/shard_map/ppermute | solution.py:456

commit v2 on v1

--- a/solution.py
+++ b/solution.py
@@ -118,10 +118,11 @@
 def send_rims(xs_ref, halo_ref, sends):
     width = halo_ref.shape[1]
     element = lax.broadcasted_iota(jnp.int32, (LANES, width), 0)
+    near_even, dom_even = evens()
     picks = []
-    for axis, even in enumerate(evens()):
-        up, down = halo_ref[2 * axis : 2 * axis + 1, :], halo_ref[2 * axis + 1 : 2 * axis + 2, :]
-        for row in (jnp.where(even, up, down), jnp.where(even, down, up)):
+    for even, first in ((dom_even, 2), (near_even, 0)):
+        up, down = halo_ref[first : first + 1, :], halo_ref[first + 1 : first + 2, :]
+        for row in (jnp.where(even, down, up), jnp.where(even, up, down)):
             pick = jnp.where(element == row, 1.0, 0.0).astype(F32)
             picks.append(jnp.transpose(pick))
     pick = jnp.concatenate(picks, axis=0).astype(BF)
@@ -148,8 +149,8 @@
 
 def remote_pick(part, slot, width):
     near_even, dom_even = evens()
-    near_block = jnp.where(near_even, 2 - part, part - 1)
-    dom_block = jnp.where(dom_even, 6 - part, part - 1)
+    near_block = jnp.where(near_even, part + 1, 4 - part)
+    dom_block = jnp.where(dom_even, part - 3, 4 - part)
     block = jnp.where(part > 2, dom_block, near_block)
     target = jnp.where(part > 0, block * width + slot, -1)
     target = jnp.concatenate([target[i : i + 1, :] for i in range(4)], axis=1)
@@ -283,15 +284,29 @@
     lifts_ref[...] = jnp.concatenate([high, low], axis=0).astype(BF)
 
 
-def first_kernel(
-    u_ref, star_ref, stiff_ref, halo_ref,
-    first_ref, second_ref, forward_ref, s0, s1, s2, s3, xs_ref, y_ref,
-):
+INPUTS = 13
+
+
+def first_kernel(*refs):
+    sources, rest = refs[:INPUTS], refs[INPUTS:]
+    held, rest = rest[:INPUTS], rest[INPUTS:]
+    first_ref, second_ref, forward_ref, s0, s1, s2, s3, xs_ref, y_ref, sems = rest
+    copies = [
+        pltpu.make_async_copy(source, target, sems.at[n])
+        for n, (source, target) in enumerate(zip(sources, held))
+    ]
+    for copy in copies:
+        copy.start()
+    u_ref, star_ref, stiff_ref, halo_ref = held[:4]
+    for copy in copies[:3]:
+        copy.wait()
     forward_ref[...] = forward_matrix(stiff_ref)
     taylor(
         lambda f: u_ref[field_rows(f), :], star_ref, forward_ref[...], xs_ref, y_ref,
         [(first_ref, integral_weights(0.0, 0.5)), (second_ref, integral_weights(0.5, 1.0))],
     )
+    for copy in copies[3:]:
+        copy.wait()
     for f in range(FIELDS):
         put_operand(xs_ref, f, first_ref[field_rows(f), :])
     send_rims(xs_ref, halo_ref, (s0, s1, s2, s3))
@@ -421,12 +436,12 @@
 GATHERED = (FIELDS * NPAD, 4 * LANES)
 
 
-def call(kernel, inputs, outs, scratch, name):
+def call(kernel, inputs, outs, scratch, name, space=pltpu.VMEM):
     out_shape = [jax.ShapeDtypeStruct(shape, kind) for shape, kind in outs]
     return pl.pallas_call(
         kernel,
         out_shape=out_shape,
-        in_specs=[VM] * len(inputs),
+        in_specs=[pl.BlockSpec(memory_space=space)] * len(inputs),
         out_specs=[VM] * len(out_shape),
         scratch_shapes=scratch,
         compiler_params=pltpu.CompilerParams(vmem_limit_bytes=24 << 20),
@@ -457,11 +472,10 @@
 
 
 def trade(sends):
-    dom_odd = swap(sends[3], "dom", 1)
-    dom_even = swap(sends[2], "dom", 0)
-    near_odd = swap(sends[1], "near", 1)
-    near_even = swap(sends[0], "near", 0)
-    return near_even, near_odd, dom_even, dom_odd
+    return [
+        swap(send, axis, kind)
+        for send, (axis, kind) in zip(sends, (("dom", 1), ("dom", 0), ("near", 1), ("near", 0)))
+    ]
 
 
 def on_device(
@@ -473,15 +487,24 @@
     star, plus, minus = [jnp.transpose(x, (1, 2, 0, 3)) for x in (star, plus, minus)]
     face_lift = jnp.transpose(face_lift, (2, 0, 1))
     face_project = jnp.transpose(face_project, (1, 0, 2))
-    cluster = cluster.reshape(1, LANES)
     state, gathered = (STATE, F32), (GATHERED, F32)
     rims = [((width, 5 * LANES), F32)] * 4
     update_rows = 3 * MODES + FACES
-    first, second, forward, *sends = call(
-        first_kernel, (u, star, stiffness, halo),
-        [state, state, ((3 * MODES, 3 * MPAD), BF)] + rims,
-        [scratch_xs(), scratch_y(3 * MODES)], "first",
-    )
+    inputs = (
+        u, star, stiffness, halo, plus, minus, face_lift, face_project,
+        part, slot, face, turn, cluster.reshape(1, LANES),
+    )
+    inputs = [pltpu.with_memory_space_constraint(x, pltpu.HBM) for x in inputs]
+    *held, first, second, forward, s0, s1, s2, s3 = call(
+        first_kernel, inputs,
+        [(x.shape, x.dtype) for x in inputs]
+        + [state, state, ((3 * MODES, 3 * MPAD), BF)] + rims,
+        [scratch_xs(), scratch_y(3 * MODES), pltpu.SemaphoreType.DMA((INPUTS,))], "first",
+        pltpu.HBM,
+    )
+    u, star, stiffness, halo, plus, minus, face_lift, face_project = held[:8]
+    part, slot, face, turn, cluster = held[8:]
+    sends = s0, s1, s2, s3
     received = trade(sends)
     base, g, marks, update, lift, pair = call(
         middle_local_kernel,

time: 36.2 us -> 31.7 us (0.88)
  local copies, waits for them, and re-layouts: 4.74 us -> 0 us
  Pallas kernels: 18 us -> 19.3 us
  waiting for transfers between devices: 0.74 us -> 0.31 us
  starting transfers between devices: 12.2 us -> 11.8 us
    unnamed x26 -> x0, local copies, waits for them, and re-layouts: 4.74 us -> none
    pallas_call x5, Pallas kernels: 18 us -> 19.3 us  [call(): pl.pallas_call(kernel, out_shape=out_shape, in_specs=[pl.BlockSpec(memory...]
    ppermute x8, waiting for transfers between devices: 0.74 us -> 0.31 us  [swap(): return lax.ppermute(x, axis, pairs)]
    ppermute x8, starting transfers between devices: 12.2 us -> 11.8 us  [swap(): return lax.ppermute(x, axis, pairs)]
  transfers between devices with their start and end apart: 8 -> 8, of which waited for: 1 -> 2; matrix products, arithmetic and copies ran while one was open for 0% -> 0% of each run, Pallas kernels for 14% -> 16%
where the time goes in v2:
time: 31.7 us; the launch traced here: 31.5 us
  Pallas kernels  19.3 us (61%)
  starting transfers between devices  11.8 us (37%)
    pallas_call x5, Pallas kernels, call(): pl.pallas_call(kernel, out_shape=out_shape, in_specs=[pl.BlockSpec(memory...  19.3 us
    ppermute x8, starting transfers between devices, swap(): return lax.ppermute(x, axis, pairs)  11.8 us
  transfers between devices with their start and end apart: 8, of which 2 were waited for; matrix products, arithmetic and copies ran while one was open for 0% of the time, Pallas kernels for 16%

profile of v2, /device:TPU:0, one launch (start us, length us, event | category | flops | bytes accessed | tf_op | source)
XLA Modules:
  0.0 31.5 jit_solution(13353065501884558774)
XLA Ops:
  0.0 6.0 %first.1 = (f32[504,128]{1,0:T(8,128)S(1)}, f32[9,9,3,128]{3,2,1,0:T(4,128)S(1)}, f32[3,56,56]{2,1,0:T(8,128)S(1)}, s32[4,16]{1,0:T(4,128)S(1)}, f32[9,9,4,128]{...) custom-call(f32[504,128]{1,0:T(8,128)} %bitcast.12, ...), custom_call_target="tpu_custom_call" | custom-call | flops 1000000000 | bytes 1000000 | tf_op jit(solution)/shard_map/first/pallas_call | solution.py:441
  6.1 6.1 %collective-permute-start = (f32[16,640]{1,0:T(8,128)S(1)}, f32[16,640]{1,0:T(8,128)S(1)}, u32[]{:S(2)}, u32[]{:S(2)}) collective-permute-start(f32[16,640]{1,0:T(8,128)S(1)} %get-tuple-element.38), channel_id=1, source_target_pairs={{4,8},{8,4},{12,16},{16,12},{20,24},{24,20},{28,0},{0,28},{5,9},{9... | collective-permute-start | bytes 122888 | tf_op jit(solution)/shard_map/ppermute | solution.py:471
  12.2 0.0 collective-permute-start.1
  12.2 0.7 %collective-permute-start.2 = (f32[16,640]{1,0:T(8,128)S(1)}, f32[16,640]{1,0:T(8,128)S(1)}, u32[]{:S(2)}, u32[]{:S(2)}) collective-permute-start(f32[16,640]{1,0:T(8,128)S(1)} %get-tuple-element.40), channel_id=1, source_target_pairs={{1,2},{2,1},{3,0},{0,3},{5,6},{6,5},{7,4},{4,7},{9,10},{10,9},{11,... | collective-permute-start | bytes 122888 | tf_op jit(solution)/shard_map/ppermute | solution.py:471
  12.8 1.0 %collective-permute-start.3 = (f32[16,640]{1,0:T(8,128)S(1)}, f32[16,640]{1,0:T(8,128)S(1)}, u32[]{:S(2)}, u32[]{:S(2)}) collective-permute-start(f32[16,640]{1,0:T(8,128)S(1)} %get-tuple-element.41), channel_id=1, source_target_pairs={{0,1},{1,0},{2,3},{3,2},{4,5},{5,4},{6,7},{7,6},{8,9},{9,8},{10,11... | collective-permute-start | bytes 122888 | tf_op jit(solution)/shard_map/ppermute | solution.py:471
  13.8 2.6 %middle_local.1 = (f32[504,128]{1,0:T(8,128)S(1)}, f32[216,512]{1,0:T(8,128)S(1)}, f32[8,64]{1,0:T(8,128)S(1)}, bf16[264,192]{1,0:T(8,128)(2,1)S(1)}, bf16[112,3...) custom-call(f32[504,128]{1,0:T(8,128)S(1)} %get-tuple-element.42.u_ref, f32[504,128]{1,0:T(8,128)S(1)} %get-tuple-element.43.first_ref, ...), custom_call_target="tpu_custom_call" | custom-call | flops 1000000000 | bytes 1000000 | tf_op jit(solution)/shard_map/middle_local/pallas_call | solution.py:441
  16.3 0.0 collective-permute-done.r0
  16.4 0.0 collective-permute-done.1.r1
  16.4 0.0 collective-permute-done.2.r2
  16.4 0.0 collective-permute-done.3.r3
  16.4 6.1 %middle_remote.1 = (f32[504,128]{1,0:T(8,128)S(1)}, f32[504,128]{1,0:T(8,128)S(1)}, f32[216,512]{1,0:T(8,128)S(1)}, f32[16,640]{1,0:T(8,128)S(1)}, f32[16,640]{1...) custom-call(f32[16,640]{1,0:T(8,128)S(1)} %collective-permute-done.r0, ...), custom_call_target="tpu_custom_call" | custom-call | flops 1000000000 | bytes 1000000 | tf_op jit(solution)/shard_map/middle_remote/pallas_call | solution.py:441
  22.4 2.5 %collective-permute-start.4 = (f32[16,640]{1,0:T(8,128)S(1)}, f32[16,640]{1,0:T(8,128)S(1)}, u32[]{:S(2)}, u32[]{:S(2)}) collective-permute-start(f32[16,640]{1,0:T(8,128)S(1)} %get-tuple-element.63), channel_id=1, source_target_pairs={{4,8},{8,4},{12,16},{16,12},{20,24},{24,20},{28,0},{0,28},{5,9},{9... | collective-permute-start | bytes 122888 | tf_op jit(solution)/shard_map/ppermute | solution.py:471
  25.0 0.0 collective-permute-start.5
  25.0 0.0 collective-permute-start.6
  25.0 1.6 %collective-permute-start.7 = (f32[16,640]{1,0:T(8,128)S(1)}, f32[16,640]{1,0:T(8,128)S(1)}, u32[]{:S(2)}, u32[]{:S(2)}) collective-permute-start(f32[16,640]{1,0:T(8,128)S(1)} %get-tuple-element.66), channel_id=1, source_target_pairs={{0,1},{1,0},{2,3},{3,2},{4,5},{5,4},{6,7},{7,6},{8,9},{9,8},{10,11... | collective-permute-start | bytes 122888 | tf_op jit(solution)/shard_map/ppermute | solution.py:471
  26.6 2.5 %last_local.1.base_ref = f32[504,128]{1,0:T(8,128)S(1)} custom-call(f32[504,128]{1,0:T(8,128)S(1)} %get-tuple-element.42.u_ref, f32[504,128]{1,0:T(8,128)S(1)} %get-tuple-element.67.middle_ref, f32[504,128]{1,0:T(8,128)S(1)} %get-tuple-element.43.first_ref, f32[504,128]{1,0:T(8,128)S(1)} %get-tuple-element.56.second_ref, ...), custom_call_target="tpu_custom_call" | custom-call | flops 1000000000 | bytes 1000000 | tf_op jit(solution)/shard_map/last_local/pallas_call | solution.py:441
  29.1 0.2 collective-permute-done.4.r0
  29.3 0.1 collective-permute-done.5.r1
  29.4 0.0 collective-permute-done.6.r2
  29.4 0.0 collective-permute-done.7.r3
  29.4 2.1 %last_remote.1 = f32[504,128]{1,0:T(8,128)} custom-call(f32[16,640]{1,0:T(8,128)S(1)} %collective-permute-done.4.r0, f32[16,640]{1,0:T(8,128)S(1)} %collective-permute-done.5.r1, f32[16,640]{1,0:T(8,128)S(1)} %collective-permute-done.6.r2, f32[16,640]{1,0:T(8,128)S(1)} %collective-permute-done.7.r3, f32[504,128]{1,0:T(8,128)S(1)} %last_local.1.base_ref, ...), custom_call_target="tpu_custom_call" | custom-call | flops 1000000000 | bytes 1000000 | tf_op jit(solution)/shard_map/last_remote/pallas_call | solution.py:441
Async XLA Ops:
  6.1 10.3 %collective-permute-start = (f32[16,640]{1,0:T(8,128)S(1)}, f32[16,640]{1,0:T(8,128)S(1)}, u32[]{:S(2)}, u32[]{:S(2)}) collective-permute-start(f32[16,640]{1,0:T(8,128)S(1)} %get-tuple-element.38), channel_id=1, source_target_pairs={{4,8},{8,4},{12,16},{16,12},{20,24},{24,20},{28,0},{0,28},{5,9},{9... | collective-permute-start | bytes 122888 | tf_op jit(solution)/shard_map/ppermute | solution.py:471
  12.2 4.2 %collective-permute-start.1 = (f32[16,640]{1,0:T(8,128)S(1)}, f32[16,640]{1,0:T(8,128)S(1)}, u32[]{:S(2)}, u32[]{:S(2)}) collective-permute-start(f32[16,640]{1,0:T(8,128)S(1)} %get-tuple-element.39), channel_id=1, source_target_pairs={{0,4},{4,0},{8,12},{12,8},{16,20},{20,16},{24,28},{28,24},{1,5},{5... | collective-permute-start | bytes 122888 | tf_op jit(solution)/shard_map/ppermute | solution.py:471
  12.2 4.2 %collective-permute-start.2 = (f32[16,640]{1,0:T(8,128)S(1)}, f32[16,640]{1,0:T(8,128)S(1)}, u32[]{:S(2)}, u32[]{:S(2)}) collective-permute-start(f32[16,640]{1,0:T(8,128)S(1)} %get-tuple-element.40), channel_id=1, source_target_pairs={{1,2},{2,1},{3,0},{0,3},{5,6},{6,5},{7,4},{4,7},{9,10},{10,9},{11,... | collective-permute-start | bytes 122888 | tf_op jit(solution)/shard_map/ppermute | solution.py:471
  12.8 3.6 %collective-permute-start.3 = (f32[16,640]{1,0:T(8,128)S(1)}, f32[16,640]{1,0:T(8,128)S(1)}, u32[]{:S(2)}, u32[]{:S(2)}) collective-permute-start(f32[16,640]{1,0:T(8,128)S(1)} %get-tuple-element.41), channel_id=1, source_target_pairs={{0,1},{1,0},{2,3},{3,2},{4,5},{5,4},{6,7},{7,6},{8,9},{9,8},{10,11... | collective-permute-start | bytes 122888 | tf_op jit(solution)/shard_map/ppermute | solution.py:471
  22.4 6.8 %collective-permute-start.4 = (f32[16,640]{1,0:T(8,128)S(1)}, f32[16,640]{1,0:T(8,128)S(1)}, u32[]{:S(2)}, u32[]{:S(2)}) collective-permute-start(f32[16,640]{1,0:T(8,128)S(1)} %get-tuple-element.63), channel_id=1, source_target_pairs={{4,8},{8,4},{12,16},{16,12},{20,24},{24,20},{28,0},{0,28},{5,9},{9... | collective-permute-start | bytes 122888 | tf_op jit(solution)/shard_map/ppermute | solution.py:471
  25.0 4.4 %collective-permute-start.5 = (f32[16,640]{1,0:T(8,128)S(1)}, f32[16,640]{1,0:T(8,128)S(1)}, u32[]{:S(2)}, u32[]{:S(2)}) collective-permute-start(f32[16,640]{1,0:T(8,128)S(1)} %get-tuple-element.64), channel_id=1, source_target_pairs={{0,4},{4,0},{8,12},{12,8},{16,20},{20,16},{24,28},{28,24},{1,5},{5... | collective-permute-start | bytes 122888 | tf_op jit(solution)/shard_map/ppermute | solution.py:471
  25.0 4.4 %collective-permute-start.6 = (f32[16,640]{1,0:T(8,128)S(1)}, f32[16,640]{1,0:T(8,128)S(1)}, u32[]{:S(2)}, u32[]{:S(2)}) collective-permute-start(f32[16,640]{1,0:T(8,128)S(1)} %get-tuple-element.65), channel_id=1, source_target_pairs={{1,2},{2,1},{3,0},{0,3},{5,6},{6,5},{7,4},{4,7},{9,10},{10,9},{11,... | collective-permute-start | bytes 122888 | tf_op jit(solution)/shard_map/ppermute | solution.py:471
  25.0 4.4 %collective-permute-start.7 = (f32[16,640]{1,0:T(8,128)S(1)}, f32[16,640]{1,0:T(8,128)S(1)}, u32[]{:S(2)}, u32[]{:S(2)}) collective-permute-start(f32[16,640]{1,0:T(8,128)S(1)} %get-tuple-element.66), channel_id=1, source_target_pairs={{0,1},{1,0},{2,3},{3,2},{4,5},{5,4},{6,7},{7,6},{8,9},{9,8},{10,11... | collective-permute-start | bytes 122888 | tf_op jit(solution)/shard_map/ppermute | solution.py:471

commit v3 on v2

--- a/solution.py
+++ b/solution.py
@@ -93,22 +93,144 @@
             emit(first + k, sums[k])
 
 
-def taylor(start_of, star_ref, forward, xs_ref, y_ref, integrals):
-    for f in range(FIELDS):
-        value = start_of(f)
-        put_operand(xs_ref, f, value)
-        for ref, weights in integrals:
-            ref[field_rows(f), :] = weights[0] * value
-    for k in range(1, ORDER):
-        wide_dot(forward, xs_ref, y_ref)
-
-        def emit(g, value, k=k):
+GROUP = 3
+
+
+class Steps:
+    def __init__(self, halo_ref):
+        self.value = halo_ref[0, 0]
+        self.bound = 4096
+
+    def __call__(self, body):
+        self.bound += 1
+        pl.when(self.value < self.bound)(body)
+
+
+def star_group(y_ref, star_ref, first, emit, order):
+    sums = [None] * GROUP
+    for f in order:
+        for d in range(3):
+            y = y_ref[d * MODES : (d + 1) * MODES, field_lanes(f)]
+            for k in range(GROUP):
+                term = y * star_ref[f, first + k, d : d + 1, :]
+                sums[k] = term if sums[k] is None else sums[k] + term
+    for k in range(GROUP):
+        emit(first + k, sums[k])
+
+
+def taylor(block, start_of, star_ref, forward_ref, xs_ref, y_ref, integrals):
+    def start():
+        for f in range(FIELDS):
+            value = start_of(f)
+            put_operand(xs_ref, f, value)
+            for ref, weights in integrals:
+                ref[field_rows(f), :] = weights[0] * value
+
+    def step(k, n):
+
+        def emit(g, value):
             if k < ORDER - 1:
                 put_operand(xs_ref, g, value)
             for ref, weights in integrals:
                 ref[field_rows(g), :] = ref[field_rows(g), :] + weights[k] * value
 
-        star_sum(y_ref, star_ref, emit)
+        if n == 0:
+            wide_dot(forward_ref[...], xs_ref, y_ref)
+        star_group(y_ref, star_ref, n * GROUP, emit, range(FIELDS))
+
+    block(start)
+    for k in range(1, ORDER):
+        block(functools.partial(step, k, 0))
+
+        def rest(k=k):
+            step(k, 1)
+            step(k, 2)
+
+        block(rest)
+
+
+PAIRS = (FIELDS + 1) // 2
+DROWS = 16
+
+
+def nt_dot(lhs, rhs):
+    return lax.dot_general(lhs, rhs, (((1,), (1,)), ((), ())), preferred_element_type=F32)
+
+
+def pair_lanes(j):
+    return slice(2 * j * LANES, min(2 * j + 2, FIELDS) * LANES)
+
+
+def pack_matrix(cluster):
+    small = jnp.where(cluster == 0, 1.0, 0.0)
+    before = lax.broadcasted_iota(jnp.int32, (LANES, LANES), 0)
+    after = lax.broadcasted_iota(jnp.int32, (LANES, LANES), 1)
+    upper = jnp.where(before < after, 1.0, 0.0).astype(BF)
+    place = big_dot(jnp.broadcast_to(small, (8, LANES)).astype(BF), upper)[0:1, :]
+    place = jnp.where(cluster == 0, place, -1.0).astype(jnp.int32)
+    row = lax.broadcasted_iota(jnp.int32, (MPAD, LANES), 0)
+    pick = jnp.where(row == place, 1.0, 0.0)
+    none = jnp.zeros_like(pick)
+    return jnp.concatenate(
+        [jnp.concatenate([pick, none], axis=1), jnp.concatenate([none, pick], axis=1)], axis=0
+    ).astype(BF)
+
+
+def pack_star(star_ref, pack_ref, packed_ref):
+    pad = jnp.zeros((DROWS - FIELDS, LANES), F32)
+    rows = []
+    for f in range(FIELDS):
+        parts = []
+        for d in range(3):
+            parts += [star_ref[f, :, d, :], pad]
+        rows.append(jnp.concatenate(parts, axis=0))
+    for j in range(PAIRS):
+        both = jnp.concatenate(rows[2 * j : 2 * j + 2], axis=1)
+        pick = pack_ref[:, 0 : both.shape[1]]
+        high, low = two_parts(both)
+        packed_ref[j] = nt_dot(high, pick) + nt_dot(low, pick)
+
+
+def packed_taylor(xs_ref, pack_ref, star_ref, forward, xp_ref, y_ref, sum_ref, weights):
+    for j in range(PAIRS):
+        lanes = pair_lanes(j)
+        pick = pack_ref[:, 0 : lanes.stop - lanes.start]
+        value = nt_dot(xs_ref[0:MPAD, lanes], pick) + nt_dot(xs_ref[MPAD : 2 * MPAD, lanes], pick)
+        value = value[0:MODES]
+        put_operand(xp_ref, j, value)
+        sum_ref[field_rows(j), :] = weights[0] * value
+    low_half = lax.broadcasted_iota(jnp.int32, (MODES, LANES), 1) < MPAD
+    for k in range(1, ORDER):
+        for j in range(0, PAIRS, 2):
+            lanes = slice(j * LANES, min(j + 2, PAIRS) * LANES)
+            y_ref[:, lanes] = big_dot(forward, xp_ref[:, lanes])
+        for j in range(PAIRS):
+            sums = []
+            for g in range(2 * j, min(2 * j + 2, FIELDS)):
+                total = None
+                for i in range(PAIRS):
+                    for d in range(3):
+                        y = y_ref[d * MODES : (d + 1) * MODES, field_lanes(i)]
+                        term = y * star_ref[i, d * DROWS + g : d * DROWS + g + 1, :]
+                        total = term if total is None else total + term
+                sums.append(total)
+            if len(sums) == 1:
+                sums.append(jnp.zeros_like(sums[0]))
+            same = jnp.where(low_half, sums[0], sums[1])
+            other = jnp.where(low_half, sums[1], sums[0])
+            value = same + pltpu.roll(other, MPAD, 1)
+            if k < ORDER - 1:
+                put_operand(xp_ref, j, value)
+            sum_ref[field_rows(j), :] = sum_ref[field_rows(j), :] + weights[k] * value
+
+
+def unpack(sum_ref, pack_ref, emit):
+    for j in range(PAIRS):
+        high, low = two_parts(sum_ref[field_rows(j), :])
+        pick = pack_ref[:, 0 : min(2, FIELDS - 2 * j) * LANES]
+        value = big_dot(high, pick) + big_dot(low, pick)
+        for n in range(min(2, FIELDS - 2 * j)):
+            emit(2 * j + n, value[:, field_lanes(n)])
 
 
 def evens():
@@ -298,14 +420,14 @@
     for copy in copies:
         copy.start()
     u_ref, star_ref, stiff_ref, halo_ref = held[:4]
-    for copy in copies[:3]:
+    for copy in copies[:4]:
         copy.wait()
     forward_ref[...] = forward_matrix(stiff_ref)
     taylor(
-        lambda f: u_ref[field_rows(f), :], star_ref, forward_ref[...], xs_ref, y_ref,
+        Steps(halo_ref), lambda f: u_ref[field_rows(f), :], star_ref, forward_ref, xs_ref, y_ref,
         [(first_ref, integral_weights(0.0, 0.5)), (second_ref, integral_weights(0.5, 1.0))],
     )
-    for copy in copies[3:]:
+    for copy in copies[4:]:
         copy.wait()
     for f in range(FIELDS):
         put_operand(xs_ref, f, first_ref[field_rows(f), :])
@@ -314,12 +436,14 @@
 
 def middle_local_kernel(
     u_ref, first_ref, star_ref, plus_ref, minus_ref, stiff_ref, face_lift_ref, project_ref,
-    part_ref, slot_ref, face_ref, turn_ref,
-    base_ref, g_ref, marks_ref, update_ref, lift_ref, pair_ref,
+    part_ref, slot_ref, face_ref, turn_ref, cluster_ref,
+    base_ref, g_ref, marks_ref, update_ref, lift_ref, pair_ref, pack_ref, packed_ref,
     xs_ref, y_ref, table_ref, z_ref, rows_ref,
 ):
     width = marks_ref.shape[1] // 4
     prepare(stiff_ref, face_lift_ref, project_ref, update_ref, lift_ref, pair_ref, rows_ref)
+    pack_ref[...] = pack_matrix(cluster_ref[...])
+    pack_star(star_ref, pack_ref, packed_ref)
     part, slot, face = part_ref[...], slot_ref[...], face_ref[...]
     for f in range(FIELDS):
         put_operand(xs_ref, f, first_ref[field_rows(f), :])
@@ -364,7 +488,9 @@
 def middle_remote_kernel(
     r0, r1, r2, r3, u_ref, base_ref, g_ref, second_ref, star_ref, minus_ref,
     forward_ref, lift_ref, pair_ref, marks_ref, part_ref, slot_ref, turn_ref, cluster_ref, halo_ref,
-    middle_ref, later_ref, gsum_ref, s0, s1, s2, s3, xs_ref, y_ref, z_ref, far_ref,
+    pack_ref,
+    middle_ref, later_ref, gsum_ref, s0, s1, s2, s3,
+    xs_ref, xp_ref, y_ref, sum_ref, z_ref, far_ref,
 ):
     pick = remote_pick(part_ref[...], slot_ref[...], r0.shape[0])
     far_ref[...] = received_faces((r0, r1, r2, r3), pair_ref[...], marks_ref, pick)
@@ -378,17 +504,20 @@
     subtract_lift(lift_ref, 3 * FACES, z_ref, base_ref, middle_ref)
     small = cluster_ref[...] == 0
     for f in range(FIELDS):
-        middle_ref[field_rows(f), :] = jnp.where(
-            small, middle_ref[field_rows(f), :], u_ref[field_rows(f), :]
-        )
-    taylor(
-        lambda f: middle_ref[field_rows(f), :], star_ref, forward_ref[...], xs_ref, y_ref,
-        [(later_ref, integral_weights(0.0, 0.5))],
-    )
-    for f in range(FIELDS):
-        later = jnp.where(small, later_ref[field_rows(f), :], second_ref[field_rows(f), :])
+        value = jnp.where(small, middle_ref[field_rows(f), :], u_ref[field_rows(f), :])
+        middle_ref[field_rows(f), :] = value
+        put_operand(xs_ref, f, value)
+    packed_taylor(
+        xs_ref, pack_ref, star_ref, forward_ref[...], xp_ref, y_ref, sum_ref,
+        integral_weights(0.0, 0.5),
+    )
+
+    def emit(f, value):
+        later = jnp.where(small, value, second_ref[field_rows(f), :])
         later_ref[field_rows(f), :] = later
         put_operand(xs_ref, f, later)
+
+    unpack(sum_ref, pack_ref, emit)
     send_rims(xs_ref, halo_ref, (s0, s1, s2, s3))
 
 
@@ -506,12 +635,14 @@
     part, slot, face, turn, cluster = held[8:]
     sends = s0, s1, s2, s3
     received = trade(sends)
-    base, g, marks, update, lift, pair = call(
+    base, g, marks, update, lift, pair, pack, packed = call(
         middle_local_kernel,
-        (u, first, star, plus, minus, stiffness, face_lift, face_project, part, slot, face, turn),
+        (u, first, star, plus, minus, stiffness, face_lift, face_project,
+         part, slot, face, turn, cluster),
         [
             state, gathered, ((8, 4 * width), F32), ((update_rows, 3 * MPAD), BF),
             ((2 * MODES, 4 * FACES), BF), ((2 * FACES, 3 * LANES), BF),
+            ((LANES, 2 * LANES), BF), ((PAIRS, 3 * DROWS, LANES), F32),
         ],
         [
             scratch_xs(), scratch_y(update_rows), pltpu.VMEM(GATHERED, F32), scratch_z(4 * FACES),
@@ -522,11 +653,15 @@
     middle, later, gsum, *sends = call(
         middle_remote_kernel,
         (
-            *received, u, base, g, second, star, minus, forward, lift, pair, marks,
-            part, slot, turn, cluster, halo,
+            *received, u, base, g, second, packed, minus, forward, lift, pair, marks,
+            part, slot, turn, cluster, halo, pack,
         ),
         [state, state, gathered] + rims,
-        [scratch_xs(), scratch_y(3 * MODES), scratch_z(3 * FACES), pltpu.VMEM(GATHERED, F32)],
+        [
+            scratch_xs(), pltpu.VMEM((3 * MPAD, PAIRS * LANES), BF),
+            pltpu.VMEM((3 * MODES, PAIRS * LANES), F32), pltpu.VMEM((PAIRS * MODES, LANES), F32),
+            scratch_z(3 * FACES), pltpu.VMEM(GATHERED, F32),
+        ],
         "middle_remote",
     )
     received = trade(sends)

time: 31.7 us -> 29.7 us (0.937)
  Pallas kernels: 19.3 us -> 17.4 us
    pallas_call x5, Pallas kernels: 19.3 us -> 17.4 us  [call(): pl.pallas_call(kernel, out_shape=out_shape, in_specs=[pl.BlockSpec(memory...]
  transfers between devices with their start and end apart: 8 -> 8, of which waited for: 2 -> 2; matrix products, arithmetic and copies ran while one was open for 0% -> 0% of each run, Pallas kernels for 16% -> 17%
where the time goes in v3:
time: 29.7 us; the launch traced here: 29.6 us
  Pallas kernels  17.4 us (59%)
  starting transfers between devices  11.8 us (40%)
  waiting for transfers between devices  0.35 us (1%)
    pallas_call x5, Pallas kernels, call(): pl.pallas_call(kernel, out_shape=out_shape, in_specs=[pl.BlockSpec(memory...  17.4 us
    ppermute x8, starting transfers between devices, swap(): return lax.ppermute(x, axis, pairs)  11.8 us
  transfers between devices with their start and end apart: 8, of which 2 were waited for; matrix products, arithmetic and copies ran while one was open for 0% of the time, Pallas kernels for 17%

profile of v3, /device:TPU:0, one launch (start us, length us, event | category | flops | bytes accessed | tf_op | source)
XLA Modules:
  0.0 29.6 jit_solution(782203443677192080)
XLA Ops:
  0.0 5.7 %first.1 = (f32[504,128]{1,0:T(8,128)S(1)}, f32[9,9,3,128]{3,2,1,0:T(4,128)S(1)}, f32[3,56,56]{2,1,0:T(8,128)S(1)}, s32[4,16]{1,0:T(4,128)S(1)}, f32[9,9,4,128]{...) custom-call(f32[504,128]{1,0:T(8,128)} %bitcast.12, ...), custom_call_target="tpu_custom_call" | custom-call | flops 1000000000 | bytes 1000000 | tf_op jit(solution)/shard_map/first/pallas_call | solution.py:570
  5.8 6.1 %collective-permute-start = (f32[16,640]{1,0:T(8,128)S(1)}, f32[16,640]{1,0:T(8,128)S(1)}, u32[]{:S(2)}, u32[]{:S(2)}) collective-permute-start(f32[16,640]{1,0:T(8,128)S(1)} %get-tuple-element.40), channel_id=1, source_target_pairs={{4,8},{8,4},{12,16},{16,12},{20,24},{24,20},{28,0},{0,28},{5,9},{9... | collective-permute-start | bytes 122888 | tf_op jit(solution)/shard_map/ppermute | solution.py:600
  11.8 0.0 collective-permute-start.1
  11.9 0.7 %collective-permute-start.2 = (f32[16,640]{1,0:T(8,128)S(1)}, f32[16,640]{1,0:T(8,128)S(1)}, u32[]{:S(2)}, u32[]{:S(2)}) collective-permute-start(f32[16,640]{1,0:T(8,128)S(1)} %get-tuple-element.42), channel_id=1, source_target_pairs={{1,2},{2,1},{3,0},{0,3},{5,6},{6,5},{7,4},{4,7},{9,10},{10,9},{11,... | collective-permute-start | bytes 122888 | tf_op jit(solution)/shard_map/ppermute | solution.py:600
  12.5 1.0 %collective-permute-start.3 = (f32[16,640]{1,0:T(8,128)S(1)}, f32[16,640]{1,0:T(8,128)S(1)}, u32[]{:S(2)}, u32[]{:S(2)}) collective-permute-start(f32[16,640]{1,0:T(8,128)S(1)} %get-tuple-element.43), channel_id=1, source_target_pairs={{0,1},{1,0},{2,3},{3,2},{4,5},{5,4},{6,7},{7,6},{8,9},{9,8},{10,11... | collective-permute-start | bytes 122888 | tf_op jit(solution)/shard_map/ppermute | solution.py:600
  13.5 2.6 %middle_local.1 = (f32[504,128]{1,0:T(8,128)S(1)}, f32[216,512]{1,0:T(8,128)S(1)}, f32[8,64]{1,0:T(8,128)S(1)}, bf16[264,192]{1,0:T(8,128)(2,1)S(1)}, bf16[112,3...) custom-call(f32[504,128]{1,0:T(8,128)S(1)} %get-tuple-element.44.u_r, ...), custom_call_target="tpu_custom_call" | custom-call | flops 1000000000 | bytes 1000000 | tf_op jit(solution)/shard_map/middle_local/pallas_call | solution.py:570
  16.1 0.0 collective-permute-done.r0
  16.1 0.0 collective-permute-done.1.r1
  16.1 0.0 collective-permute-done.2.r2
  16.1 0.0 collective-permute-done.3.r3
  16.1 4.4 %middle_remote.1 = (f32[504,128]{1,0:T(8,128)S(1)}, f32[504,128]{1,0:T(8,128)S(1)}, f32[216,512]{1,0:T(8,128)S(1)}, f32[16,640]{1,0:T(8,128)S(1)}, f32[16,640]{1...) custom-call(f32[16,640]{1,0:T(8,128)S(1)} %collective-permute-done.r0, ...), custom_call_target="tpu_custom_call" | custom-call | flops 1000000000 | bytes 1000000 | tf_op jit(solution)/shard_map/middle_remote/pallas_call | solution.py:570
  20.6 2.5 %collective-permute-start.4 = (f32[16,640]{1,0:T(8,128)S(1)}, f32[16,640]{1,0:T(8,128)S(1)}, u32[]{:S(2)}, u32[]{:S(2)}) collective-permute-start(f32[16,640]{1,0:T(8,128)S(1)} %get-tuple-element.67), channel_id=1, source_target_pairs={{4,8},{8,4},{12,16},{16,12},{20,24},{24,20},{28,0},{0,28},{5,9},{9... | collective-permute-start | bytes 122888 | tf_op jit(solution)/shard_map/ppermute | solution.py:600
  23.0 0.0 collective-permute-start.5
  23.0 0.0 collective-permute-start.6
  23.0 1.6 %collective-permute-start.7 = (f32[16,640]{1,0:T(8,128)S(1)}, f32[16,640]{1,0:T(8,128)S(1)}, u32[]{:S(2)}, u32[]{:S(2)}) collective-permute-start(f32[16,640]{1,0:T(8,128)S(1)} %get-tuple-element.70), channel_id=1, source_target_pairs={{0,1},{1,0},{2,3},{3,2},{4,5},{5,4},{6,7},{7,6},{8,9},{9,8},{10,11... | collective-permute-start | bytes 122888 | tf_op jit(solution)/shard_map/ppermute | solution.py:600
  24.6 2.5 %last_local.1.base_ref = f32[504,128]{1,0:T(8,128)S(1)} custom-call(f32[504,128]{1,0:T(8,128)S(1)} %get-tuple-element.44.u_ref, f32[504,128]{1,0:T(8,128)S(1)} %get-tuple-element.71.middle_ref, f32[504,128]{1,0:T(8,128)S(1)} %get-tuple-element.45.first_ref, f32[504,128]{1,0:T(8,128)S(1)} %get-tuple-element.59.second_ref, ...), custom_call_target="tpu_custom_call" | custom-call | flops 1000000000 | bytes 1000000 | tf_op jit(solution)/shard_map/last_local/pallas_call | solution.py:570
  27.1 0.3 collective-permute-done.4.r0
  27.4 0.1 collective-permute-done.5.r1
  27.5 0.0 collective-permute-done.6.r2
  27.5 0.0 collective-permute-done.7.r3
  27.5 2.1 %last_remote.1 = f32[504,128]{1,0:T(8,128)} custom-call(f32[16,640]{1,0:T(8,128)S(1)} %collective-permute-done.4.r0, f32[16,640]{1,0:T(8,128)S(1)} %collective-permute-done.5.r1, f32[16,640]{1,0:T(8,128)S(1)} %collective-permute-done.6.r2, f32[16,640]{1,0:T(8,128)S(1)} %collective-permute-done.7.r3, f32[504,128]{1,0:T(8,128)S(1)} %last_local.1.base_ref, ...), custom_call_target="tpu_custom_call" | custom-call | flops 1000000000 | bytes 1000000 | tf_op jit(solution)/shard_map/last_remote/pallas_call | solution.py:570
Async XLA Ops:
  5.8 10.3 %collective-permute-start = (f32[16,640]{1,0:T(8,128)S(1)}, f32[16,640]{1,0:T(8,128)S(1)}, u32[]{:S(2)}, u32[]{:S(2)}) collective-permute-start(f32[16,640]{1,0:T(8,128)S(1)} %get-tuple-element.40), channel_id=1, source_target_pairs={{4,8},{8,4},{12,16},{16,12},{20,24},{24,20},{28,0},{0,28},{5,9},{9... | collective-permute-start | bytes 122888 | tf_op jit(solution)/shard_map/ppermute | solution.py:600
  11.8 4.3 %collective-permute-start.1 = (f32[16,640]{1,0:T(8,128)S(1)}, f32[16,640]{1,0:T(8,128)S(1)}, u32[]{:S(2)}, u32[]{:S(2)}) collective-permute-start(f32[16,640]{1,0:T(8,128)S(1)} %get-tuple-element.41), channel_id=1, source_target_pairs={{0,4},{4,0},{8,12},{12,8},{16,20},{20,16},{24,28},{28,24},{1,5},{5... | collective-permute-start | bytes 122888 | tf_op jit(solution)/shard_map/ppermute | solution.py:600
  11.9 4.3 %collective-permute-start.2 = (f32[16,640]{1,0:T(8,128)S(1)}, f32[16,640]{1,0:T(8,128)S(1)}, u32[]{:S(2)}, u32[]{:S(2)}) collective-permute-start(f32[16,640]{1,0:T(8,128)S(1)} %get-tuple-element.42), channel_id=1, source_target_pairs={{1,2},{2,1},{3,0},{0,3},{5,6},{6,5},{7,4},{4,7},{9,10},{10,9},{11,... | collective-permute-start | bytes 122888 | tf_op jit(solution)/shard_map/ppermute | solution.py:600
  12.5 3.6 %collective-permute-start.3 = (f32[16,640]{1,0:T(8,128)S(1)}, f32[16,640]{1,0:T(8,128)S(1)}, u32[]{:S(2)}, u32[]{:S(2)}) collective-permute-start(f32[16,640]{1,0:T(8,128)S(1)} %get-tuple-element.43), channel_id=1, source_target_pairs={{0,1},{1,0},{2,3},{3,2},{4,5},{5,4},{6,7},{7,6},{8,9},{9,8},{10,11... | collective-permute-start | bytes 122888 | tf_op jit(solution)/shard_map/ppermute | solution.py:600
  20.6 6.8 %collective-permute-start.4 = (f32[16,640]{1,0:T(8,128)S(1)}, f32[16,640]{1,0:T(8,128)S(1)}, u32[]{:S(2)}, u32[]{:S(2)}) collective-permute-start(f32[16,640]{1,0:T(8,128)S(1)} %get-tuple-element.67), channel_id=1, source_target_pairs={{4,8},{8,4},{12,16},{16,12},{20,24},{24,20},{28,0},{0,28},{5,9},{9... | collective-permute-start | bytes 122888 | tf_op jit(solution)/shard_map/ppermute | solution.py:600
  23.0 4.4 %collective-permute-start.5 = (f32[16,640]{1,0:T(8,128)S(1)}, f32[16,640]{1,0:T(8,128)S(1)}, u32[]{:S(2)}, u32[]{:S(2)}) collective-permute-start(f32[16,640]{1,0:T(8,128)S(1)} %get-tuple-element.68), channel_id=1, source_target_pairs={{0,4},{4,0},{8,12},{12,8},{16,20},{20,16},{24,28},{28,24},{1,5},{5... | collective-permute-start | bytes 122888 | tf_op jit(solution)/shard_map/ppermute | solution.py:600
  23.0 4.4 %collective-permute-start.6 = (f32[16,640]{1,0:T(8,128)S(1)}, f32[16,640]{1,0:T(8,128)S(1)}, u32[]{:S(2)}, u32[]{:S(2)}) collective-permute-start(f32[16,640]{1,0:T(8,128)S(1)} %get-tuple-element.69), channel_id=1, source_target_pairs={{1,2},{2,1},{3,0},{0,3},{5,6},{6,5},{7,4},{4,7},{9,10},{10,9},{11,... | collective-permute-start | bytes 122888 | tf_op jit(solution)/shard_map/ppermute | solution.py:600
  23.0 4.4 %collective-permute-start.7 = (f32[16,640]{1,0:T(8,128)S(1)}, f32[16,640]{1,0:T(8,128)S(1)}, u32[]{:S(2)}, u32[]{:S(2)}) collective-permute-start(f32[16,640]{1,0:T(8,128)S(1)} %get-tuple-element.70), channel_id=1, source_target_pairs={{0,1},{1,0},{2,3},{3,2},{4,5},{5,4},{6,7},{7,6},{8,9},{9,8},{10,11... | collective-permute-start | bytes 122888 | tf_op jit(solution)/shard_map/ppermute | solution.py:600

commit v4 on v3

--- a/solution.py
+++ b/solution.py
@@ -173,7 +173,7 @@
     none = jnp.zeros_like(pick)
     return jnp.concatenate(
         [jnp.concatenate([pick, none], axis=1), jnp.concatenate([none, pick], axis=1)], axis=0
-    ).astype(BF)
+    )
 
 
 def pack_star(star_ref, pack_ref, packed_ref):
@@ -191,15 +191,7 @@
         packed_ref[j] = nt_dot(high, pick) + nt_dot(low, pick)
 
 
-def packed_taylor(xs_ref, pack_ref, star_ref, forward, xp_ref, y_ref, sum_ref, weights):
-    for j in range(PAIRS):
-        lanes = pair_lanes(j)
-        pick = pack_ref[:, 0 : lanes.stop - lanes.start]
-        value = nt_dot(xs_ref[0:MPAD, lanes], pick) + nt_dot(xs_ref[MPAD : 2 * MPAD, lanes], pick)
-        value = value[0:MODES]
-        put_operand(xp_ref, j, value)
-        sum_ref[field_rows(j), :] = weights[0] * value
-    low_half = lax.broadcasted_iota(jnp.int32, (MODES, LANES), 1) < MPAD
+def packed_taylor(star_ref, forward, xp_ref, y_ref, sum_ref, weights):
     for k in range(1, ORDER):
         for j in range(0, PAIRS, 2):
             lanes = slice(j * LANES, min(j + 2, PAIRS) * LANES)
@@ -216,12 +208,19 @@
                 sums.append(total)
             if len(sums) == 1:
                 sums.append(jnp.zeros_like(sums[0]))
-            same = jnp.where(low_half, sums[0], sums[1])
-            other = jnp.where(low_half, sums[1], sums[0])
-            value = same + pltpu.roll(other, MPAD, 1)
+            value = join_halves(*sums)
             if k < ORDER - 1:
                 put_operand(xp_ref, j, value)
             sum_ref[field_rows(j), :] = sum_ref[field_rows(j), :] + weights[k] * value
+
+
+def pack_state(base_ref, turned_ref, packed_ref):
+    for j in range(PAIRS):
+        fields = range(2 * j, min(2 * j + 2, FIELDS))
+        both = jnp.concatenate([base_ref[field_rows(f), :] for f in fields], axis=1)
+        pick = turned_ref[0 : both.shape[1], :]
+        high, low = two_parts(both)
+        packed_ref[field_rows(j), :] = big_dot(high, pick) + big_dot(low, pick)
 
 
 def unpack(sum_ref, pack_ref, emit):
@@ -237,7 +236,7 @@
     return [lax.rem(lax.axis_index(axis), 2) == 0 for axis in ("near", "dom")]
 
 
-def send_rims(xs_ref, halo_ref, sends):
+def send_pick(halo_ref):
     width = halo_ref.shape[1]
     element = lax.broadcasted_iota(jnp.int32, (LANES, width), 0)
     near_even, dom_even = evens()
@@ -247,7 +246,11 @@
         for row in (jnp.where(even, down, up), jnp.where(even, up, down)):
             pick = jnp.where(element == row, 1.0, 0.0).astype(F32)
             picks.append(jnp.transpose(pick))
-    pick = jnp.concatenate(picks, axis=0).astype(BF)
+    return jnp.concatenate(picks, axis=0).astype(BF)
+
+
+def send_rims(xs_ref, pick, sends):
+    width = sends[0].shape[0]
     for q in range((FIELDS + 1) // 2):
         fields = (2 * q, min(2 * q + 1, FIELDS - 1))
         total = None
@@ -262,6 +265,19 @@
             sends[r][:, field_lanes(q)] = total[r * width : (r + 1) * width, :]
 
 
+def send_packed(sum_ref, pick, large_sends, sends):
+    width = sends[0].shape[0]
+    half = 4 * width
+    for j in range(PAIRS):
+        value = tall(sum_ref[field_rows(j), :], MPAD)
+        high, low = two_parts(jnp.concatenate([value, value], axis=0))
+        out = nt_dot(pick, high) + nt_dot(pick, low)
+        total = jnp.where(low_half(half), out[0:half], out[half:])
+        for r in range(4):
+            rows = slice(r * width, (r + 1) * width)
+            sends[r][:, field_lanes(j)] = large_sends[r][:, field_lanes(j)] + total[rows, :]
+
+
 def local_pick(part, slot, face):
     target = jnp.where(part == 0, face * LANES + slot, -1)
     target = jnp.concatenate([target[i : i + 1, :] for i in range(4)], axis=1)
@@ -339,26 +355,123 @@
             out_ref[field_rows(g), :] = base_ref[field_rows(g), :] - lifted[:, field_lanes(n)]
 
 
-def received_faces(received, pair_matrix, marks_ref, pick):
+KINDS = 32
+LARGE_ROW = 16
+
+
+def slot_tables(
+    far, part, face, turn, cluster, minus_ref, marks_ref, slot_flux_ref, scatter_ref,
+    turned_ref, packed_scatter_ref,
+):
+    far2 = jnp.concatenate([far, far], axis=0)
+    rows = [jnp.where(face == j, 1.0, 0.0) for j in range(4)]
+    rows = [jnp.concatenate([row[i : i + 1, :] for i in range(4)], axis=1) for row in rows]
+    none = jnp.zeros((1, LANES), F32)
+    for h in range(3):
+        turned = jnp.where(turn == h, 1.0, 0.0)
+        for i in range(4):
+            pieces = [none] * 4
+            pieces[i] = turned[i : i + 1, :]
+            rows.append(jnp.concatenate(pieces, axis=1))
+    rows.append(jnp.concatenate([jnp.where(cluster == 0, 0.0, 1.0)] * 4, axis=1))
+    kinds = tall(jnp.concatenate(rows, axis=0), KINDS).astype(BF)
+    marks_ref[...] = nt_dot(kinds, far2)
+    tiles = []
+    for f in range(2 * PAIRS):
+        if f < FIELDS:
+            row = jnp.concatenate([minus_ref[f, :, i, :] for i in range(4)], axis=1)
+            tiles.append(tall(row, DROWS))
+        else:
+            tiles.append(jnp.zeros((DROWS, 4 * LANES), F32))
+    flux = jnp.concatenate(
+        [jnp.concatenate(tiles[2 * j : 2 * j + 2], axis=1) for j in range(PAIRS)], axis=0
+    )
+    none = jnp.zeros_like(far)
+    pick = jnp.concatenate(
+        [jnp.concatenate([far, none], axis=1), jnp.concatenate([none, far], axis=1)], axis=0
+    )
+    high, low = two_parts(flux)
+    slot_flux_ref[...] = nt_dot(high, pick) + nt_dot(low, pick)
+    place = far[:, 0:LANES] + far[:, LANES : 2 * LANES]
+    place = place + far[:, 2 * LANES : 3 * LANES] + far[:, 3 * LANES :]
+    packed_scatter_ref[...] = packed_pick(place, turned_ref)
+    none = jnp.zeros_like(place)
+    scatter_ref[...] = jnp.concatenate(
+        [jnp.concatenate([place, none], axis=1), jnp.concatenate([none, place], axis=1)], axis=0
+    )
+
+
+def packed_pick(pick, turned_ref):
+    halves = [big_dot(pick, turned_ref[n * LANES : (n + 1) * LANES, :]) for n in range(2)]
+    return jnp.concatenate(halves, axis=0).astype(BF)
+
+
+def low_half(rows):
+    return lax.broadcasted_iota(jnp.int32, (rows, LANES), 1) < MPAD
+
+
+def slot_traces(received, pair_matrix, marks_ref):
     rims = jnp.concatenate([ref[...] for ref in received], axis=0)
-    high, low = two_parts(rims)
-    parts = []
-    for q in range((FIELDS + 1) // 2):
-        lanes = field_lanes(q)
-        rhs = jnp.concatenate([high[:, lanes], low[:, lanes], high[:, lanes]], axis=1)
-        out = lax.dot_general(
-            pair_matrix, rhs, (((1,), (1,)), ((), ())), preferred_element_type=F32
-        )
-        for side in range(2):
-            if 2 * q + side < FIELDS:
-                total = None
-                for j in range(4):
-                    start = side * FACES + j * NPAD
-                    term = out[start : start + NPAD, :] * marks_ref[j : j + 1, :]
+    rims = jnp.concatenate([rims, rims], axis=0)
+    rhs = []
+    for q in range(PAIRS):
+        high, low = two_parts(jnp.transpose(rims[:, field_lanes(q)]))
+        rhs.append(jnp.concatenate([high, low, high], axis=0))
+    traces = []
+    for q in range(0, PAIRS, 2):
+        out = big_dot(pair_matrix, jnp.concatenate(rhs[q : q + 2], axis=1))
+        for n in range(min(2, PAIRS - q)):
+            tile = out[:, field_lanes(n)]
+            both = jnp.where(low_half(FACES), tile[0:FACES], tile[FACES:])
+            total = None
+            for j in range(4):
+                term = both[j * NPAD : (j + 1) * NPAD, :] * marks_ref[j : j + 1, :]
+                total = term if total is None else total + term
+            traces.append(total)
+    return traces
+
+
+def join_halves(first, second):
+    low = low_half(first.shape[0])
+    same = jnp.where(low, first, second)
+    other = jnp.where(low, second, first)
+    return same + pltpu.roll(other, MPAD, 1)
+
+
+def slot_lift(traces, slot_flux_ref, marks_ref, lift_ref, scatter_ref, z_ref, emit):
+    masks = []
+    for n in range(0, 12, 2):
+        rows = [
+            jnp.broadcast_to(marks_ref[4 + n + i : 5 + n + i, :], (NPAD, LANES)) for i in range(2)
+        ]
+        masks.append(jnp.concatenate(rows, axis=0).astype(BF))
+    for j in range(PAIRS):
+        sums = []
+        for g in range(2 * j, 2 * j + 2):
+            total = None
+            if g < FIELDS:
+                for i in range(PAIRS):
+                    row = i * DROWS + g
+                    term = traces[i] * slot_flux_ref[row : row + 1, :]
                     total = term if total is None else total + term
-                parts.append(total)
-    high, low = two_parts(jnp.concatenate(parts, axis=0))
-    return big_dot(high, pick) + big_dot(low, pick)
+            else:
+                total = jnp.zeros_like(traces[0])
+            sums.append(total)
+        value = join_halves(*sums)
+        for piece, part in enumerate(two_parts(jnp.concatenate([value, value], axis=0))):
+            for n in range(6):
+                z_ref[piece, 2 * n * NPAD : 2 * (n + 1) * NPAD, field_lanes(j)] = part * masks[n]
+    both = lift_ref[:, 0 : 3 * FACES]
+    for j in range(0, PAIRS, 2):
+        tiles = range(j, min(j + 2, PAIRS))
+        lanes = slice(j * LANES, (tiles[-1] + 1) * LANES)
+        high = big_dot(both, z_ref[0, :, lanes])
+        lifted = high[0:MODES] + high[MODES:] + big_dot(both[0:MODES], z_ref[1, :, lanes])
+        for n, tile in enumerate(tiles):
+            high, low = two_parts(lifted[:, field_lanes(n)])
+            count = min(scatter_ref.shape[1], (FIELDS - 2 * tile) * LANES)
+            pick = scatter_ref[:, 0:count]
+            emit(tile, big_dot(high, pick) + big_dot(low, pick))
 
 
 def wide(x):
@@ -431,37 +544,45 @@
         copy.wait()
     for f in range(FIELDS):
         put_operand(xs_ref, f, first_ref[field_rows(f), :])
-    send_rims(xs_ref, halo_ref, (s0, s1, s2, s3))
+    send_rims(xs_ref, send_pick(halo_ref), (s0, s1, s2, s3))
 
 
 def middle_local_kernel(
-    u_ref, first_ref, star_ref, plus_ref, minus_ref, stiff_ref, face_lift_ref, project_ref,
-    part_ref, slot_ref, face_ref, turn_ref, cluster_ref,
-    base_ref, g_ref, marks_ref, update_ref, lift_ref, pair_ref, pack_ref, packed_ref,
-    xs_ref, y_ref, table_ref, z_ref, rows_ref,
+    u_ref, first_ref, second_ref, star_ref, plus_ref, minus_ref, stiff_ref, face_lift_ref, project_ref,
+    part_ref, slot_ref, face_ref, turn_ref, cluster_ref, halo_ref,
+    start_ref, g_ref, marks_ref, update_ref, lift_ref, pair_ref, pack_ref, packed_ref,
+    slot_flux_ref, scatter_ref, pick_ref, packed_scatter_ref, packed_send_ref, s0, s1, s2, s3,
+    turned_ref, base_ref, xs_ref, y_ref, table_ref, z_ref, rows_ref,
 ):
-    width = marks_ref.shape[1] // 4
+    width = halo_ref.shape[1]
     prepare(stiff_ref, face_lift_ref, project_ref, update_ref, lift_ref, pair_ref, rows_ref)
-    pack_ref[...] = pack_matrix(cluster_ref[...])
+    pack = pack_matrix(cluster_ref[...])
+    pack_ref[...] = pack.astype(BF)
+    turned_ref[...] = jnp.concatenate(
+        [jnp.transpose(pack[:, 0:LANES]), jnp.transpose(pack[:, LANES:])], axis=0
+    ).astype(BF)
     pack_star(star_ref, pack_ref, packed_ref)
     part, slot, face = part_ref[...], slot_ref[...], face_ref[...]
     for f in range(FIELDS):
         put_operand(xs_ref, f, first_ref[field_rows(f), :])
     wide_dot(update_ref[...], xs_ref, y_ref)
-    g_ref[...] = pick_faces(y_ref, 3 * MODES, table_ref, local_pick(part, slot, face))
-    far = remote_pick(part, slot, width)
-    rows = [jnp.where(face == j, 1.0, 0.0) for j in range(4)]
-    kinds = jnp.concatenate(
-        [jnp.concatenate([row[i : i + 1, :] for i in range(4)], axis=1) for row in rows], axis=0
-    )
-    kinds = jnp.concatenate([kinds, jnp.zeros_like(kinds)], axis=0).astype(BF)
-    marks_ref[...] = lax.dot_general(
-        kinds, far, (((1,), (1,)), ((), ())), preferred_element_type=F32
+    pick_ref[...] = local_pick(part, slot, face)
+    g_ref[...] = pick_faces(y_ref, 3 * MODES, table_ref, pick_ref[...])
+    slot_tables(
+        remote_pick(part, slot, width), part, face, turn_ref[...], cluster_ref[...], minus_ref,
+        marks_ref, slot_flux_ref, scatter_ref, turned_ref, packed_scatter_ref,
     )
     finish_local(
         lambda f: u_ref[field_rows(f), :], star_ref, plus_ref, minus_ref, lift_ref,
         turn_ref[...], y_ref, g_ref, z_ref, base_ref,
     )
+    pack_state(base_ref, turned_ref, start_ref)
+    large = cluster_ref[...] != 0
+    for f in range(FIELDS):
+        put_operand(xs_ref, f, jnp.where(large, second_ref[field_rows(f), :], 0.0))
+    pick = send_pick(halo_ref)
+    send_rims(xs_ref, pick, (s0, s1, s2, s3))
+    packed_send_ref[...] = packed_pick(pick, turned_ref)
 
 
 def finish_local(base_of, star_ref, plus_ref, minus_ref, lift_ref, turn, y_ref, g_ref, z_ref, base_ref):
@@ -486,53 +607,49 @@
 
 
 def middle_remote_kernel(
-    r0, r1, r2, r3, u_ref, base_ref, g_ref, second_ref, star_ref, minus_ref,
-    forward_ref, lift_ref, pair_ref, marks_ref, part_ref, slot_ref, turn_ref, cluster_ref, halo_ref,
-    pack_ref,
-    middle_ref, later_ref, gsum_ref, s0, s1, s2, s3,
-    xs_ref, xp_ref, y_ref, sum_ref, z_ref, far_ref,
+    r0, r1, r2, r3, start_ref, star_ref, slot_flux_ref, scatter_ref, forward_ref, lift_ref, pair_ref,
+    marks_ref, pick_ref, l0, l1, l2, l3,
+    middle_ref, sum_ref, traces_ref, s0, s1, s2, s3,
+    xp_ref, y_ref, z_ref,
 ):
-    pick = remote_pick(part_ref[...], slot_ref[...], r0.shape[0])
-    far_ref[...] = received_faces((r0, r1, r2, r3), pair_ref[...], marks_ref, pick)
-    gsum_ref[...] = g_ref[...] + far_ref[...]
-    masks = turn_masks(turn_ref[...])
-    flux_sum(
-        lambda i, f: far_ref[f * NPAD : (f + 1) * NPAD, i * LANES : (i + 1) * LANES],
-        minus_ref,
-        lambda g, value: stack_turned(z_ref, g, value, masks),
-    )
-    subtract_lift(lift_ref, 3 * FACES, z_ref, base_ref, middle_ref)
-    small = cluster_ref[...] == 0
-    for f in range(FIELDS):
-        value = jnp.where(small, middle_ref[field_rows(f), :], u_ref[field_rows(f), :])
-        middle_ref[field_rows(f), :] = value
-        put_operand(xs_ref, f, value)
-    packed_taylor(
-        xs_ref, pack_ref, star_ref, forward_ref[...], xp_ref, y_ref, sum_ref,
-        integral_weights(0.0, 0.5),
-    )
-
-    def emit(f, value):
-        later = jnp.where(small, value, second_ref[field_rows(f), :])
-        later_ref[field_rows(f), :] = later
-        put_operand(xs_ref, f, later)
-
-    unpack(sum_ref, pack_ref, emit)
-    send_rims(xs_ref, halo_ref, (s0, s1, s2, s3))
+    weights = integral_weights(0.0, 0.5)
+    traces = slot_traces((r0, r1, r2, r3), pair_ref[...], marks_ref)
+    traces_ref[...] = jnp.concatenate(traces, axis=0)
+
+    def take(j, lifted):
+        rows = field_rows(j)
+        value = start_ref[rows, :] - lifted
+        middle_ref[rows, :] = value
+        sum_ref[rows, :] = weights[0] * value
+        put_operand(xp_ref, j, value)
+
+    slot_lift(traces, slot_flux_ref, marks_ref, lift_ref, scatter_ref, z_ref, take)
+    packed_taylor(star_ref, forward_ref[...], xp_ref, y_ref, sum_ref, weights)
+    send_packed(sum_ref, pick_ref[...], (l0, l1, l2, l3), (s0, s1, s2, s3))
 
 
 def last_local_kernel(
-    u_ref, middle_ref, first_ref, second_ref, later_ref, gsum_ref, star_ref, plus_ref, minus_ref,
-    update_ref, lift_ref, part_ref, slot_ref, face_ref, turn_ref, cluster_ref,
-    base_ref, xs_ref, y_ref, table_ref, z_ref, g_ref,
+    u_ref, packed_middle_ref, first_ref, second_ref, packed_later_ref, gfirst_ref, star_ref, plus_ref,
+    minus_ref, update_ref, lift_ref, pick_ref, turn_ref, cluster_ref, pack_ref,
+    base_ref, xs_ref, y_ref, table_ref, z_ref, g_ref, middle_ref, later_ref,
 ):
     small = cluster_ref[...] == 0
+
+    def choose(target, other):
+        def emit(f, value):
+            rows = field_rows(f)
+            target[rows, :] = jnp.where(small, value, other[rows, :])
+
+        return emit
+
+    unpack(packed_later_ref, pack_ref, choose(later_ref, second_ref))
+    unpack(packed_middle_ref, pack_ref, choose(middle_ref, u_ref))
     for f in range(FIELDS):
         put_operand(xs_ref, f, later_ref[field_rows(f), :])
     wide_dot(update_ref[3 * MODES :, :], xs_ref, y_ref)
-    near = pick_faces(y_ref, 0, table_ref, local_pick(part_ref[...], slot_ref[...], face_ref[...]))
+    near = pick_faces(y_ref, 0, table_ref, pick_ref[...])
     large4 = jnp.concatenate([jnp.where(small, 0.0, 1.0)] * 4, axis=1)
-    g_ref[...] = near + gsum_ref[...] * large4
+    g_ref[...] = near + gfirst_ref[...] * large4
     for f in range(FIELDS):
         rows = field_rows(f)
         put_operand(
@@ -546,32 +663,41 @@
 
 
 def last_remote_kernel(
-    r0, r1, r2, r3, base_ref, minus_ref, lift_ref, pair_ref, marks_ref, part_ref, slot_ref, turn_ref,
-    out_ref, z_ref, far_ref,
+    r0, r1, r2, r3, base_ref, traces_ref, slot_flux_ref, scatter_ref, lift_ref, pair_ref, marks_ref,
+    out_hbm, z_ref, done_ref, sems,
 ):
-    pick = remote_pick(part_ref[...], slot_ref[...], r0.shape[0])
-    far_ref[...] = received_faces((r0, r1, r2, r3), pair_ref[...], marks_ref, pick)
-    masks = turn_masks(turn_ref[...])
-    flux_sum(
-        lambda i, f: far_ref[f * NPAD : (f + 1) * NPAD, i * LANES : (i + 1) * LANES],
-        minus_ref,
-        lambda g, value: stack_turned(z_ref, g, value, masks),
-    )
-    subtract_lift(lift_ref, 3 * FACES, z_ref, base_ref, out_ref)
-
-
-VM = pl.BlockSpec(memory_space=pltpu.VMEM)
+    large = marks_ref[LARGE_ROW : LARGE_ROW + 1, :]
+    traces = slot_traces((r0, r1, r2, r3), pair_ref[...], marks_ref)
+    for j in range(PAIRS):
+        traces[j] = traces[j] + traces_ref[j * NPAD : (j + 1) * NPAD, :] * large
+    copies = []
+
+    def emit(tile, lifted):
+        for k in range(lifted.shape[1] // LANES):
+            rows = field_rows(2 * tile + k)
+            done_ref[rows, :] = base_ref[rows, :] - lifted[:, field_lanes(k)]
+            copy = pltpu.make_async_copy(
+                done_ref.at[rows, :], out_hbm.at[rows, :], sems.at[2 * tile + k]
+            )
+            copy.start()
+            copies.append(copy)
+
+    slot_lift(traces, slot_flux_ref, marks_ref, lift_ref, scatter_ref, z_ref, emit)
+    for copy in copies:
+        copy.wait()
+
+
 STATE = (FIELDS * MODES, LANES)
 GATHERED = (FIELDS * NPAD, 4 * LANES)
 
 
-def call(kernel, inputs, outs, scratch, name, space=pltpu.VMEM):
+def call(kernel, inputs, outs, scratch, name, space=pltpu.VMEM, out_space=pltpu.VMEM):
     out_shape = [jax.ShapeDtypeStruct(shape, kind) for shape, kind in outs]
     return pl.pallas_call(
         kernel,
         out_shape=out_shape,
         in_specs=[pl.BlockSpec(memory_space=space)] * len(inputs),
-        out_specs=[VM] * len(out_shape),
+        out_specs=[pl.BlockSpec(memory_space=out_space)] * len(out_shape),
         scratch_shapes=scratch,
         compiler_params=pltpu.CompilerParams(vmem_limit_bytes=24 << 20),
         cost_estimate=pl.CostEstimate(flops=10**9, bytes_accessed=10**6, transcendentals=0),
@@ -585,6 +711,10 @@
 
 def scratch_y(rows):
     return pltpu.VMEM((rows, FIELDS * LANES), F32)
+
+
+def scratch_slots():
+    return pltpu.VMEM((2, 3 * FACES, PAIRS * LANES), BF)
 
 
 def scratch_z(rows):
@@ -635,32 +765,41 @@
     part, slot, face, turn, cluster = held[8:]
     sends = s0, s1, s2, s3
     received = trade(sends)
-    base, g, marks, update, lift, pair, pack, packed = call(
+    packed_state = ((PAIRS * MODES, LANES), F32)
+    square, tall_square = ((LANES, LANES), BF), ((LANES, 2 * LANES), BF)
+    (
+        start, g, marks, update, lift, pair, pack, packed, slot_flux, scatter, pick,
+        packed_scatter, packed_send, *large_sends,
+    ) = call(
         middle_local_kernel,
-        (u, first, star, plus, minus, stiffness, face_lift, face_project,
-         part, slot, face, turn, cluster),
+        (
+            u, first, second, star, plus, minus, stiffness, face_lift, face_project,
+            part, slot, face, turn, cluster, halo,
+        ),
         [
-            state, gathered, ((8, 4 * width), F32), ((update_rows, 3 * MPAD), BF),
+            packed_state, gathered, ((KINDS, LANES), F32), ((update_rows, 3 * MPAD), BF),
             ((2 * MODES, 4 * FACES), BF), ((2 * FACES, 3 * LANES), BF),
-            ((LANES, 2 * LANES), BF), ((PAIRS, 3 * DROWS, LANES), F32),
-        ],
+            tall_square, ((PAIRS, 3 * DROWS, LANES), F32),
+            ((PAIRS * DROWS, LANES), F32), tall_square, ((4 * LANES, 4 * LANES), BF),
+            square, square,
+        ] + rims,
         [
+            pltpu.VMEM((2 * LANES, LANES), BF), pltpu.VMEM(STATE, F32),
             scratch_xs(), scratch_y(update_rows), pltpu.VMEM(GATHERED, F32), scratch_z(4 * FACES),
             pltpu.VMEM((4 * FACES, LANES), F32),
         ],
         "middle_local",
     )
-    middle, later, gsum, *sends = call(
+    middle, later, traces, *sends = call(
         middle_remote_kernel,
         (
-            *received, u, base, g, second, packed, minus, forward, lift, pair, marks,
-            part, slot, turn, cluster, halo, pack,
+            *received, start, packed, slot_flux, packed_scatter, forward, lift, pair, marks,
+            packed_send, *large_sends,
         ),
-        [state, state, gathered] + rims,
+        [packed_state, packed_state, ((PAIRS * NPAD, LANES), F32)] + rims,
         [
-            scratch_xs(), pltpu.VMEM((3 * MPAD, PAIRS * LANES), BF),
-            pltpu.VMEM((3 * MODES, PAIRS * LANES), F32), pltpu.VMEM((PAIRS * MODES, LANES), F32),
-            scratch_z(3 * FACES), pltpu.VMEM(GATHERED, F32),
+            pltpu.VMEM((3 * MPAD, PAIRS * LANES), BF), pltpu.VMEM((3 * MODES, PAIRS * LANES), F32),
+            scratch_slots(),
         ],
         "middle_remote",
     )
@@ -668,22 +807,22 @@
     (base,) = call(
         last_local_kernel,
         (
-            u, middle, first, second, later, gsum, star, plus, minus, update, lift,
-            part, slot, face, turn, cluster,
+            u, middle, first, second, later, g, star, plus, minus, update, lift,
+            pick, turn, cluster, pack,
         ),
         [state],
         [
             scratch_xs(), scratch_y(update_rows), pltpu.VMEM(GATHERED, F32), scratch_z(4 * FACES),
-            pltpu.VMEM(GATHERED, F32),
+            pltpu.VMEM(GATHERED, F32), pltpu.VMEM(STATE, F32), pltpu.VMEM(STATE, F32),
         ],
         "last_local",
     )
     (out,) = call(
         last_remote_kernel,
-        (*received, base, minus, lift, pair, marks, part, slot, turn),
+        (*received, base, traces, slot_flux, scatter, lift, pair, marks),
         [state],
-        [scratch_z(3 * FACES), pltpu.VMEM(GATHERED, F32)],
-        "last_remote",
+        [scratch_slots(), pltpu.VMEM(STATE, F32), pltpu.SemaphoreType.DMA((FIELDS,))],
+        "last_remote", out_space=pltpu.HBM,
     )
     return jnp.transpose(out.reshape(FIELDS, MODES, LANES), (1, 0, 2))
 

time: 29.7 us -> 30.3 us (1.020)
  starting transfers between devices: 11.8 us -> 11 us
  Pallas kernels: 17.4 us -> 18 us
  waiting for transfers between devices: 0.35 us -> 0.84 us
    ppermute x8, starting transfers between devices: 11.8 us -> 11 us  [swap(): return lax.ppermute(x, axis, pairs)]
    pallas_call x5, Pallas kernels: 17.4 us -> 18 us  [call(): pl.pallas_call(kernel, out_shape=out_shape, in_specs=[pl.BlockSpec(memory...]
    ppermute x8, waiting for transfers between devices: 0.35 us -> 0.84 us  [swap(): return lax.ppermute(x, axis, pairs)]
  transfers between devices with their start and end apart: 8 -> 8, of which waited for: 2 -> 1; matrix products, arithmetic and copies ran while one was open for 0% -> 0% of each run, Pallas kernels for 17% -> 20%
where the time goes in v4:
time: 30.3 us; the launch traced here: 30.1 us
  Pallas kernels  18 us (59%)
  starting transfers between devices  11 us (36%)
  waiting for transfers between devices  0.84 us (3%)
    pallas_call x5, Pallas kernels, call(): pl.pallas_call(kernel, out_shape=out_shape, in_specs=[pl.BlockSpec(memory...  18 us
    ppermute x8, starting transfers between devices, swap(): return lax.ppermute(x, axis, pairs)  11 us
    ppermute x8, waiting for transfers between devices, swap(): return lax.ppermute(x, axis, pairs)  0.84 us
  transfers between devices with their start and end apart: 8, of which 1 were waited for; matrix products, arithmetic and copies ran while one was open for 0% of the time, Pallas kernels for 20%

profile of v4, /device:TPU:0, one launch (start us, length us, event | category | flops | bytes accessed | tf_op | source)
XLA Modules:
  0.0 30.1 jit_solution(6612923310460828138)
XLA Ops:
  0.0 5.9 %first.1 = (f32[504,128]{1,0:T(8,128)S(1)}, f32[9,9,3,128]{3,2,1,0:T(4,128)S(1)}, f32[3,56,56]{2,1,0:T(8,128)S(1)}, s32[4,16]{1,0:T(4,128)S(1)}, f32[9,9,4,128]{...) custom-call(f32[504,128]{1,0:T(8,128)} %bitcast.12, ...), custom_call_target="tpu_custom_call" | custom-call | flops 1000000000 | bytes 1000000 | tf_op jit(solution)/shard_map/first/pallas_call | solution.py:696
  5.9 6.1 %collective-permute-start = (f32[16,640]{1,0:T(8,128)S(1)}, f32[16,640]{1,0:T(8,128)S(1)}, u32[]{:S(2)}, u32[]{:S(2)}) collective-permute-start(f32[16,640]{1,0:T(8,128)S(1)} %get-tuple-element.49), channel_id=1, source_target_pairs={{4,8},{8,4},{12,16},{16,12},{20,24},{24,20},{28,0},{0,28},{5,9},{9... | collective-permute-start | bytes 122888 | tf_op jit(solution)/shard_map/ppermute | solution.py:730
  12.0 0.0 collective-permute-start.1
  12.0 0.7 %collective-permute-start.2 = (f32[16,640]{1,0:T(8,128)S(1)}, f32[16,640]{1,0:T(8,128)S(1)}, u32[]{:S(2)}, u32[]{:S(2)}) collective-permute-start(f32[16,640]{1,0:T(8,128)S(1)} %get-tuple-element.51), channel_id=1, source_target_pairs={{1,2},{2,1},{3,0},{0,3},{5,6},{6,5},{7,4},{4,7},{9,10},{10,9},{11,... | collective-permute-start | bytes 122888 | tf_op jit(solution)/shard_map/ppermute | solution.py:730
  12.7 1.0 %collective-permute-start.3 = (f32[16,640]{1,0:T(8,128)S(1)}, f32[16,640]{1,0:T(8,128)S(1)}, u32[]{:S(2)}, u32[]{:S(2)}) collective-permute-start(f32[16,640]{1,0:T(8,128)S(1)} %get-tuple-element.52), channel_id=1, source_target_pairs={{0,1},{1,0},{2,3},{3,2},{4,5},{5,4},{6,7},{7,6},{8,9},{9,8},{10,11... | collective-permute-start | bytes 122888 | tf_op jit(solution)/shard_map/ppermute | solution.py:730
  13.6 3.4 %middle_local.1 = (f32[280,128]{1,0:T(8,128)S(1)}, f32[216,512]{1,0:T(8,128)S(1)}, f32[32,128]{1,0:T(8,128)S(1)}, bf16[264,192]{1,0:T(8,128)(2,1)S(1)}, bf16[112...) custom-call(f32[504,128]{1,0:T(8,128)S(1)} %get-tuple-element.53.u_r, ...), custom_call_target="tpu_custom_call" | custom-call | flops 1000000000 | bytes 1000000 | tf_op jit(solution)/shard_map/middle_local/pallas_call | solution.py:696
  17.1 0.0 collective-permute-done.r0
  17.1 0.0 collective-permute-done.1.r1
  17.1 0.0 collective-permute-done.2.r2
  17.1 0.0 collective-permute-done.3.r3
  17.1 4.0 %middle_remote.1 = (f32[280,128]{1,0:T(8,128)S(1)}, f32[280,128]{1,0:T(8,128)S(1)}, f32[120,128]{1,0:T(8,128)S(1)}, f32[16,640]{1,0:T(8,128)S(1)}, f32[16,640]{1...) custom-call(f32[16,640]{1,0:T(8,128)S(1)} %collective-permute-done.r0, ...), custom_call_target="tpu_custom_call" | custom-call | flops 1000000000 | bytes 1000000 | tf_op jit(solution)/shard_map/middle_remote/pallas_call | solution.py:696
  21.1 2.0 %collective-permute-start.4 = (f32[16,640]{1,0:T(8,128)S(1)}, f32[16,640]{1,0:T(8,128)S(1)}, u32[]{:S(2)}, u32[]{:S(2)}) collective-permute-start(f32[16,640]{1,0:T(8,128)S(1)} %get-tuple-element.81), channel_id=1, source_target_pairs={{4,8},{8,4},{12,16},{16,12},{20,24},{24,20},{28,0},{0,28},{5,9},{9... | collective-permute-start | bytes 122888 | tf_op jit(solution)/shard_map/ppermute | solution.py:730
  23.1 0.2 collective-permute-start.5
  23.3 0.0 collective-permute-start.6
  23.3 1.1 %collective-permute-start.7 = (f32[16,640]{1,0:T(8,128)S(1)}, f32[16,640]{1,0:T(8,128)S(1)}, u32[]{:S(2)}, u32[]{:S(2)}) collective-permute-start(f32[16,640]{1,0:T(8,128)S(1)} %get-tuple-element.84), channel_id=1, source_target_pairs={{0,1},{1,0},{2,3},{3,2},{4,5},{5,4},{6,7},{7,6},{8,9},{9,8},{10,11... | collective-permute-start | bytes 122888 | tf_op jit(solution)/shard_map/ppermute | solution.py:730
  24.4 2.6 %last_local.1.base_ref = f32[504,128]{1,0:T(8,128)S(1)} custom-call(f32[504,128]{1,0:T(8,128)S(1)} %get-tuple-element.53.u_ref, f32[280,128]{1,0:T(8,128)S(1)} %get-tuple-element.85.packed_middle_ref, f32[504,128]{1,0:T(8,128)S(1)} %get-tuple-element.54.first_ref, f32[504,128]{1,0:T(8,128)S(1)} %get-tuple-element.55.second_ref, ...), custom_call_target="tpu_custom_call" | custom-call | flops 1000000000 | bytes 1000000 | tf_op jit(solution)/shard_map/last_local/pallas_call | solution.py:696
  27.1 0.8 %collective-permute-done.4.r0 = f32[16,640]{1,0:T(8,128)S(1)} collective-permute-done((f32[16,640]{1,0:T(8,128)S(1)}, f32[16,640]{1,0:T(8,128)S(1)}, u32[]{:S(2)}, u32[]{:S(2)}) %collective-permute-start.4) | collective-permute-done | bytes 40992 | tf_op jit(solution)/shard_map/ppermute | solution.py:730
  27.9 0.0 collective-permute-done.5.r1
  27.9 0.0 collective-permute-done.6.r2
  27.9 0.0 collective-permute-done.7.r3
  27.9 2.1 %last_remote.1 = f32[504,128]{1,0:T(8,128)} custom-call(f32[16,640]{1,0:T(8,128)S(1)} %collective-permute-done.4.r0, f32[16,640]{1,0:T(8,128)S(1)} %collective-permute-done.5.r1, f32[16,640]{1,0:T(8,128)S(1)} %collective-permute-done.6.r2, f32[16,640]{1,0:T(8,128)S(1)} %collective-permute-done.7.r3, f32[504,128]{1,0:T(8,128)S(1)} %last_local.1.base_ref, ...), custom_call_target="tpu_custom_call" | custom-call | flops 1000000000 | bytes 1000000 | tf_op jit(solution)/shard_map/last_remote/pallas_call | solution.py:696
Async XLA Ops:
  5.9 11.1 %collective-permute-start = (f32[16,640]{1,0:T(8,128)S(1)}, f32[16,640]{1,0:T(8,128)S(1)}, u32[]{:S(2)}, u32[]{:S(2)}) collective-permute-start(f32[16,640]{1,0:T(8,128)S(1)} %get-tuple-element.49), channel_id=1, source_target_pairs={{4,8},{8,4},{12,16},{16,12},{20,24},{24,20},{28,0},{0,28},{5,9},{9... | collective-permute-start | bytes 122888 | tf_op jit(solution)/shard_map/ppermute | solution.py:730
  12.0 5.1 %collective-permute-start.1 = (f32[16,640]{1,0:T(8,128)S(1)}, f32[16,640]{1,0:T(8,128)S(1)}, u32[]{:S(2)}, u32[]{:S(2)}) collective-permute-start(f32[16,640]{1,0:T(8,128)S(1)} %get-tuple-element.50), channel_id=1, source_target_pairs={{0,4},{4,0},{8,12},{12,8},{16,20},{20,16},{24,28},{28,24},{1,5},{5... | collective-permute-start | bytes 122888 | tf_op jit(solution)/shard_map/ppermute | solution.py:730
  12.0 5.1 %collective-permute-start.2 = (f32[16,640]{1,0:T(8,128)S(1)}, f32[16,640]{1,0:T(8,128)S(1)}, u32[]{:S(2)}, u32[]{:S(2)}) collective-permute-start(f32[16,640]{1,0:T(8,128)S(1)} %get-tuple-element.51), channel_id=1, source_target_pairs={{1,2},{2,1},{3,0},{0,3},{5,6},{6,5},{7,4},{4,7},{9,10},{10,9},{11,... | collective-permute-start | bytes 122888 | tf_op jit(solution)/shard_map/ppermute | solution.py:730
  12.7 4.4 %collective-permute-start.3 = (f32[16,640]{1,0:T(8,128)S(1)}, f32[16,640]{1,0:T(8,128)S(1)}, u32[]{:S(2)}, u32[]{:S(2)}) collective-permute-start(f32[16,640]{1,0:T(8,128)S(1)} %get-tuple-element.52), channel_id=1, source_target_pairs={{0,1},{1,0},{2,3},{3,2},{4,5},{5,4},{6,7},{7,6},{8,9},{9,8},{10,11... | collective-permute-start | bytes 122888 | tf_op jit(solution)/shard_map/ppermute | solution.py:730
  21.1 6.8 %collective-permute-start.4 = (f32[16,640]{1,0:T(8,128)S(1)}, f32[16,640]{1,0:T(8,128)S(1)}, u32[]{:S(2)}, u32[]{:S(2)}) collective-permute-start(f32[16,640]{1,0:T(8,128)S(1)} %get-tuple-element.81), channel_id=1, source_target_pairs={{4,8},{8,4},{12,16},{16,12},{20,24},{24,20},{28,0},{0,28},{5,9},{9... | collective-permute-start | bytes 122888 | tf_op jit(solution)/shard_map/ppermute | solution.py:730
  23.1 4.8 %collective-permute-start.5 = (f32[16,640]{1,0:T(8,128)S(1)}, f32[16,640]{1,0:T(8,128)S(1)}, u32[]{:S(2)}, u32[]{:S(2)}) collective-permute-start(f32[16,640]{1,0:T(8,128)S(1)} %get-tuple-element.82), channel_id=1, source_target_pairs={{0,4},{4,0},{8,12},{12,8},{16,20},{20,16},{24,28},{28,24},{1,5},{5... | collective-permute-start | bytes 122888 | tf_op jit(solution)/shard_map/ppermute | solution.py:730
  23.3 4.6 %collective-permute-start.6 = (f32[16,640]{1,0:T(8,128)S(1)}, f32[16,640]{1,0:T(8,128)S(1)}, u32[]{:S(2)}, u32[]{:S(2)}) collective-permute-start(f32[16,640]{1,0:T(8,128)S(1)} %get-tuple-element.83), channel_id=1, source_target_pairs={{1,2},{2,1},{3,0},{0,3},{5,6},{6,5},{7,4},{4,7},{9,10},{10,9},{11,... | collective-permute-start | bytes 122888 | tf_op jit(solution)/shard_map/ppermute | solution.py:730
  23.3 4.6 %collective-permute-start.7 = (f32[16,640]{1,0:T(8,128)S(1)}, f32[16,640]{1,0:T(8,128)S(1)}, u32[]{:S(2)}, u32[]{:S(2)}) collective-permute-start(f32[16,640]{1,0:T(8,128)S(1)} %get-tuple-element.84), channel_id=1, source_target_pairs={{0,1},{1,0},{2,3},{3,2},{4,5},{5,4},{6,7},{7,6},{8,9},{9,8},{10,11... | collective-permute-start | bytes 122888 | tf_op jit(solution)/shard_map/ppermute | solution.py:730

commit v5 on v4

--- a/solution.py
+++ b/solution.py
@@ -118,7 +118,7 @@
         emit(first + k, sums[k])
 
 
-def taylor(block, start_of, star_ref, forward_ref, xs_ref, y_ref, integrals):
+def taylor(block, start_of, star_ref, forward_ref, xs_ref, ys, integrals, star_ready):
     def start():
         for f in range(FIELDS):
             value = start_of(f)
@@ -127,6 +127,7 @@
                 ref[field_rows(f), :] = weights[0] * value
 
     def step(k, n):
+        y_ref = ys[k % 2]
 
         def emit(g, value):
             if k < ORDER - 1:
@@ -139,12 +140,15 @@
         star_group(y_ref, star_ref, n * GROUP, emit, range(FIELDS))
 
     block(start)
+    star_ready()
+    block(functools.partial(step, 1, 0))
     for k in range(1, ORDER):
-        block(functools.partial(step, k, 0))
 
         def rest(k=k):
             step(k, 1)
             step(k, 2)
+            if k < ORDER - 1:
+                step(k + 1, 0)
 
         block(rest)
 
@@ -191,7 +195,14 @@
         packed_ref[j] = nt_dot(high, pick) + nt_dot(low, pick)
 
 
-def packed_taylor(star_ref, forward, xp_ref, y_ref, sum_ref, weights):
+def packed_taylor(xs_ref, turned_ref, star_ref, forward, xp_ref, y_ref, sum_ref, weights):
+    for j in range(PAIRS):
+        lanes = pair_lanes(j)
+        pick = turned_ref[0 : lanes.stop - lanes.start, :]
+        value = big_dot(xs_ref[0:MPAD, lanes], pick) + big_dot(xs_ref[MPAD : 2 * MPAD, lanes], pick)
+        value = value[0:MODES]
+        put_operand(xp_ref, j, value)
+        sum_ref[field_rows(j), :] = weights[0] * value
     for k in range(1, ORDER):
         for j in range(0, PAIRS, 2):
             lanes = slice(j * LANES, min(j + 2, PAIRS) * LANES)
@@ -214,15 +225,6 @@
             sum_ref[field_rows(j), :] = sum_ref[field_rows(j), :] + weights[k] * value
 
 
-def pack_state(base_ref, turned_ref, packed_ref):
-    for j in range(PAIRS):
-        fields = range(2 * j, min(2 * j + 2, FIELDS))
-        both = jnp.concatenate([base_ref[field_rows(f), :] for f in fields], axis=1)
-        pick = turned_ref[0 : both.shape[1], :]
-        high, low = two_parts(both)
-        packed_ref[field_rows(j), :] = big_dot(high, pick) + big_dot(low, pick)
-
-
 def unpack(sum_ref, pack_ref, emit):
     for j in range(PAIRS):
         high, low = two_parts(sum_ref[field_rows(j), :])
@@ -236,7 +238,7 @@
     return [lax.rem(lax.axis_index(axis), 2) == 0 for axis in ("near", "dom")]
 
 
-def send_pick(halo_ref):
+def send_rims(xs_ref, halo_ref, sends):
     width = halo_ref.shape[1]
     element = lax.broadcasted_iota(jnp.int32, (LANES, width), 0)
     near_even, dom_even = evens()
@@ -246,11 +248,7 @@
         for row in (jnp.where(even, down, up), jnp.where(even, up, down)):
             pick = jnp.where(element == row, 1.0, 0.0).astype(F32)
             picks.append(jnp.transpose(pick))
-    return jnp.concatenate(picks, axis=0).astype(BF)
-
-
-def send_rims(xs_ref, pick, sends):
-    width = sends[0].shape[0]
+    pick = jnp.concatenate(picks, axis=0).astype(BF)
     for q in range((FIELDS + 1) // 2):
         fields = (2 * q, min(2 * q + 1, FIELDS - 1))
         total = None
@@ -265,19 +263,6 @@
             sends[r][:, field_lanes(q)] = total[r * width : (r + 1) * width, :]
 
 
-def send_packed(sum_ref, pick, large_sends, sends):
-    width = sends[0].shape[0]
-    half = 4 * width
-    for j in range(PAIRS):
-        value = tall(sum_ref[field_rows(j), :], MPAD)
-        high, low = two_parts(jnp.concatenate([value, value], axis=0))
-        out = nt_dot(pick, high) + nt_dot(pick, low)
-        total = jnp.where(low_half(half), out[0:half], out[half:])
-        for r in range(4):
-            rows = slice(r * width, (r + 1) * width)
-            sends[r][:, field_lanes(j)] = large_sends[r][:, field_lanes(j)] + total[rows, :]
-
-
 def local_pick(part, slot, face):
     target = jnp.where(part == 0, face * LANES + slot, -1)
     target = jnp.concatenate([target[i : i + 1, :] for i in range(4)], axis=1)
@@ -359,10 +344,7 @@
 LARGE_ROW = 16
 
 
-def slot_tables(
-    far, part, face, turn, cluster, minus_ref, marks_ref, slot_flux_ref, scatter_ref,
-    turned_ref, packed_scatter_ref,
-):
+def slot_tables(far, part, face, turn, cluster, minus_ref, marks_ref, slot_flux_ref, scatter_ref):
     far2 = jnp.concatenate([far, far], axis=0)
     rows = [jnp.where(face == j, 1.0, 0.0) for j in range(4)]
     rows = [jnp.concatenate([row[i : i + 1, :] for i in range(4)], axis=1) for row in rows]
@@ -394,16 +376,10 @@
     slot_flux_ref[...] = nt_dot(high, pick) + nt_dot(low, pick)
     place = far[:, 0:LANES] + far[:, LANES : 2 * LANES]
     place = place + far[:, 2 * LANES : 3 * LANES] + far[:, 3 * LANES :]
-    packed_scatter_ref[...] = packed_pick(place, turned_ref)
     none = jnp.zeros_like(place)
     scatter_ref[...] = jnp.concatenate(
         [jnp.concatenate([place, none], axis=1), jnp.concatenate([none, place], axis=1)], axis=0
     )
-
-
-def packed_pick(pick, turned_ref):
-    halves = [big_dot(pick, turned_ref[n * LANES : (n + 1) * LANES, :]) for n in range(2)]
-    return jnp.concatenate(halves, axis=0).astype(BF)
 
 
 def low_half(rows):
@@ -469,9 +445,11 @@
         lifted = high[0:MODES] + high[MODES:] + big_dot(both[0:MODES], z_ref[1, :, lanes])
         for n, tile in enumerate(tiles):
             high, low = two_parts(lifted[:, field_lanes(n)])
-            count = min(scatter_ref.shape[1], (FIELDS - 2 * tile) * LANES)
-            pick = scatter_ref[:, 0:count]
-            emit(tile, big_dot(high, pick) + big_dot(low, pick))
+            count = min(2, FIELDS - 2 * tile)
+            pick = scatter_ref[:, 0 : count * LANES]
+            value = big_dot(high, pick) + big_dot(low, pick)
+            for k in range(count):
+                emit(2 * tile + k, value[:, field_lanes(k)])
 
 
 def wide(x):
@@ -525,34 +503,35 @@
 def first_kernel(*refs):
     sources, rest = refs[:INPUTS], refs[INPUTS:]
     held, rest = rest[:INPUTS], rest[INPUTS:]
-    first_ref, second_ref, forward_ref, s0, s1, s2, s3, xs_ref, y_ref, sems = rest
+    first_ref, second_ref, forward_ref, s0, s1, s2, s3, xs_ref, y_ref, y2_ref, sems = rest
     copies = [
         pltpu.make_async_copy(source, target, sems.at[n])
         for n, (source, target) in enumerate(zip(sources, held))
     ]
-    for copy in copies:
-        copy.start()
+    for n in (0, 2, 3, 1, *range(4, INPUTS)):
+        copies[n].start()
     u_ref, star_ref, stiff_ref, halo_ref = held[:4]
-    for copy in copies[:4]:
-        copy.wait()
+    for n in (0, 2, 3):
+        copies[n].wait()
     forward_ref[...] = forward_matrix(stiff_ref)
     taylor(
-        Steps(halo_ref), lambda f: u_ref[field_rows(f), :], star_ref, forward_ref, xs_ref, y_ref,
+        Steps(halo_ref), lambda f: u_ref[field_rows(f), :], star_ref, forward_ref, xs_ref, (y_ref, y2_ref),
         [(first_ref, integral_weights(0.0, 0.5)), (second_ref, integral_weights(0.5, 1.0))],
+        copies[1].wait,
     )
     for copy in copies[4:]:
         copy.wait()
     for f in range(FIELDS):
         put_operand(xs_ref, f, first_ref[field_rows(f), :])
-    send_rims(xs_ref, send_pick(halo_ref), (s0, s1, s2, s3))
+    send_rims(xs_ref, halo_ref, (s0, s1, s2, s3))
 
 
 def middle_local_kernel(
-    u_ref, first_ref, second_ref, star_ref, plus_ref, minus_ref, stiff_ref, face_lift_ref, project_ref,
+    u_ref, first_ref, star_ref, plus_ref, minus_ref, stiff_ref, face_lift_ref, project_ref,
     part_ref, slot_ref, face_ref, turn_ref, cluster_ref, halo_ref,
-    start_ref, g_ref, marks_ref, update_ref, lift_ref, pair_ref, pack_ref, packed_ref,
-    slot_flux_ref, scatter_ref, pick_ref, packed_scatter_ref, packed_send_ref, s0, s1, s2, s3,
-    turned_ref, base_ref, xs_ref, y_ref, table_ref, z_ref, rows_ref,
+    base_ref, g_ref, marks_ref, update_ref, lift_ref, pair_ref, pack_ref, packed_ref,
+    slot_flux_ref, scatter_ref, pick_ref, turned_ref,
+    xs_ref, y_ref, table_ref, z_ref, rows_ref,
 ):
     width = halo_ref.shape[1]
     prepare(stiff_ref, face_lift_ref, project_ref, update_ref, lift_ref, pair_ref, rows_ref)
@@ -570,19 +549,12 @@
     g_ref[...] = pick_faces(y_ref, 3 * MODES, table_ref, pick_ref[...])
     slot_tables(
         remote_pick(part, slot, width), part, face, turn_ref[...], cluster_ref[...], minus_ref,
-        marks_ref, slot_flux_ref, scatter_ref, turned_ref, packed_scatter_ref,
+        marks_ref, slot_flux_ref, scatter_ref,
     )
     finish_local(
         lambda f: u_ref[field_rows(f), :], star_ref, plus_ref, minus_ref, lift_ref,
         turn_ref[...], y_ref, g_ref, z_ref, base_ref,
     )
-    pack_state(base_ref, turned_ref, start_ref)
-    large = cluster_ref[...] != 0
-    for f in range(FIELDS):
-        put_operand(xs_ref, f, jnp.where(large, second_ref[field_rows(f), :], 0.0))
-    pick = send_pick(halo_ref)
-    send_rims(xs_ref, pick, (s0, s1, s2, s3))
-    packed_send_ref[...] = packed_pick(pick, turned_ref)
 
 
 def finish_local(base_of, star_ref, plus_ref, minus_ref, lift_ref, turn, y_ref, g_ref, z_ref, base_ref):
@@ -607,43 +579,42 @@
 
 
 def middle_remote_kernel(
-    r0, r1, r2, r3, start_ref, star_ref, slot_flux_ref, scatter_ref, forward_ref, lift_ref, pair_ref,
-    marks_ref, pick_ref, l0, l1, l2, l3,
-    middle_ref, sum_ref, traces_ref, s0, s1, s2, s3,
-    xp_ref, y_ref, z_ref,
+    r0, r1, r2, r3, u_ref, base_ref, second_ref, star_ref, slot_flux_ref, scatter_ref,
+    forward_ref, lift_ref, pair_ref, marks_ref, cluster_ref, halo_ref, pack_ref, turned_ref,
+    middle_ref, later_ref, traces_ref, s0, s1, s2, s3,
+    xs_ref, xp_ref, y_ref, sum_ref, z_ref,
 ):
-    weights = integral_weights(0.0, 0.5)
+    small = cluster_ref[...] == 0
     traces = slot_traces((r0, r1, r2, r3), pair_ref[...], marks_ref)
     traces_ref[...] = jnp.concatenate(traces, axis=0)
 
-    def take(j, lifted):
-        rows = field_rows(j)
-        value = start_ref[rows, :] - lifted
-        middle_ref[rows, :] = value
-        sum_ref[rows, :] = weights[0] * value
-        put_operand(xp_ref, j, value)
+    def take(f, lifted):
+        value = base_ref[field_rows(f), :] - lifted
+        value = jnp.where(small, value, u_ref[field_rows(f), :])
+        middle_ref[field_rows(f), :] = value
+        put_operand(xs_ref, f, value)
 
     slot_lift(traces, slot_flux_ref, marks_ref, lift_ref, scatter_ref, z_ref, take)
-    packed_taylor(star_ref, forward_ref[...], xp_ref, y_ref, sum_ref, weights)
-    send_packed(sum_ref, pick_ref[...], (l0, l1, l2, l3), (s0, s1, s2, s3))
+    packed_taylor(
+        xs_ref, turned_ref, star_ref, forward_ref[...], xp_ref, y_ref, sum_ref,
+        integral_weights(0.0, 0.5),
+    )
+
+    def emit(f, value):
+        later = jnp.where(small, value, second_ref[field_rows(f), :])
+        later_ref[field_rows(f), :] = later
+        put_operand(xs_ref, f, later)
+
+    unpack(sum_ref, pack_ref, emit)
+    send_rims(xs_ref, halo_ref, (s0, s1, s2, s3))
 
 
 def last_local_kernel(
-    u_ref, packed_middle_ref, first_ref, second_ref, packed_later_ref, gfirst_ref, star_ref, plus_ref,
-    minus_ref, update_ref, lift_ref, pick_ref, turn_ref, cluster_ref, pack_ref,
-    base_ref, xs_ref, y_ref, table_ref, z_ref, g_ref, middle_ref, later_ref,
+    u_ref, middle_ref, first_ref, second_ref, later_ref, gfirst_ref, star_ref, plus_ref, minus_ref,
+    update_ref, lift_ref, pick_ref, turn_ref, cluster_ref,
+    base_ref, xs_ref, y_ref, table_ref, z_ref, g_ref,
 ):
     small = cluster_ref[...] == 0
-
-    def choose(target, other):
-        def emit(f, value):
-            rows = field_rows(f)
-            target[rows, :] = jnp.where(small, value, other[rows, :])
-
-        return emit
-
-    unpack(packed_later_ref, pack_ref, choose(later_ref, second_ref))
-    unpack(packed_middle_ref, pack_ref, choose(middle_ref, u_ref))
     for f in range(FIELDS):
         put_operand(xs_ref, f, later_ref[field_rows(f), :])
     wide_dot(update_ref[3 * MODES :, :], xs_ref, y_ref)
@@ -672,15 +643,12 @@
         traces[j] = traces[j] + traces_ref[j * NPAD : (j + 1) * NPAD, :] * large
     copies = []
 
-    def emit(tile, lifted):
-        for k in range(lifted.shape[1] // LANES):
-            rows = field_rows(2 * tile + k)
-            done_ref[rows, :] = base_ref[rows, :] - lifted[:, field_lanes(k)]
-            copy = pltpu.make_async_copy(
-                done_ref.at[rows, :], out_hbm.at[rows, :], sems.at[2 * tile + k]
-            )
-            copy.start()
-            copies.append(copy)
+    def emit(f, lifted):
+        rows = field_rows(f)
+        done_ref[rows, :] = base_ref[rows, :] - lifted
+        copy = pltpu.make_async_copy(done_ref.at[rows, :], out_hbm.at[rows, :], sems.at[f])
+        copy.start()
+        copies.append(copy)
 
     slot_lift(traces, slot_flux_ref, marks_ref, lift_ref, scatter_ref, z_ref, emit)
     for copy in copies:
@@ -758,33 +726,28 @@
         first_kernel, inputs,
         [(x.shape, x.dtype) for x in inputs]
         + [state, state, ((3 * MODES, 3 * MPAD), BF)] + rims,
-        [scratch_xs(), scratch_y(3 * MODES), pltpu.SemaphoreType.DMA((INPUTS,))], "first",
+        [
+            scratch_xs(), scratch_y(3 * MODES), scratch_y(3 * MODES),
+            pltpu.SemaphoreType.DMA((INPUTS,)),
+        ], "first",
         pltpu.HBM,
     )
     u, star, stiffness, halo, plus, minus, face_lift, face_project = held[:8]
     part, slot, face, turn, cluster = held[8:]
     sends = s0, s1, s2, s3
     received = trade(sends)
-    packed_state = ((PAIRS * MODES, LANES), F32)
-    square, tall_square = ((LANES, LANES), BF), ((LANES, 2 * LANES), BF)
-    (
-        start, g, marks, update, lift, pair, pack, packed, slot_flux, scatter, pick,
-        packed_scatter, packed_send, *large_sends,
-    ) = call(
+    base, g, marks, update, lift, pair, pack, packed, slot_flux, scatter, pick, turned = call(
         middle_local_kernel,
-        (
-            u, first, second, star, plus, minus, stiffness, face_lift, face_project,
-            part, slot, face, turn, cluster, halo,
-        ),
+        (u, first, star, plus, minus, stiffness, face_lift, face_project,
+         part, slot, face, turn, cluster, halo),
         [
-            packed_state, gathered, ((KINDS, LANES), F32), ((update_rows, 3 * MPAD), BF),
+            state, gathered, ((KINDS, LANES), F32), ((update_rows, 3 * MPAD), BF),
             ((2 * MODES, 4 * FACES), BF), ((2 * FACES, 3 * LANES), BF),
-            tall_square, ((PAIRS, 3 * DROWS, LANES), F32),
-            ((PAIRS * DROWS, LANES), F32), tall_square, ((4 * LANES, 4 * LANES), BF),
-            square, square,
-        ] + rims,
+            ((LANES, 2 * LANES), BF), ((PAIRS, 3 * DROWS, LANES), F32),
+            ((PAIRS * DROWS, LANES), F32), ((LANES, 2 * LANES), BF), ((4 * LANES, 4 * LANES), BF),
+            ((2 * LANES, LANES), BF),
+        ],
         [
-            pltpu.VMEM((2 * LANES, LANES), BF), pltpu.VMEM(STATE, F32),
             scratch_xs(), scratch_y(update_rows), pltpu.VMEM(GATHERED, F32), scratch_z(4 * FACES),
             pltpu.VMEM((4 * FACES, LANES), F32),
         ],
@@ -793,12 +756,14 @@
     middle, later, traces, *sends = call(
         middle_remote_kernel,
         (
-            *received, start, packed, slot_flux, packed_scatter, forward, lift, pair, marks,
-            packed_send, *large_sends,
+            *received, u, base, second, packed, slot_flux, scatter, forward, lift, pair, marks,
+            cluster, halo, pack, turned,
         ),
-        [packed_state, packed_state, ((PAIRS * NPAD, LANES), F32)] + rims,
+        [state, state, ((PAIRS * NPAD, LANES), F32)] + rims,
         [
-            pltpu.VMEM((3 * MPAD, PAIRS * LANES), BF), pltpu.VMEM((3 * MODES, PAIRS * LANES), F32),
+            scratch_xs(), pltpu.VMEM((3 * MPAD, PAIRS * LANES), BF),
+            pltpu.VMEM((3 * MODES, PAIRS * LANES), F32),
+            pltpu.VMEM((PAIRS * MODES, LANES), F32),
             scratch_slots(),
         ],
         "middle_remote",
@@ -808,12 +773,12 @@
         last_local_kernel,
         (
             u, middle, first, second, later, g, star, plus, minus, update, lift,
-            pick, turn, cluster, pack,
+            pick, turn, cluster,
         ),
         [state],
         [
             scratch_xs(), scratch_y(update_rows), pltpu.VMEM(GATHERED, F32), scratch_z(4 * FACES),
-            pltpu.VMEM(GATHERED, F32), pltpu.VMEM(STATE, F32), pltpu.VMEM(STATE, F32),
+            pltpu.VMEM(GATHERED, F32),
         ],
         "last_local",
     )

time: 30.3 us -> 29.5 us (0.974)
  Pallas kernels: 18 us -> 17 us
  starting transfers between devices: 11 us -> 11.7 us
  waiting for transfers between devices: 0.84 us -> 0.4 us
    pallas_call x5, Pallas kernels: 18 us -> 17 us  [call(): pl.pallas_call(kernel, out_shape=out_shape, in_specs=[pl.BlockSpec(memory...]
    ppermute x8, starting transfers between devices: 11 us -> 11.7 us  [swap(): return lax.ppermute(x, axis, pairs)]
    ppermute x8, waiting for transfers between devices: 0.84 us -> 0.4 us  [swap(): return lax.ppermute(x, axis, pairs)]
  transfers between devices with their start and end apart: 8 -> 8, of which waited for: 1 -> 1; matrix products, arithmetic and copies ran while one was open for 0% -> 0% of each run, Pallas kernels for 20% -> 18%
where the time goes in v5:
time: 29.5 us; the launch traced here: 29.4 us
  Pallas kernels  17 us (58%)
  starting transfers between devices  11.7 us (40%)
  waiting for transfers between devices  0.4 us (1%)
    pallas_call x5, Pallas kernels, call(): pl.pallas_call(kernel, out_shape=out_shape, in_specs=[pl.BlockSpec(memory...  17 us
    ppermute x8, starting transfers between devices, swap(): return lax.ppermute(x, axis, pairs)  11.7 us
  transfers between devices with their start and end apart: 8, of which 1 were waited for; matrix products, arithmetic and copies ran while one was open for 0% of the time, Pallas kernels for 18%

profile of v5, /device:TPU:0, one launch (start us, length us, event | category | flops | bytes accessed | tf_op | source)
XLA Modules:
  0.0 29.4 jit_solution(4100561310539048639)
XLA Ops:
  0.0 5.5 %first.1 = (f32[504,128]{1,0:T(8,128)S(1)}, f32[9,9,3,128]{3,2,1,0:T(4,128)S(1)}, f32[3,56,56]{2,1,0:T(8,128)S(1)}, s32[4,16]{1,0:T(4,128)S(1)}, f32[9,9,4,128]{...) custom-call(f32[504,128]{1,0:T(8,128)} %bitcast.12, ...), custom_call_target="tpu_custom_call" | custom-call | flops 1000000000 | bytes 1000000 | tf_op jit(solution)/shard_map/first/pallas_call | solution.py:664
  5.5 6.1 %collective-permute-start = (f32[16,640]{1,0:T(8,128)S(1)}, f32[16,640]{1,0:T(8,128)S(1)}, u32[]{:S(2)}, u32[]{:S(2)}) collective-permute-start(f32[16,640]{1,0:T(8,128)S(1)} %get-tuple-element.44), channel_id=1, source_target_pairs={{4,8},{8,4},{12,16},{16,12},{20,24},{24,20},{28,0},{0,28},{5,9},{9... | collective-permute-start | bytes 122888 | tf_op jit(solution)/shard_map/ppermute | solution.py:698
  11.6 0.0 collective-permute-start.1
  11.6 0.7 %collective-permute-start.2 = (f32[16,640]{1,0:T(8,128)S(1)}, f32[16,640]{1,0:T(8,128)S(1)}, u32[]{:S(2)}, u32[]{:S(2)}) collective-permute-start(f32[16,640]{1,0:T(8,128)S(1)} %get-tuple-element.46), channel_id=1, source_target_pairs={{1,2},{2,1},{3,0},{0,3},{5,6},{6,5},{7,4},{4,7},{9,10},{10,9},{11,... | collective-permute-start | bytes 122888 | tf_op jit(solution)/shard_map/ppermute | solution.py:698
  12.3 1.0 %collective-permute-start.3 = (f32[16,640]{1,0:T(8,128)S(1)}, f32[16,640]{1,0:T(8,128)S(1)}, u32[]{:S(2)}, u32[]{:S(2)}) collective-permute-start(f32[16,640]{1,0:T(8,128)S(1)} %get-tuple-element.47), channel_id=1, source_target_pairs={{0,1},{1,0},{2,3},{3,2},{4,5},{5,4},{6,7},{7,6},{8,9},{9,8},{10,11... | collective-permute-start | bytes 122888 | tf_op jit(solution)/shard_map/ppermute | solution.py:698
  13.2 2.7 %middle_local.1 = (f32[504,128]{1,0:T(8,128)S(1)}, f32[216,512]{1,0:T(8,128)S(1)}, f32[32,128]{1,0:T(8,128)S(1)}, bf16[264,192]{1,0:T(8,128)(2,1)S(1)}, bf16[112...) custom-call(f32[504,128]{1,0:T(8,128)S(1)} %get-tuple-element.48.u_r, ...), custom_call_target="tpu_custom_call" | custom-call | flops 1000000000 | bytes 1000000 | tf_op jit(solution)/shard_map/middle_local/pallas_call | solution.py:664
  16.0 0.0 collective-permute-done.r0
  16.0 0.0 collective-permute-done.1.r1
  16.0 0.0 collective-permute-done.2.r2
  16.0 0.0 collective-permute-done.3.r3
  16.0 4.3 %middle_remote.1 = (f32[504,128]{1,0:T(8,128)S(1)}, f32[504,128]{1,0:T(8,128)S(1)}, f32[120,128]{1,0:T(8,128)S(1)}, f32[16,640]{1,0:T(8,128)S(1)}, f32[16,640]{1...) custom-call(f32[16,640]{1,0:T(8,128)S(1)} %collective-permute-done.r0, ...), custom_call_target="tpu_custom_call" | custom-call | flops 1000000000 | bytes 1000000 | tf_op jit(solution)/shard_map/middle_remote/pallas_call | solution.py:664
  20.3 2.4 %collective-permute-start.4 = (f32[16,640]{1,0:T(8,128)S(1)}, f32[16,640]{1,0:T(8,128)S(1)}, u32[]{:S(2)}, u32[]{:S(2)}) collective-permute-start(f32[16,640]{1,0:T(8,128)S(1)} %get-tuple-element.73), channel_id=1, source_target_pairs={{4,8},{8,4},{12,16},{16,12},{20,24},{24,20},{28,0},{0,28},{5,9},{9... | collective-permute-start | bytes 122888 | tf_op jit(solution)/shard_map/ppermute | solution.py:698
  22.7 0.0 collective-permute-start.5
  22.7 0.0 collective-permute-start.6
  22.7 1.6 %collective-permute-start.7 = (f32[16,640]{1,0:T(8,128)S(1)}, f32[16,640]{1,0:T(8,128)S(1)}, u32[]{:S(2)}, u32[]{:S(2)}) collective-permute-start(f32[16,640]{1,0:T(8,128)S(1)} %get-tuple-element.76), channel_id=1, source_target_pairs={{0,1},{1,0},{2,3},{3,2},{4,5},{5,4},{6,7},{7,6},{8,9},{9,8},{10,11... | collective-permute-start | bytes 122888 | tf_op jit(solution)/shard_map/ppermute | solution.py:698
  24.3 2.4 %last_local.1.base_ref = f32[504,128]{1,0:T(8,128)S(1)} custom-call(f32[504,128]{1,0:T(8,128)S(1)} %get-tuple-element.48.u_ref, f32[504,128]{1,0:T(8,128)S(1)} %get-tuple-element.77.middle_ref, f32[504,128]{1,0:T(8,128)S(1)} %get-tuple-element.49.first_ref, f32[504,128]{1,0:T(8,128)S(1)} %get-tuple-element.63.second_ref, ...), custom_call_target="tpu_custom_call" | custom-call | flops 1000000000 | bytes 1000000 | tf_op jit(solution)/shard_map/last_local/pallas_call | solution.py:664
  26.7 0.4 %collective-permute-done.4.r0 = f32[16,640]{1,0:T(8,128)S(1)} collective-permute-done((f32[16,640]{1,0:T(8,128)S(1)}, f32[16,640]{1,0:T(8,128)S(1)}, u32[]{:S(2)}, u32[]{:S(2)}) %collective-permute-start.4) | collective-permute-done | bytes 40992 | tf_op jit(solution)/shard_map/ppermute | solution.py:698
  27.1 0.0 collective-permute-done.5.r1
  27.1 0.0 collective-permute-done.6.r2
  27.1 0.0 collective-permute-done.7.r3
  27.1 2.1 %last_remote.1 = f32[504,128]{1,0:T(8,128)} custom-call(f32[16,640]{1,0:T(8,128)S(1)} %collective-permute-done.4.r0, f32[16,640]{1,0:T(8,128)S(1)} %collective-permute-done.5.r1, f32[16,640]{1,0:T(8,128)S(1)} %collective-permute-done.6.r2, f32[16,640]{1,0:T(8,128)S(1)} %collective-permute-done.7.r3, f32[504,128]{1,0:T(8,128)S(1)} %last_local.1.base_ref, ...), custom_call_target="tpu_custom_call" | custom-call | flops 1000000000 | bytes 1000000 | tf_op jit(solution)/shard_map/last_remote/pallas_call | solution.py:664
Async XLA Ops:
  5.5 10.4 %collective-permute-start = (f32[16,640]{1,0:T(8,128)S(1)}, f32[16,640]{1,0:T(8,128)S(1)}, u32[]{:S(2)}, u32[]{:S(2)}) collective-permute-start(f32[16,640]{1,0:T(8,128)S(1)} %get-tuple-element.44), channel_id=1, source_target_pairs={{4,8},{8,4},{12,16},{16,12},{20,24},{24,20},{28,0},{0,28},{5,9},{9... | collective-permute-start | bytes 122888 | tf_op jit(solution)/shard_map/ppermute | solution.py:698
  11.6 4.4 %collective-permute-start.1 = (f32[16,640]{1,0:T(8,128)S(1)}, f32[16,640]{1,0:T(8,128)S(1)}, u32[]{:S(2)}, u32[]{:S(2)}) collective-permute-start(f32[16,640]{1,0:T(8,128)S(1)} %get-tuple-element.45), channel_id=1, source_target_pairs={{0,4},{4,0},{8,12},{12,8},{16,20},{20,16},{24,28},{28,24},{1,5},{5... | collective-permute-start | bytes 122888 | tf_op jit(solution)/shard_map/ppermute | solution.py:698
  11.6 4.4 %collective-permute-start.2 = (f32[16,640]{1,0:T(8,128)S(1)}, f32[16,640]{1,0:T(8,128)S(1)}, u32[]{:S(2)}, u32[]{:S(2)}) collective-permute-start(f32[16,640]{1,0:T(8,128)S(1)} %get-tuple-element.46), channel_id=1, source_target_pairs={{1,2},{2,1},{3,0},{0,3},{5,6},{6,5},{7,4},{4,7},{9,10},{10,9},{11,... | collective-permute-start | bytes 122888 | tf_op jit(solution)/shard_map/ppermute | solution.py:698
  12.3 3.7 %collective-permute-start.3 = (f32[16,640]{1,0:T(8,128)S(1)}, f32[16,640]{1,0:T(8,128)S(1)}, u32[]{:S(2)}, u32[]{:S(2)}) collective-permute-start(f32[16,640]{1,0:T(8,128)S(1)} %get-tuple-element.47), channel_id=1, source_target_pairs={{0,1},{1,0},{2,3},{3,2},{4,5},{5,4},{6,7},{7,6},{8,9},{9,8},{10,11... | collective-permute-start | bytes 122888 | tf_op jit(solution)/shard_map/ppermute | solution.py:698
  20.3 6.8 %collective-permute-start.4 = (f32[16,640]{1,0:T(8,128)S(1)}, f32[16,640]{1,0:T(8,128)S(1)}, u32[]{:S(2)}, u32[]{:S(2)}) collective-permute-start(f32[16,640]{1,0:T(8,128)S(1)} %get-tuple-element.73), channel_id=1, source_target_pairs={{4,8},{8,4},{12,16},{16,12},{20,24},{24,20},{28,0},{0,28},{5,9},{9... | collective-permute-start | bytes 122888 | tf_op jit(solution)/shard_map/ppermute | solution.py:698
  22.7 4.4 %collective-permute-start.5 = (f32[16,640]{1,0:T(8,128)S(1)}, f32[16,640]{1,0:T(8,128)S(1)}, u32[]{:S(2)}, u32[]{:S(2)}) collective-permute-start(f32[16,640]{1,0:T(8,128)S(1)} %get-tuple-element.74), channel_id=1, source_target_pairs={{0,4},{4,0},{8,12},{12,8},{16,20},{20,16},{24,28},{28,24},{1,5},{5... | collective-permute-start | bytes 122888 | tf_op jit(solution)/shard_map/ppermute | solution.py:698
  22.7 4.4 %collective-permute-start.6 = (f32[16,640]{1,0:T(8,128)S(1)}, f32[16,640]{1,0:T(8,128)S(1)}, u32[]{:S(2)}, u32[]{:S(2)}) collective-permute-start(f32[16,640]{1,0:T(8,128)S(1)} %get-tuple-element.75), channel_id=1, source_target_pairs={{1,2},{2,1},{3,0},{0,3},{5,6},{6,5},{7,4},{4,7},{9,10},{10,9},{11,... | collective-permute-start | bytes 122888 | tf_op jit(solution)/shard_map/ppermute | solution.py:698
  22.7 4.4 %collective-permute-start.7 = (f32[16,640]{1,0:T(8,128)S(1)}, f32[16,640]{1,0:T(8,128)S(1)}, u32[]{:S(2)}, u32[]{:S(2)}) collective-permute-start(f32[16,640]{1,0:T(8,128)S(1)} %get-tuple-element.76), channel_id=1, source_target_pairs={{0,1},{1,0},{2,3},{3,2},{4,5},{5,4},{6,7},{7,6},{8,9},{9,8},{10,11... | collective-permute-start | bytes 122888 | tf_op jit(solution)/shard_map/ppermute | solution.py:698

commit v6 on v5

--- a/solution.py
+++ b/solution.py
@@ -635,24 +635,18 @@
 
 def last_remote_kernel(
     r0, r1, r2, r3, base_ref, traces_ref, slot_flux_ref, scatter_ref, lift_ref, pair_ref, marks_ref,
-    out_hbm, z_ref, done_ref, sems,
+    out_ref, z_ref,
 ):
     large = marks_ref[LARGE_ROW : LARGE_ROW + 1, :]
     traces = slot_traces((r0, r1, r2, r3), pair_ref[...], marks_ref)
     for j in range(PAIRS):
         traces[j] = traces[j] + traces_ref[j * NPAD : (j + 1) * NPAD, :] * large
-    copies = []
 
     def emit(f, lifted):
         rows = field_rows(f)
-        done_ref[rows, :] = base_ref[rows, :] - lifted
-        copy = pltpu.make_async_copy(done_ref.at[rows, :], out_hbm.at[rows, :], sems.at[f])
-        copy.start()
-        copies.append(copy)
+        out_ref[rows, :] = base_ref[rows, :] - lifted
 
     slot_lift(traces, slot_flux_ref, marks_ref, lift_ref, scatter_ref, z_ref, emit)
-    for copy in copies:
-        copy.wait()
 
 
 STATE = (FIELDS * MODES, LANES)
@@ -786,8 +780,8 @@
         last_remote_kernel,
         (*received, base, traces, slot_flux, scatter, lift, pair, marks),
         [state],
-        [scratch_slots(), pltpu.VMEM(STATE, F32), pltpu.SemaphoreType.DMA((FIELDS,))],
-        "last_remote", out_space=pltpu.HBM,
+        [scratch_slots()],
+        "last_remote",
     )
     return jnp.transpose(out.reshape(FIELDS, MODES, LANES), (1, 0, 2))
 

time: 29.5 us -> 29.3 us (level)
  no operation moved by 1% of the time
where the time goes in v6:
time: 29.3 us; the launch traced here: 29.2 us
  Pallas kernels  17.1 us (58%)
  starting transfers between devices  11.7 us (40%)
  waiting for transfers between devices  0.4 us (1%)
    pallas_call x5, Pallas kernels, call(): pl.pallas_call(kernel, out_shape=out_shape, in_specs=[pl.BlockSpec(memory...  17.1 us
    ppermute x8, starting transfers between devices, swap(): return lax.ppermute(x, axis, pairs)  11.7 us
  transfers between devices with their start and end apart: 8, of which 1 were waited for; matrix products, arithmetic and copies ran while one was open for 0% of the time, Pallas kernels for 18%

profile of v6, /device:TPU:0, one launch (start us, length us, event | category | flops | bytes accessed | tf_op | source)
XLA Modules:
  0.0 29.2 jit_solution(5950544207483354403)
XLA Ops:
  0.0 5.5 %first.1 = (f32[504,128]{1,0:T(8,128)S(1)}, f32[9,9,3,128]{3,2,1,0:T(4,128)S(1)}, f32[3,56,56]{2,1,0:T(8,128)S(1)}, s32[4,16]{1,0:T(4,128)S(1)}, f32[9,9,4,128]{...) custom-call(f32[504,128]{1,0:T(8,128)} %bitcast.12, ...), custom_call_target="tpu_custom_call" | custom-call | flops 1000000000 | bytes 1000000 | tf_op jit(solution)/shard_map/first/pallas_call | solution.py:658
  5.5 6.1 %collective-permute-start = (f32[16,640]{1,0:T(8,128)S(1)}, f32[16,640]{1,0:T(8,128)S(1)}, u32[]{:S(2)}, u32[]{:S(2)}) collective-permute-start(f32[16,640]{1,0:T(8,128)S(1)} %get-tuple-element.44), channel_id=1, source_target_pairs={{4,8},{8,4},{12,16},{16,12},{20,24},{24,20},{28,0},{0,28},{5,9},{9... | collective-permute-start | bytes 122888 | tf_op jit(solution)/shard_map/ppermute | solution.py:692
  11.6 0.0 collective-permute-start.1
  11.6 0.7 %collective-permute-start.2 = (f32[16,640]{1,0:T(8,128)S(1)}, f32[16,640]{1,0:T(8,128)S(1)}, u32[]{:S(2)}, u32[]{:S(2)}) collective-permute-start(f32[16,640]{1,0:T(8,128)S(1)} %get-tuple-element.46), channel_id=1, source_target_pairs={{1,2},{2,1},{3,0},{0,3},{5,6},{6,5},{7,4},{4,7},{9,10},{10,9},{11,... | collective-permute-start | bytes 122888 | tf_op jit(solution)/shard_map/ppermute | solution.py:692
  12.3 1.0 %collective-permute-start.3 = (f32[16,640]{1,0:T(8,128)S(1)}, f32[16,640]{1,0:T(8,128)S(1)}, u32[]{:S(2)}, u32[]{:S(2)}) collective-permute-start(f32[16,640]{1,0:T(8,128)S(1)} %get-tuple-element.47), channel_id=1, source_target_pairs={{0,1},{1,0},{2,3},{3,2},{4,5},{5,4},{6,7},{7,6},{8,9},{9,8},{10,11... | collective-permute-start | bytes 122888 | tf_op jit(solution)/shard_map/ppermute | solution.py:692
  13.2 2.7 %middle_local.1 = (f32[504,128]{1,0:T(8,128)S(1)}, f32[216,512]{1,0:T(8,128)S(1)}, f32[32,128]{1,0:T(8,128)S(1)}, bf16[264,192]{1,0:T(8,128)(2,1)S(1)}, bf16[112...) custom-call(f32[504,128]{1,0:T(8,128)S(1)} %get-tuple-element.48.u_r, ...), custom_call_target="tpu_custom_call" | custom-call | flops 1000000000 | bytes 1000000 | tf_op jit(solution)/shard_map/middle_local/pallas_call | solution.py:658
  16.0 0.0 collective-permute-done.r0
  16.0 0.0 collective-permute-done.1.r1
  16.0 0.0 collective-permute-done.2.r2
  16.0 0.0 collective-permute-done.3.r3
  16.0 4.3 %middle_remote.1 = (f32[504,128]{1,0:T(8,128)S(1)}, f32[504,128]{1,0:T(8,128)S(1)}, f32[120,128]{1,0:T(8,128)S(1)}, f32[16,640]{1,0:T(8,128)S(1)}, f32[16,640]{1...) custom-call(f32[16,640]{1,0:T(8,128)S(1)} %collective-permute-done.r0, ...), custom_call_target="tpu_custom_call" | custom-call | flops 1000000000 | bytes 1000000 | tf_op jit(solution)/shard_map/middle_remote/pallas_call | solution.py:658
  20.3 2.4 %collective-permute-start.4 = (f32[16,640]{1,0:T(8,128)S(1)}, f32[16,640]{1,0:T(8,128)S(1)}, u32[]{:S(2)}, u32[]{:S(2)}) collective-permute-start(f32[16,640]{1,0:T(8,128)S(1)} %get-tuple-element.73), channel_id=1, source_target_pairs={{4,8},{8,4},{12,16},{16,12},{20,24},{24,20},{28,0},{0,28},{5,9},{9... | collective-permute-start | bytes 122888 | tf_op jit(solution)/shard_map/ppermute | solution.py:692
  22.7 0.0 collective-permute-start.5
  22.7 0.0 collective-permute-start.6
  22.7 1.6 %collective-permute-start.7 = (f32[16,640]{1,0:T(8,128)S(1)}, f32[16,640]{1,0:T(8,128)S(1)}, u32[]{:S(2)}, u32[]{:S(2)}) collective-permute-start(f32[16,640]{1,0:T(8,128)S(1)} %get-tuple-element.76), channel_id=1, source_target_pairs={{0,1},{1,0},{2,3},{3,2},{4,5},{5,4},{6,7},{7,6},{8,9},{9,8},{10,11... | collective-permute-start | bytes 122888 | tf_op jit(solution)/shard_map/ppermute | solution.py:692
  24.3 2.4 %last_local.1.base_ref = f32[504,128]{1,0:T(8,128)S(1)} custom-call(f32[504,128]{1,0:T(8,128)S(1)} %get-tuple-element.48.u_ref, f32[504,128]{1,0:T(8,128)S(1)} %get-tuple-element.77.middle_ref, f32[504,128]{1,0:T(8,128)S(1)} %get-tuple-element.49.first_ref, f32[504,128]{1,0:T(8,128)S(1)} %get-tuple-element.63.second_ref, ...), custom_call_target="tpu_custom_call" | custom-call | flops 1000000000 | bytes 1000000 | tf_op jit(solution)/shard_map/last_local/pallas_call | solution.py:658
  26.7 0.4 %collective-permute-done.4.r0 = f32[16,640]{1,0:T(8,128)S(1)} collective-permute-done((f32[16,640]{1,0:T(8,128)S(1)}, f32[16,640]{1,0:T(8,128)S(1)}, u32[]{:S(2)}, u32[]{:S(2)}) %collective-permute-start.4) | collective-permute-done | bytes 40992 | tf_op jit(solution)/shard_map/ppermute | solution.py:692
  27.1 0.0 collective-permute-done.5.r1
  27.1 0.0 collective-permute-done.6.r2
  27.1 0.0 collective-permute-done.7.r3
  27.1 2.1 %last_remote.1 = f32[504,128]{1,0:T(8,128)} custom-call(f32[16,640]{1,0:T(8,128)S(1)} %collective-permute-done.4.r0, f32[16,640]{1,0:T(8,128)S(1)} %collective-permute-done.5.r1, f32[16,640]{1,0:T(8,128)S(1)} %collective-permute-done.6.r2, f32[16,640]{1,0:T(8,128)S(1)} %collective-permute-done.7.r3, f32[504,128]{1,0:T(8,128)S(1)} %last_local.1.base_ref, ...), custom_call_target="tpu_custom_call" | custom-call | flops 1000000000 | bytes 1000000 | tf_op jit(solution)/shard_map/last_remote/pallas_call | solution.py:658
Async XLA Ops:
  5.5 10.4 %collective-permute-start = (f32[16,640]{1,0:T(8,128)S(1)}, f32[16,640]{1,0:T(8,128)S(1)}, u32[]{:S(2)}, u32[]{:S(2)}) collective-permute-start(f32[16,640]{1,0:T(8,128)S(1)} %get-tuple-element.44), channel_id=1, source_target_pairs={{4,8},{8,4},{12,16},{16,12},{20,24},{24,20},{28,0},{0,28},{5,9},{9... | collective-permute-start | bytes 122888 | tf_op jit(solution)/shard_map/ppermute | solution.py:692
  11.6 4.4 %collective-permute-start.1 = (f32[16,640]{1,0:T(8,128)S(1)}, f32[16,640]{1,0:T(8,128)S(1)}, u32[]{:S(2)}, u32[]{:S(2)}) collective-permute-start(f32[16,640]{1,0:T(8,128)S(1)} %get-tuple-element.45), channel_id=1, source_target_pairs={{0,4},{4,0},{8,12},{12,8},{16,20},{20,16},{24,28},{28,24},{1,5},{5... | collective-permute-start | bytes 122888 | tf_op jit(solution)/shard_map/ppermute | solution.py:692
  11.6 4.4 %collective-permute-start.2 = (f32[16,640]{1,0:T(8,128)S(1)}, f32[16,640]{1,0:T(8,128)S(1)}, u32[]{:S(2)}, u32[]{:S(2)}) collective-permute-start(f32[16,640]{1,0:T(8,128)S(1)} %get-tuple-element.46), channel_id=1, source_target_pairs={{1,2},{2,1},{3,0},{0,3},{5,6},{6,5},{7,4},{4,7},{9,10},{10,9},{11,... | collective-permute-start | bytes 122888 | tf_op jit(solution)/shard_map/ppermute | solution.py:692
  12.3 3.7 %collective-permute-start.3 = (f32[16,640]{1,0:T(8,128)S(1)}, f32[16,640]{1,0:T(8,128)S(1)}, u32[]{:S(2)}, u32[]{:S(2)}) collective-permute-start(f32[16,640]{1,0:T(8,128)S(1)} %get-tuple-element.47), channel_id=1, source_target_pairs={{0,1},{1,0},{2,3},{3,2},{4,5},{5,4},{6,7},{7,6},{8,9},{9,8},{10,11... | collective-permute-start | bytes 122888 | tf_op jit(solution)/shard_map/ppermute | solution.py:692
  20.3 6.8 %collective-permute-start.4 = (f32[16,640]{1,0:T(8,128)S(1)}, f32[16,640]{1,0:T(8,128)S(1)}, u32[]{:S(2)}, u32[]{:S(2)}) collective-permute-start(f32[16,640]{1,0:T(8,128)S(1)} %get-tuple-element.73), channel_id=1, source_target_pairs={{4,8},{8,4},{12,16},{16,12},{20,24},{24,20},{28,0},{0,28},{5,9},{9... | collective-permute-start | bytes 122888 | tf_op jit(solution)/shard_map/ppermute | solution.py:692
  22.7 4.4 %collective-permute-start.5 = (f32[16,640]{1,0:T(8,128)S(1)}, f32[16,640]{1,0:T(8,128)S(1)}, u32[]{:S(2)}, u32[]{:S(2)}) collective-permute-start(f32[16,640]{1,0:T(8,128)S(1)} %get-tuple-element.74), channel_id=1, source_target_pairs={{0,4},{4,0},{8,12},{12,8},{16,20},{20,16},{24,28},{28,24},{1,5},{5... | collective-permute-start | bytes 122888 | tf_op jit(solution)/shard_map/ppermute | solution.py:692
  22.7 4.4 %collective-permute-start.6 = (f32[16,640]{1,0:T(8,128)S(1)}, f32[16,640]{1,0:T(8,128)S(1)}, u32[]{:S(2)}, u32[]{:S(2)}) collective-permute-start(f32[16,640]{1,0:T(8,128)S(1)} %get-tuple-element.75), channel_id=1, source_target_pairs={{1,2},{2,1},{3,0},{0,3},{5,6},{6,5},{7,4},{4,7},{9,10},{10,9},{11,... | collective-permute-start | bytes 122888 | tf_op jit(solution)/shard_map/ppermute | solution.py:692
  22.7 4.4 %collective-permute-start.7 = (f32[16,640]{1,0:T(8,128)S(1)}, f32[16,640]{1,0:T(8,128)S(1)}, u32[]{:S(2)}, u32[]{:S(2)}) collective-permute-start(f32[16,640]{1,0:T(8,128)S(1)} %get-tuple-element.76), channel_id=1, source_target_pairs={{0,1},{1,0},{2,3},{3,2},{4,5},{5,4},{6,7},{7,6},{8,9},{9,8},{10,11... | collective-permute-start | bytes 122888 | tf_op jit(solution)/shard_map/ppermute | solution.py:692
